TPU v7x, 128 devices: a whole 4x4x4 slice. The times are simulated.
128 devices in a mesh: xd: 8 (over z, y_lo), ta: 16 (over x, y_hi, core).
Axes of the slice: x: 4, y: 4 (y_hi: 2, y_lo: 2; y = y_hi * 2 + y_lo), z: 4, core: 2. Of those that a mesh axis runs over, the one named last changes fastest.
Arguments:
- gauge_links: float32 [4, 2, 3, 3, 32, 16, 4, 128], P(None, None, None, None, 'xd', 'ta'), may hold values from -1 to 1, as said below
- momenta: float32 [4, 2, 3, 3, 32, 16, 4, 128], P(None, None, None, None, 'xd', 'ta'), as said below
- noise_table: float32 [2, 4, 3, 4096], replicated, may hold values from -6 to 6
- noise_index: int32 [32, 16, 4, 128], P('xd', 'ta'), may hold values from 0 to 4095
- partner: int32 [32], P('xd'), may hold values from 0 to 31, as said below
Outputs:
- new_links: float32 [4, 2, 3, 3, 32, 16, 4, 128], P(None, None, None, None, 'xd', 'ta')
- new_momenta: float32 [4, 2, 3, 3, 32, 16, 4, 128], P(None, None, None, None, 'xd', 'ta')
Inputs may be any that keep to these rules, and one draw needn't show every extreme that they name: partner is an involution without fixed points: each row x1 is paired with a row of the aligned block of 4 rows that lies 32 / 2 rows away, and partner[partner[x1]] = x1. Every gauge_links[mu] at every site is a special unitary 3 x 3 matrix. Every momenta[mu] at every site is a Hermitian traceless 3 x 3 matrix.
All inputs are finite; a program needn't handle non-finite values.
Results may differ from a plain program's by a relative error of at most 0.0001.
Values sent between devices are 32-bit elements; how exact they have to be, the bound alone decides.
No kernel may reach another device: no remote copies, remote signals or barrier semaphores. Data moves between devices by JAX's collectives and lax.ppermute only.
A program may use at most 128 MiB of HBM per device.

v0:
```python
import jax
import jax.numpy as jnp
from jax import lax
from jax.experimental import pallas as pl
from jax.experimental.pallas import tpu as pltpu
from jax.sharding import PartitionSpec as P

HOPPING = 0.13
STEP = 0.25
DEGREE = 6
F32 = jnp.float32
GAMMA = (
    ((3, 2, 1, 0), ((0, 1), (0, 1), (0, -1), (0, -1))),
    ((2, 3, 0, 1), ((1, 0), (1, 0), (1, 0), (1, 0))),
    ((3, 2, 1, 0), ((-1, 0), (1, 0), (1, 0), (-1, 0))),
    ((2, 3, 0, 1), ((0, 1), (0, -1), (0, -1), (0, 1))),
)
ROWS = 16
HALO = 24


def ld(ref, k, h):
    return ref[k * ROWS + 8 * h : k * ROWS + 8 * h + 8, :]


def st(ref, k, h, value):
    ref[k * ROWS + 8 * h : k * ROWS + 8 * h + 8, :] = value


def cadd(a, b):
    return (a[0] + b[0], a[1] + b[1])


def csub(a, b):
    return (a[0] - b[0], a[1] - b[1])


def cmul(a, b):
    return (a[0] * b[0] - a[1] * b[1], a[0] * b[1] + a[1] * b[0])


def cmul_conj(a, b):
    return (a[0] * b[0] + a[1] * b[1], a[1] * b[0] - a[0] * b[1])


def add_unit(x, y, coef, sign):
    re, im = coef
    if re:
        if re * sign > 0:
            return cadd(x, y)
        return csub(x, y)
    if im * sign > 0:
        return (x[0] - y[1], x[1] + y[0])
    return (x[0] + y[1], x[1] - y[0])


def spinor(ref, h):
    return [[(ld(ref, c * 4 + s, h), ld(ref, 12 + c * 4 + s, h)) for c in range(3)] for s in range(4)]


def project(psi, mu, sign):
    source, coef = GAMMA[mu]
    return [[add_unit(psi[t][c], psi[source[t]][c], coef[t], sign) for c in range(3)] for t in range(2)]


def matrix(ref, mu, h):
    return [[(ld(ref, mu * 18 + i * 3 + j, h), ld(ref, mu * 18 + 9 + i * 3 + j, h)) for j in range(3)] for i in range(3)]


def mat_half(u, v):
    out = []
    for t in range(2):
        row = []
        for i in range(3):
            acc = cmul(u[i][0], v[t][0])
            for j in (1, 2):
                acc = cadd(acc, cmul(u[i][j], v[t][j]))
            row.append(acc)
        out.append(row)
    return out


def mat_dag_half(u, v):
    out = []
    for t in range(2):
        row = []
        for i in range(3):
            acc = cmul_conj(v[t][0], u[0][i])
            for j in (1, 2):
                acc = cadd(acc, cmul_conj(v[t][j], u[j][i]))
            row.append(acc)
        out.append(row)
    return out


def half_index(part, t, c):
    return part * 6 + t * 3 + c


def put_half(ref, h, v, base=0):
    for t in range(2):
        for c in range(3):
            for part in range(2):
                st(ref, base + half_index(part, t, c), h, v[t][c][part])


def get_half(fn):
    return [[tuple(fn(half_index(part, t, c)) for part in range(2)) for c in range(3)] for t in range(2)]


def map_half(fn, *vs):
    return [[tuple(fn(*(v[t][c][part] for v in vs)) for part in range(2)) for c in range(3)] for t in range(2)]


class Info:
    def __init__(self, table, partner):
        self.even_t = table[0] == 0
        self.even_x = table[1] == 0
        self.sign_ahead = table[2].astype(F32)
        self.sign_behind = table[3].astype(F32)
        self.partner = [partner[j] & 3 for j in range(4)]


def row_in_pair():
    return lax.broadcasted_iota(jnp.int32, (8, 128), 0) & 3


def send_rows(dst, base, src, k, info, row):
    for j in range(4):
        dst[pl.ds(base * 4 + info.partner[j], 1), :] = src[k * ROWS + 4 * j + row : k * ROWS + 4 * j + row + 1, :]


def send_both(psi_ref, u_ref, info, t_a, t_b, x_a, x_b, mirror, q0, q2, q3, h0, h2):
    for h in range(2):
        psi = spinor(psi_ref, h)
        front = map_half(lambda a: a * info.sign_ahead, project(psi, 1, 1))
        back = map_half(
            lambda a: a * info.sign_behind, mat_dag_half(matrix(u_ref, 1, h), project(psi, 1, -1))
        )
        put_half(t_a, h, map_half(lambda a, b: jnp.where(info.even_t, b, a), front, back))
        put_half(t_b, h, map_half(lambda a, b: jnp.where(info.even_t, a, b), front, back))
        put_half(h0, h, project(psi, 0, 1))
        put_half(h2, h, project(psi, 2, 1))
        for mu, ref in ((0, q0), (2, q2), (3, q3)):
            put_half(ref, h, mat_dag_half(matrix(u_ref, mu, h), project(psi, mu, -1)))
    for k in range(12):
        front = h0[k * ROWS : k * ROWS + 4, :]
        back = q0[k * ROWS + 12 : k * ROWS + 16, :]
        x_a[k * 4 : k * 4 + 4, :] = jnp.where(info.even_x, back, front)
        x_b[k * 4 : k * 4 + 4, :] = jnp.where(info.even_x, front, back)
        send_rows(mirror, k, h2, k, info, 0)
        send_rows(mirror, 12 + k, q2, k, info, 3)


def dirac(psi_ref, u_ref, arrived, q0, q2, q3, scratch, out_ref, w_ref):
    ahead_t, behind_t, ahead_x, behind_x, ahead_m, behind_m = arrived
    a0, b0, fa, fb = scratch
    for k in range(12):
        a0[k * HALO + 16 : k * HALO + 20, :] = ahead_x(k)
        b0[k * HALO : k * HALO + 4, :] = behind_x(k)
        b0[k * HALO + 4 : k * HALO + 20, :] = q0[k * ROWS : k * ROWS + 16, :]
        fa[pl.ds(k * ROWS + 3, 4, stride=4), :] = ahead_m(k)
        fb[pl.ds(k * ROWS, 4, stride=4), :] = behind_m(k)
    for h in range(2):
        v = project(spinor(psi_ref, h), 0, 1)
        for t in range(2):
            for c in range(3):
                for part in range(2):
                    k = half_index(part, t, c)
                    a0[k * HALO + 8 * h : k * HALO + 8 * h + 8, :] = v[t][c][part]
    x2 = row_in_pair()
    for h in range(2):
        psi = spinor(psi_ref, h)
        acc = None
        for mu in range(4):
            if mu == 0:
                ahead = get_half(lambda k: a0[k * HALO + 8 * h + 4 : k * HALO + 8 * h + 12, :])
                behind = get_half(lambda k: b0[k * HALO + 8 * h : k * HALO + 8 * h + 8, :])
            elif mu == 1:
                ahead = get_half(lambda k: ahead_t(k, h))
                behind = get_half(lambda k: behind_t(k, h))
            elif mu == 2:
                raw = project(psi, 2, 1)
                face = get_half(lambda k: ld(fa, k, h))
                ahead = map_half(lambda r, f: jnp.where(x2 == 3, f, pltpu.roll(r, 7, 0)), raw, face)
                behind = get_half(lambda k: jnp.where(x2 == 0, ld(fb, k, h), pltpu.roll(ld(q2, k, h), 1, 0)))
            else:
                ahead = map_half(lambda r: pltpu.roll(r, 127, 1), project(psi, 3, 1))
                behind = get_half(lambda k: pltpu.roll(ld(q3, k, h), 1, 1))
            w = mat_half(matrix(u_ref, mu, h), ahead)
            if w_ref is not None:
                put_half(w_ref, h, w, mu * 12)
            total = map_half(lambda a, b: a + b, w, behind)
            delta = map_half(lambda a, b: a - b, w, behind)
            source, coef = GAMMA[mu]
            if acc is None:
                zero = jnp.zeros((8, 128), F32)
                acc = [total[0], total[1]] + [
                    [add_unit((zero, zero), delta[source[s]][c], coef[s], 1) for c in range(3)] for s in (2, 3)
                ]
            else:
                for s in range(2):
                    acc[s] = [cadd(acc[s][c], total[s][c]) for c in range(3)]
                for s in (2, 3):
                    acc[s] = [add_unit(acc[s][c], delta[source[s]][c], coef[s], 1) for c in range(3)]
        for s in range(4):
            for c in range(3):
                for part in range(2):
                    st(out_ref, part * 12 + c * 4 + s, h, psi[s][c][part] - HOPPING * acc[s][c][part])


def arrived_swap(info, t_a, t_b, x_a, x_b, mirror):
    def rows(ref, k):
        return ref[k * 4 : k * 4 + 4, :]

    return (
        lambda k, h: jnp.where(info.even_t, ld(t_a, k, h), ld(t_b, k, h)),
        lambda k, h: jnp.where(info.even_t, ld(t_b, k, h), ld(t_a, k, h)),
        lambda k: jnp.where(info.even_x, rows(x_a, k), rows(x_b, k)),
        lambda k: jnp.where(info.even_x, rows(x_b, k), rows(x_a, k)),
        lambda k: rows(mirror, k),
        lambda k: rows(mirror, 12 + k),
    )


def noise_kernel(table_i, partner, index, table, u, *rest):
    psi, t_a, t_b, x_a, x_b, mirror, q0, q2, q3, flat, parts, h0, h2 = rest
    info = Info(table_i, partner)
    for part in range(2):
        for c in range(3):
            flat[(part * 3 + c) * 4 : (part * 3 + c) * 4 + 4, :] = table[part, c]
    for hi in range(16):
        block = flat[:, hi * 256 : hi * 256 + 256]
        first = block.astype(jnp.bfloat16)
        left = block - first.astype(F32)
        second = left.astype(jnp.bfloat16)
        third = (left - second.astype(F32)).astype(jnp.bfloat16)
        for n, value in enumerate((first, second, third)):
            parts[hi * 24 : hi * 24 + 24, n * 256 : n * 256 + 256] = value
    low_iota = lax.broadcasted_iota(jnp.int32, (256, 128), 0)
    table_parts = parts[...]
    for r in range(16):
        wanted = index[r : r + 1, :]
        hot = jnp.where(low_iota == (wanted & 255), 1.0, 0.0).astype(jnp.bfloat16)
        found = jnp.dot(table_parts, jnp.concatenate([hot, hot, hot], axis=0), preferred_element_type=F32)
        high = jnp.broadcast_to(wanted >> 8, (24, 128))
        value = found[0:24]
        for hi in range(1, 16):
            value = jnp.where(high == hi, found[hi * 24 : hi * 24 + 24], value)
        psi[pl.ds(r, 24, stride=16), :] = value
    send_both(psi, u, info, t_a, t_b, x_a, x_b, mirror, q0, q2, q3, h0, h2)


def phi_kernel(table_i, partner, psi, u, q0, q2, q3, t_a, t_b, x_a, x_b, mirror, *rest):
    phi, o_ta, o_tb, o_xa, o_xb, o_m, o_q0, o_q2, o_q3, a0, b0, fa, fb, h0, h2 = rest
    info = Info(table_i, partner)
    arrived = arrived_swap(info, t_a, t_b, x_a, x_b, mirror)
    dirac(psi, u, arrived, q0, q2, q3, (a0, b0, fa, fb), phi, None)
    send_both(phi, u, info, o_ta, o_tb, o_xa, o_xb, o_m, o_q0, o_q2, o_q3, h0, h2)


def send_response(y, info, o_t, o_x, o_m, h2):
    for h in range(2):
        v = spinor(y, h)
        put_half(o_t, h, map_half(lambda a: a * info.sign_ahead, project(v, 1, -1)))
        put_half(h2, h, project(v, 2, -1))
        if h == 0:
            face = project(v, 0, -1)
            for t in range(2):
                for c in range(3):
                    for part in range(2):
                        k = half_index(part, t, c)
                        o_x[k * 4 : k * 4 + 4, :] = face[t][c][part][0:4]
    for k in range(12):
        send_rows(o_m, k, h2, k, info, 0)


def response_kernel(table_i, partner, phi, u, q0, q2, q3, t_a, t_b, x_a, x_b, mirror, *rest):
    y, w, o_t, o_x, o_m, a0, b0, fa, fb, h2 = rest
    info = Info(table_i, partner)
    arrived = arrived_swap(info, t_a, t_b, x_a, x_b, mirror)
    dirac(phi, u, arrived, q0, q2, q3, (a0, b0, fa, fb), y, w)
    send_response(y, info, o_t, o_x, o_m, h2)


def response2_kernel(table_i, partner, phi, u, q0, q2, q3, t_a, t_b, x_a, x_b, mirror, b_t, b_x, b_m, *rest):
    y, w, o_t, o_x, o_m, a0, b0, fa, fb, h2 = rest
    info = Info(table_i, partner)
    arrived = list(arrived_swap(info, t_a, t_b, x_a, x_b, mirror))
    arrived[1] = lambda k, h: ld(b_t, k, h)
    arrived[3] = lambda k: b_x[k * 4 : k * 4 + 4, :]
    arrived[5] = lambda k: b_m[k * 4 : k * 4 + 4, :]
    dirac(phi, u, arrived, q0, q2, q3, (a0, b0, fa, fb), y, w)
    send_response(y, info, o_t, o_x, o_m, h2)


def force_kernel(table_i, partner, phi, u, y, w, r_t, r_x, r_m, force, sent, a0, fa):
    info = Info(table_i, partner)
    for k in range(12):
        a0[k * HALO + 16 : k * HALO + 20, :] = r_x[k * 4 : k * 4 + 4, :]
        fa[pl.ds(k * ROWS + 3, 4, stride=4), :] = r_m[k * 4 : k * 4 + 4, :]
    for h in range(2):
        v = project(spinor(y, h), 0, -1)
        for t in range(2):
            for c in range(3):
                for part in range(2):
                    k = half_index(part, t, c)
                    a0[k * HALO + 8 * h : k * HALO + 8 * h + 8, :] = v[t][c][part]
    x2 = row_in_pair()
    for h in range(2):
        ysp = spinor(y, h)
        psp = spinor(phi, h)
        for mu in range(4):
            if mu == 0:
                x = get_half(lambda k: a0[k * HALO + 8 * h + 4 : k * HALO + 8 * h + 12, :])
            elif mu == 1:
                x = get_half(lambda k: ld(r_t, k, h))
            elif mu == 2:
                face = get_half(lambda k: ld(fa, k, h))
                x = map_half(
                    lambda r, f: jnp.where(x2 == 3, f, pltpu.roll(r, 7, 0)), project(ysp, 2, -1), face
                )
            else:
                x = map_half(lambda r: pltpu.roll(r, 127, 1), project(ysp, 3, -1))
            left = mat_half(matrix(u, mu, h), x) + get_half(lambda k: ld(w, mu * 12 + k, h))
            right = project(psp, mu, -1) + project(ysp, mu, 1)

            def g_im(i, j):
                return sum(left[n][i][1] * right[n][j][0] - left[n][i][0] * right[n][j][1] for n in range(4))

            def g_re(i, j):
                return sum(left[n][i][0] * right[n][j][0] + left[n][i][1] * right[n][j][1] for n in range(4))

            d = [g_im(i, i) for i in range(3)]
            third = (d[0] + d[1] + d[2]) * (1.0 / 3.0)
            scale = -2.0 * HOPPING
            values = [scale * (d[0] - third), scale * (d[1] - third)]
            for i, j in ((0, 1), (0, 2), (1, 2)):
                values.append((0.5 * scale) * (g_im(i, j) + g_im(j, i)))
                values.append((0.5 * scale) * (g_re(j, i) - g_re(i, j)))
            for n, value in enumerate(values):
                st(force, mu * 8 + n, h, value)
    for k in range(32):
        for j in range(4):
            at = pl.multiple_of(k * ROWS + 4 * info.partner[j], 4)
            sent[pl.ds(at, 4), :] = force[k * ROWS + 4 * j : k * ROWS + 4 * j + 4, :]


OFF = ((0, 1), (0, 2), (1, 2))


def updated_momenta(read, force, mirrored, mu, h):
    diag_force = [ld(force, mu * 8 + n, h) - ld(mirrored, mu * 8 + n, h) for n in range(2)]
    diag_force.append(-(diag_force[0] + diag_force[1]))
    diag = [read(n) + STEP * diag_force[n] for n in range(3)]
    upper = []
    for n in range(3):
        re = ld(force, mu * 8 + 2 + 2 * n, h) - ld(mirrored, mu * 8 + 2 + 2 * n, h)
        im = ld(force, mu * 8 + 3 + 2 * n, h) + ld(mirrored, mu * 8 + 3 + 2 * n, h)
        upper.append((read(3 + 2 * n) + STEP * re, read(4 + 2 * n) + STEP * im))
    return diag, upper


def link_step(diag, upper, u):
    b = [STEP * value for value in diag]
    b01, b02, b12 = ((STEP * value[0], STEP * value[1]) for value in upper)
    n01, n02, n12 = (v[0] * v[0] + v[1] * v[1] for v in (b01, b02, b12))
    square_diag = [b[0] * b[0] + n01 + n02, b[1] * b[1] + n01 + n12, b[2] * b[2] + n02 + n12]

    def scaled(v, by):
        return (v[0] * by, v[1] * by)

    square = [
        cadd(scaled(b01, b[0] + b[1]), cmul_conj(b02, b12)),
        cadd(scaled(b02, b[0] + b[2]), cmul(b01, b12)),
        cadd(scaled(b12, b[1] + b[2]), cmul_conj(b02, b01)),
    ]
    c1 = 0.5 * (square_diag[0] + square_diag[1] + square_diag[2])
    triple = cmul_conj(cmul(b01, b12), b02)[0]
    c0 = b[0] * (b[1] * b[2] - n12) - b[1] * n02 - b[2] * n01 + 2.0 * triple
    one = jnp.ones_like(c1)
    zero = jnp.zeros_like(c1)
    r0, r1, r2 = (one, zero), (zero, zero), (zero, zero)
    for k in range(DEGREE, 0, -1):
        inv = 1.0 / k
        new0 = (1.0 + (r2[1] * c0) * inv, -(r2[0] * c0) * inv)
        new1 = ((r0[0] - r2[0] * c1) * inv, (r0[1] - r2[1] * c1) * inv)
        new2 = (r1[0] * inv, r1[1] * inv)
        r0, r1, r2 = new0, new1, new2
    ir1 = (-r1[1], r1[0])
    e = [[None] * 3 for _ in range(3)]
    for i in range(3):
        e[i][i] = cadd(r0, csub(scaled(ir1, b[i]), scaled(r2, square_diag[i])))
    for (i, j), v, s in zip(OFF, (b01, b02, b12), square):
        e[i][j] = csub(cmul(ir1, v), cmul(r2, s))
        e[j][i] = csub(cmul_conj(ir1, v), cmul_conj(r2, s))
    return [[cadd(cadd(cmul(e[i][0], u[0][j]), cmul(e[i][1], u[1][j])), cmul(e[i][2], u[2][j])) for j in range(3)] for i in range(3)]


def input_momentum(ref, mu, h):
    def read(n):
        if n < 3:
            return ld(ref, mu * 18 + 4 * n, h)
        i, j = OFF[(n - 3) // 2]
        return ld(ref, mu * 18 + 9 * ((n - 3) % 2) + 3 * i + j, h)

    return read


def put_matrix(ref, mu, h, value):
    for i in range(3):
        for j in range(3):
            for part in range(2):
                st(ref, mu * 18 + part * 9 + i * 3 + j, h, value[i][j][part])


def update_kernel(table_i, partner, phi, u, p, force, mirrored, *rest):
    new_u, new_p, o_t, o_x, o_m, q0, q2, q3 = rest
    info = Info(table_i, partner)
    for h in range(2):
        psi = spinor(phi, h)
        for mu in range(4):
            diag, upper = updated_momenta(input_momentum(p, mu, h), force, mirrored, mu, h)
            for n in range(3):
                st(new_p, mu * 9 + n, h, diag[n])
                st(new_p, mu * 9 + 3 + 2 * n, h, upper[n][0])
                st(new_p, mu * 9 + 4 + 2 * n, h, upper[n][1])
            link = link_step(diag, upper, matrix(u, mu, h))
            put_matrix(new_u, mu, h, link)
            back = mat_dag_half(link, project(psi, mu, -1))
            if mu == 1:
                put_half(o_t, h, map_half(lambda a: a * info.sign_behind, back))
            else:
                put_half({0: q0, 2: q2, 3: q3}[mu], h, back)
    for k in range(12):
        o_x[k * 4 : k * 4 + 4, :] = q0[k * ROWS + 12 : k * ROWS + 16, :]
        send_rows(o_m, k, q2, k, info, 3)


def last_kernel(u, p, old_p, force, mirrored, new_u, new_p):
    for h in range(2):
        for mu in range(4):
            diag, upper = updated_momenta(lambda n: ld(p, mu * 9 + n, h), force, mirrored, mu, h)
            for i in range(3):
                st(new_p, mu * 18 + 4 * i, h, diag[i])
                st(new_p, mu * 18 + 9 + 4 * i, h, ld(old_p, mu * 18 + 9 + 4 * i, h))
            for (i, j), v in zip(OFF, upper):
                st(new_p, mu * 18 + 3 * i + j, h, v[0])
                st(new_p, mu * 18 + 3 * j + i, h, v[0])
                st(new_p, mu * 18 + 9 + 3 * i + j, h, v[1])
                st(new_p, mu * 18 + 9 + 3 * j + i, h, -v[1])
            put_matrix(new_u, mu, h, link_step(diag, upper, matrix(u, mu, h)))


VM = pl.BlockSpec(memory_space=pltpu.VMEM)
SM = pl.BlockSpec(memory_space=pltpu.SMEM)
FULL = ROWS * 12
FACE = 4 * 12


def call(kernel, name, n_scalar, args, outs, scratch, limit=4):
    return pl.pallas_call(
        kernel,
        name=name,
        out_shape=[jax.ShapeDtypeStruct((rows, 128), F32) for rows in outs],
        in_specs=[SM] * n_scalar + [VM] * (len(args) - n_scalar),
        out_specs=[VM] * len(outs),
        scratch_shapes=[s if not isinstance(s, int) else pltpu.VMEM((s, 128), F32) for s in scratch],
        compiler_params=pltpu.CompilerParams(vmem_limit_bytes=limit << 20),
    )(*args)


def swap(value, axis, far):
    n = lax.axis_size(axis)
    if far:
        pairs = [(i, (i + 1) % n if i % 2 else (i - 1) % n) for i in range(n)]
    else:
        pairs = [(i, i ^ 1) for i in range(n)]
    return lax.ppermute(value, axis, pairs)


def shift(value, axis, by):
    n = lax.axis_size(axis)
    return lax.ppermute(value, axis, [(i, (i + by) % n) for i in range(n)])


def mirror_swap(value):
    n = lax.axis_size("xd")
    return lax.ppermute(value, "xd", [(i, i ^ (n // 2)) for i in range(n)])


def exchange(t_a, t_b, x_a, x_b, m):
    far_t = swap(t_b, "ta", True)
    mirrored = mirror_swap(m)
    far_x = swap(x_b, "xd", True)
    near_x = swap(x_a, "xd", False)
    near_t = swap(t_a, "ta", False)
    return near_t, far_t, near_x, far_x, mirrored


def per_device(gauge_links, momenta, noise_table, noise_index, partner):
    ta = lax.axis_index("ta")
    xd = lax.axis_index("xd")
    lane = lax.iota(jnp.int32, 8)
    last = lax.axis_size("ta") - 1
    info = jnp.where(
        lane == 0,
        ta & 1,
        jnp.where(
            lane == 1,
            xd & 1,
            jnp.where(lane == 2, jnp.where(ta == 0, -1, 1), jnp.where(ta == last, -1, 1)),
        ),
    ).astype(jnp.int32)
    s = (info, partner)
    u = gauge_links.reshape(72 * ROWS, 128)
    p = momenta.reshape(72 * ROWS, 128)
    table = jnp.transpose(noise_table, (0, 2, 1, 3))
    index = noise_index.reshape(ROWS, 128)
    messages = [FULL, FULL, FACE, FACE, 2 * FACE]
    local = [FULL, FULL, FULL]
    halo = [12 * HALO, 12 * HALO, FULL, FULL]
    spin = 24 * ROWS

    psi, *rest = call(
        noise_kernel,
        "noise",
        2,
        (*s, index, table, u),
        [spin] + messages + local,
        [pltpu.VMEM((24, 4096), F32), pltpu.VMEM((384, 768), jnp.bfloat16), FULL, FULL],
        12,
    )
    arrived = exchange(*rest[:5])
    phi, *rest = call(
        phi_kernel, "phi", 2, (*s, psi, u, *rest[5:], *arrived), [spin] + messages + local, halo + [FULL, FULL]
    )
    arrived = exchange(*rest[:5])
    y, w, o_t, o_x, o_m = call(
        response_kernel,
        "response",
        2,
        (*s, phi, u, *rest[5:], *arrived),
        [spin, 4 * FULL, FULL, FACE, FACE],
        halo + [FULL],
    )
    force, sent = call(
        force_kernel,
        "force",
        2,
        (*s, phi, u, y, w, shift(o_t, "ta", -1), shift(o_x, "xd", -1), mirror_swap(o_m)),
        [32 * ROWS, 32 * ROWS],
        [12 * HALO, FULL],
    )
    u, p1, o_t, o_x, o_m, *q = call(
        update_kernel,
        "update",
        2,
        (*s, phi, u, p, force, mirror_swap(sent)),
        [72 * ROWS, 36 * ROWS, FULL, FACE, FACE] + local,
        [],
    )
    y, w, o_t, o_x, o_m = call(
        response2_kernel,
        "response2",
        2,
        (*s, phi, u, *q, *arrived, shift(o_t, "ta", 1), shift(o_x, "xd", 1), mirror_swap(o_m)),
        [spin, 4 * FULL, FULL, FACE, FACE],
        halo + [FULL],
    )
    force, sent = call(
        force_kernel,
        "force2",
        2,
        (*s, phi, u, y, w, shift(o_t, "ta", -1), shift(o_x, "xd", -1), mirror_swap(o_m)),
        [32 * ROWS, 32 * ROWS],
        [12 * HALO, FULL],
    )
    new_u, new_p = call(
        last_kernel, "last", 0, (u, p1, p, force, mirror_swap(sent)), [72 * ROWS, 72 * ROWS], []
    )
    return new_u.reshape(gauge_links.shape), new_p.reshape(momenta.shape)


def solution(mesh):
    sites = P(None, None, None, None, "xd", "ta", None, None)
    return jax.shard_map(
        per_device,
        mesh=mesh,
        in_specs=(sites, sites, P(), P("xd", "ta", None, None), P("xd")),
        out_specs=(sites, sites),
        check_vma=False,
    )
```

profile of v0, /device:TPU:0, one launch (start us, length us, event | category | flops | bytes accessed | tf_op | source)
XLA Modules:
  0.0 83.7 jit_solution(15999884607889849832)
XLA Ops:
  1.3 1.1 %copy-done = f32[4,2,3,3,4,1,4,128]{7,6,5,4,3,2,1,0:T(4,128)S(1)} copy-done((f32[4,2,3,3,4,1,4,128]{7,6,5,4,3,2,1,0:T(4,128)S(1)}, f32[4,2,3,3,4,1,4,128]{7,6,5,4,3,2,1,0:T(4,128)}, u32[]{:S(2)}) %copy-start) | copy-done | bytes 589848
  2.4 1.0 %copy-done.2 = f32[2,4,3,4096]{3,1,2,0:T(4,128)S(1)} copy-done((f32[2,4,3,4096]{3,1,2,0:T(4,128)S(1)}, f32[2,4,3,4096]{3,1,2,0:T(4,128)}, u32[]{:S(2)}) %copy-start.2) | copy-done | bytes 393240
  3.4 3.3 %noise.1 = (f32[384,128]{1,0:T(8,128)S(1)}, f32[192,128]{1,0:T(8,128)S(1)}, f32[192,128]{1,0:T(8,128)S(1)}, f32[48,128]{1,0:T(8,128)S(1)}, f32[48,128]{1,0:T(8,1...) custom-call(s32[8]{0:T(128)S(1)} %compare_select_fusion.2.table_i, ...), custom_call_target="tpu_custom_call" | custom-call | tf_op jit(solution)/shard_map/noise/pallas_call | solution.py:462
  6.8 5.6 %collective-permute-start.1 = (f32[192,128]{1,0:T(8,128)S(1)}, f32[192,128]{1,0:T(8,128)S(1)}, u32[]{:S(2)}, u32[]{:S(2)}) collective-permute-start(f32[192,128]{1,0:T(8,128)S(1)} %get-tuple-element.49), channel_id=1, source_target_pairs={{0,15},{1,2},{2,1},{3,4},{4,3},{5,6},{6,5},{7,8},{8,7},{9,10},{10,... | collective-permute-start | bytes 294920 | tf_op jit(solution)/shard_map/ppermute | solution.py:479
  12.5 3.9 %collective-permute-start.4 = (f32[96,128]{1,0:T(8,128)S(1)}, f32[96,128]{1,0:T(8,128)S(1)}, u32[]{:S(2)}, u32[]{:S(2)}) collective-permute-start(f32[96,128]{1,0:T(8,128)S(1)} %get-tuple-element.52), channel_id=1, source_target_pairs={{0,64},{16,80},{32,96},{48,112},{64,0},{80,16},{96,32},{112,48},{1... | collective-permute-start | bytes 147464 | tf_op jit(solution)/shard_map/ppermute | solution.py:489
  16.3 0.7 collective-permute-start.2
  17.0 1.5 %collective-permute-start.3 = (f32[48,128]{1,0:T(8,128)S(1)}, f32[48,128]{1,0:T(8,128)S(1)}, u32[]{:S(2)}, u32[]{:S(2)}) collective-permute-start(f32[48,128]{1,0:T(8,128)S(1)} %get-tuple-element.51), channel_id=1, source_target_pairs={{0,112},{16,32},{32,16},{48,64},{64,48},{80,96},{96,80},{112,0},{1... | collective-permute-start | bytes 73736 | tf_op jit(solution)/shard_map/ppermute | solution.py:479
  18.5 1.7 %collective-permute-done.2.x_a = f32[48,128]{1,0:T(8,128)S(1)} collective-permute-done((f32[48,128]{1,0:T(8,128)S(1)}, f32[48,128]{1,0:T(8,128)S(1)}, u32[]{:S(2)}, u32[]{:S(2)}) %collective-permute-start.2) | collective-permute-done | bytes 24608 | tf_op jit(solution)/shard_map/ppermute | solution.py:479
  20.1 2.8 %collective-permute-done.3.x_b = f32[48,128]{1,0:T(8,128)S(1)} collective-permute-done((f32[48,128]{1,0:T(8,128)S(1)}, f32[48,128]{1,0:T(8,128)S(1)}, u32[]{:S(2)}, u32[]{:S(2)}) %collective-permute-start.3) | collective-permute-done | bytes 24608 | tf_op jit(solution)/shard_map/ppermute | solution.py:479
  22.9 1.1 %phi.1 = (f32[384,128]{1,0:T(8,128)S(1)}, f32[192,128]{1,0:T(8,128)S(1)}, f32[192,128]{1,0:T(8,128)S(1)}, f32[48,128]{1,0:T(8,128)S(1)}, f32[48,128]{1,0:T(8,128...) custom-call(s32[8]{0:T(128)S(1)} %compare_select_fusion.2.table_i, ...), custom_call_target="tpu_custom_call" | custom-call | tf_op jit(solution)/shard_map/phi/pallas_call | solution.py:462
  24.2 1.9 %collective-permute-start.6 = (f32[192,128]{1,0:T(8,128)S(1)}, f32[192,128]{1,0:T(8,128)S(1)}, u32[]{:S(2)}, u32[]{:S(2)}) collective-permute-start(f32[192,128]{1,0:T(8,128)S(1)} %get-tuple-element.58), channel_id=1, source_target_pairs={{0,15},{1,2},{2,1},{3,4},{4,3},{5,6},{6,5},{7,8},{8,7},{9,10},{10,... | collective-permute-start | bytes 294920 | tf_op jit(solution)/shard_map/ppermute | solution.py:479
  26.1 3.9 %collective-permute-start.8 = (f32[48,128]{1,0:T(8,128)S(1)}, f32[48,128]{1,0:T(8,128)S(1)}, u32[]{:S(2)}, u32[]{:S(2)}) collective-permute-start(f32[48,128]{1,0:T(8,128)S(1)} %get-tuple-element.60), channel_id=1, source_target_pairs={{0,112},{16,32},{32,16},{48,64},{64,48},{80,96},{96,80},{112,0},{1... | collective-permute-start | bytes 73736 | tf_op jit(solution)/shard_map/ppermute | solution.py:479
  30.1 2.1 %collective-permute-done.8.x_b = f32[48,128]{1,0:T(8,128)S(1)} collective-permute-done((f32[48,128]{1,0:T(8,128)S(1)}, f32[48,128]{1,0:T(8,128)S(1)}, u32[]{:S(2)}, u32[]{:S(2)}) %collective-permute-start.8) | collective-permute-done | bytes 24608 | tf_op jit(solution)/shard_map/ppermute | solution.py:479
  32.1 0.9 %response.1 = (f32[384,128]{1,0:T(8,128)S(1)}, f32[768,128]{1,0:T(8,128)S(1)}, f32[192,128]{1,0:T(8,128)S(1)}, f32[48,128]{1,0:T(8,128)S(1)}, f32[48,128]{1,0:T(8,128)S(1)}) custom-call(s32[8]{0:T(128)S(1)} %compare_select_fusion.2.table_i, s32[4]{0:T(128)S(1)} %copy-done.3, f32[384,128]{1,0:T(8,128)S(1)} %get-tuple-element.53.phi, ...), custom_call_target="tpu_custom_call" | custom-call | tf_op jit(solution)/shard_map/response/pallas_call | solution.py:462
  33.0 2.8 %collective-permute-start.10 = (f32[192,128]{1,0:T(8,128)S(1)}, f32[192,128]{1,0:T(8,128)S(1)}, u32[]{:S(2)}, u32[]{:S(2)}) collective-permute-start(f32[192,128]{1,0:T(8,128)S(1)} %get-tuple-element.64), channel_id=1, source_target_pairs={{0,15},{1,0},{2,1},{3,2},{4,3},{5,4},{6,5},{7,6},{8,7},{9,8},{10,9... | collective-permute-start | bytes 294920 | tf_op jit(solution)/shard_map/ppermute | solution.py:484
  35.8 2.5 %collective-permute-start.11 = (f32[48,128]{1,0:T(8,128)S(1)}, f32[48,128]{1,0:T(8,128)S(1)}, u32[]{:S(2)}, u32[]{:S(2)}) collective-permute-start(f32[48,128]{1,0:T(8,128)S(1)} %get-tuple-element.65), channel_id=1, source_target_pairs={{0,112},{16,0},{32,16},{48,32},{64,48},{80,64},{96,80},{112,96},{1... | collective-permute-start | bytes 73736 | tf_op jit(solution)/shard_map/ppermute | solution.py:484
  38.4 1.5 %collective-permute-done.11.r_x = f32[48,128]{1,0:T(8,128)S(1)} collective-permute-done((f32[48,128]{1,0:T(8,128)S(1)}, f32[48,128]{1,0:T(8,128)S(1)}, u32[]{:S(2)}, u32[]{:S(2)}) %collective-permute-start.11) | collective-permute-done | bytes 24608 | tf_op jit(solution)/shard_map/ppermute | solution.py:484
  39.9 3.8 %collective-permute-done.12.r_m = f32[48,128]{1,0:T(8,128)S(1)} collective-permute-done((f32[48,128]{1,0:T(8,128)S(1)}, f32[48,128]{1,0:T(8,128)S(1)}, u32[]{:S(2)}, u32[]{:S(2)}) %collective-permute-start.12) | collective-permute-done | bytes 24608 | tf_op jit(solution)/shard_map/ppermute | solution.py:489
  43.7 1.1 %force.1 = (f32[512,128]{1,0:T(8,128)S(1)}, f32[512,128]{1,0:T(8,128)S(1)}) custom-call(s32[8]{0:T(128)S(1)} %compare_select_fusion.2.table_i, s32[4]{0:T(128)S(1)} %copy-done.3, f32[384,128]{1,0:T(8,128)S(1)} %get-tuple-element.53.phi, f32[1152,128]{1,0:T(8,128)S(1)} %bitcast.13, f32[384,128]{1,0:T(8,128)S(1)} %get-tuple-element.62.y, ...), custom_call_target="tpu_custom_call" | custom-call | tf_op jit(solution)/shard_map/force/pallas_call | solution.py:462
  44.9 7.9 %collective-permute-done.13.mirrored = f32[512,128]{1,0:T(8,128)S(1)} collective-permute-done((f32[512,128]{1,0:T(8,128)S(1)}, f32[512,128]{1,0:T(8,128)S(1)}, u32[]{:S(2)}, u32[]{:S(2)}) %collective-permute-start.13) | collective-permute-done | bytes 262176 | tf_op jit(solution)/shard_map/ppermute | solution.py:489
  52.7 1.3 %update.1 = (f32[1152,128]{1,0:T(8,128)S(1)}, f32[576,128]{1,0:T(8,128)S(1)}, f32[192,128]{1,0:T(8,128)S(1)}, f32[48,128]{1,0:T(8,128)S(1)}, f32[48,128]{1,0:T(8...) custom-call(s32[8]{0:T(128)S(1)} %compare_select_fusion.2.table_i, ...), custom_call_target="tpu_custom_call" | custom-call | tf_op jit(solution)/shard_map/update/pallas_call | solution.py:462
  54.2 1.5 %collective-permute-start.16 = (f32[48,128]{1,0:T(8,128)S(1)}, f32[48,128]{1,0:T(8,128)S(1)}, u32[]{:S(2)}, u32[]{:S(2)}) collective-permute-start(f32[48,128]{1,0:T(8,128)S(1)} %get-tuple-element.76), channel_id=1, source_target_pairs={{0,64},{16,80},{32,96},{48,112},{64,0},{80,16},{96,32},{112,48},{1... | collective-permute-start | bytes 73736 | tf_op jit(solution)/shard_map/ppermute | solution.py:489
  55.7 4.4 %collective-permute-done.15.b_x = f32[48,128]{1,0:T(8,128)S(1)} collective-permute-done((f32[48,128]{1,0:T(8,128)S(1)}, f32[48,128]{1,0:T(8,128)S(1)}, u32[]{:S(2)}, u32[]{:S(2)}) %collective-permute-start.15) | collective-permute-done | bytes 24608 | tf_op jit(solution)/shard_map/ppermute | solution.py:484
  60.1 1.6 %collective-permute-done.14.b_t = f32[192,128]{1,0:T(8,128)S(1)} collective-permute-done((f32[192,128]{1,0:T(8,128)S(1)}, f32[192,128]{1,0:T(8,128)S(1)}, u32[]{:S(2)}, u32[]{:S(2)}) %collective-permute-start.14) | collective-permute-done | bytes 98336 | tf_op jit(solution)/shard_map/ppermute | solution.py:484
  61.7 0.9 %response2.1 = (f32[384,128]{1,0:T(8,128)S(1)}, f32[768,128]{1,0:T(8,128)S(1)}, f32[192,128]{1,0:T(8,128)S(1)}, f32[48,128]{1,0:T(8,128)S(1)}, f32[48,128]{1,0:T(8,128)S(1)}) custom-call(s32[8]{0:T(128)S(1)} %compare_select_fusion.2.table_i, s32[4]{0:T(128)S(1)} %copy-done.3, f32[384,128]{1,0:T(8,128)S(1)} %get-tuple-element.53.phi, ...), custom_call_target="tpu_custom_call" | custom-call | tf_op jit(solution)/shard_map/response2/pallas_call | solution.py:462
  62.6 2.6 %collective-permute-start.17 = (f32[192,128]{1,0:T(8,128)S(1)}, f32[192,128]{1,0:T(8,128)S(1)}, u32[]{:S(2)}, u32[]{:S(2)}) collective-permute-start(f32[192,128]{1,0:T(8,128)S(1)} %get-tuple-element.79), channel_id=1, source_target_pairs={{0,15},{1,0},{2,1},{3,2},{4,3},{5,4},{6,5},{7,6},{8,7},{9,8},{10,9... | collective-permute-start | bytes 294920 | tf_op jit(solution)/shard_map/ppermute | solution.py:484
  65.2 2.6 %collective-permute-start.18 = (f32[48,128]{1,0:T(8,128)S(1)}, f32[48,128]{1,0:T(8,128)S(1)}, u32[]{:S(2)}, u32[]{:S(2)}) collective-permute-start(f32[48,128]{1,0:T(8,128)S(1)} %get-tuple-element.80), channel_id=1, source_target_pairs={{0,112},{16,0},{32,16},{48,32},{64,48},{80,64},{96,80},{112,96},{1... | collective-permute-start | bytes 73736 | tf_op jit(solution)/shard_map/ppermute | solution.py:484
  67.8 1.5 %collective-permute-done.18.r_x = f32[48,128]{1,0:T(8,128)S(1)} collective-permute-done((f32[48,128]{1,0:T(8,128)S(1)}, f32[48,128]{1,0:T(8,128)S(1)}, u32[]{:S(2)}, u32[]{:S(2)}) %collective-permute-start.18) | collective-permute-done | bytes 24608 | tf_op jit(solution)/shard_map/ppermute | solution.py:484
  69.3 3.8 %collective-permute-done.19.r_m = f32[48,128]{1,0:T(8,128)S(1)} collective-permute-done((f32[48,128]{1,0:T(8,128)S(1)}, f32[48,128]{1,0:T(8,128)S(1)}, u32[]{:S(2)}, u32[]{:S(2)}) %collective-permute-start.19) | collective-permute-done | bytes 24608 | tf_op jit(solution)/shard_map/ppermute | solution.py:489
  73.2 1.1 %force2.1 = (f32[512,128]{1,0:T(8,128)S(1)}, f32[512,128]{1,0:T(8,128)S(1)}) custom-call(s32[8]{0:T(128)S(1)} %compare_select_fusion.2.table_i, s32[4]{0:T(128)S(1)} %copy-done.3, f32[384,128]{1,0:T(8,128)S(1)} %get-tuple-element.53.phi, f32[1152,128]{1,0:T(8,128)S(1)} %get-tuple-element.69.u, f32[384,128]{1,0:T(8,128)S(1)} %get-tuple-element.77.y, ...), custom_call_target="tpu_custom_call" | custom-call | tf_op jit(solution)/shard_map/force2/pallas_call | solution.py:462
  74.4 7.9 %collective-permute-done.20.mirrored = f32[512,128]{1,0:T(8,128)S(1)} collective-permute-done((f32[512,128]{1,0:T(8,128)S(1)}, f32[512,128]{1,0:T(8,128)S(1)}, u32[]{:S(2)}, u32[]{:S(2)}) %collective-permute-start.20) | collective-permute-done | bytes 262176 | tf_op jit(solution)/shard_map/ppermute | solution.py:489
  82.2 1.5 %last.1 = (f32[1152,128]{1,0:T(8,128)}, f32[1152,128]{1,0:T(8,128)}) custom-call(f32[1152,128]{1,0:T(8,128)S(1)} %get-tuple-element.69.u, f32[576,128]{1,0:T(8,128)S(1)} %get-tuple-element.70.p, f32[1152,128]{1,0:T(8,128)S(1)} %bitcast.16, f32[512,128]{1,0:T(8,128)S(1)} %get-tuple-element.82.force, f32[512,128]{1,0:T(8,128)S(1)} %collective-permute-done.20.mirrored), custom_call_target="tpu_custom_call" | custom-call | tf_op jit(solution)/shard_map/last/pallas_call | solution.py:462
  (29 shorter events, 1.2 us)
Async XLA Ops:
  0.6 0.7 copy-start.4
  0.7 0.7 copy-start.3
  1.3 1.1 %copy-start = (f32[4,2,3,3,4,1,4,128]{7,6,5,4,3,2,1,0:T(4,128)S(1)}, f32[4,2,3,3,4,1,4,128]{7,6,5,4,3,2,1,0:T(4,128)}, u32[]{:S(2)}) copy-start(f32[4,2,3,3,4,1,4,128]{7,6,5,4,3,2,1,0:T(4,128)} %param.5) | copy-start | bytes 1769476
  2.4 1.0 %copy-start.2 = (f32[2,4,3,4096]{3,1,2,0:T(4,128)S(1)}, f32[2,4,3,4096]{3,1,2,0:T(4,128)}, u32[]{:S(2)}) copy-start(f32[2,4,3,4096]{3,1,2,0:T(4,128)} %param.7) | copy-start | bytes 1179652
  6.8 16.2 %collective-permute-start = (f32[192,128]{1,0:T(8,128)S(1)}, f32[192,128]{1,0:T(8,128)S(1)}, u32[]{:S(2)}, u32[]{:S(2)}) collective-permute-start(f32[192,128]{1,0:T(8,128)S(1)} %get-tuple-element.48), channel_id=1, source_target_pairs={{0,1},{1,0},{2,3},{3,2},{4,5},{5,4},{6,7},{7,6},{8,9},{9,8},{10,11... | collective-permute-start | bytes 294920 | tf_op jit(solution)/shard_map/ppermute | solution.py:479
  6.8 16.1 %collective-permute-start.1 = (f32[192,128]{1,0:T(8,128)S(1)}, f32[192,128]{1,0:T(8,128)S(1)}, u32[]{:S(2)}, u32[]{:S(2)}) collective-permute-start(f32[192,128]{1,0:T(8,128)S(1)} %get-tuple-element.49), channel_id=1, source_target_pairs={{0,15},{1,2},{2,1},{3,4},{4,3},{5,6},{6,5},{7,8},{8,7},{9,10},{10,... | collective-permute-start | bytes 294920 | tf_op jit(solution)/shard_map/ppermute | solution.py:479
  12.5 10.5 %collective-permute-start.4 = (f32[96,128]{1,0:T(8,128)S(1)}, f32[96,128]{1,0:T(8,128)S(1)}, u32[]{:S(2)}, u32[]{:S(2)}) collective-permute-start(f32[96,128]{1,0:T(8,128)S(1)} %get-tuple-element.52), channel_id=1, source_target_pairs={{0,64},{16,80},{32,96},{48,112},{64,0},{80,16},{96,32},{112,48},{1... | collective-permute-start | bytes 147464 | tf_op jit(solution)/shard_map/ppermute | solution.py:489
  16.3 3.8 %collective-permute-start.2 = (f32[48,128]{1,0:T(8,128)S(1)}, f32[48,128]{1,0:T(8,128)S(1)}, u32[]{:S(2)}, u32[]{:S(2)}) collective-permute-start(f32[48,128]{1,0:T(8,128)S(1)} %get-tuple-element.50), channel_id=1, source_target_pairs={{0,16},{16,0},{32,48},{48,32},{64,80},{80,64},{96,112},{112,96},{1... | collective-permute-start | bytes 73736 | tf_op jit(solution)/shard_map/ppermute | solution.py:479
  17.0 5.9 %collective-permute-start.3 = (f32[48,128]{1,0:T(8,128)S(1)}, f32[48,128]{1,0:T(8,128)S(1)}, u32[]{:S(2)}, u32[]{:S(2)}) collective-permute-start(f32[48,128]{1,0:T(8,128)S(1)} %get-tuple-element.51), channel_id=1, source_target_pairs={{0,112},{16,32},{32,16},{48,64},{64,48},{80,96},{96,80},{112,0},{1... | collective-permute-start | bytes 73736 | tf_op jit(solution)/shard_map/ppermute | solution.py:479
  24.1 8.0 %collective-permute-start.5 = (f32[192,128]{1,0:T(8,128)S(1)}, f32[192,128]{1,0:T(8,128)S(1)}, u32[]{:S(2)}, u32[]{:S(2)}) collective-permute-start(f32[192,128]{1,0:T(8,128)S(1)} %get-tuple-element.57), channel_id=1, source_target_pairs={{0,1},{1,0},{2,3},{3,2},{4,5},{5,4},{6,7},{7,6},{8,9},{9,8},{10,11... | collective-permute-start | bytes 294920 | tf_op jit(solution)/shard_map/ppermute | solution.py:479
  24.2 8.0 %collective-permute-start.6 = (f32[192,128]{1,0:T(8,128)S(1)}, f32[192,128]{1,0:T(8,128)S(1)}, u32[]{:S(2)}, u32[]{:S(2)}) collective-permute-start(f32[192,128]{1,0:T(8,128)S(1)} %get-tuple-element.58), channel_id=1, source_target_pairs={{0,15},{1,2},{2,1},{3,4},{4,3},{5,6},{6,5},{7,8},{8,7},{9,10},{10,... | collective-permute-start | bytes 294920 | tf_op jit(solution)/shard_map/ppermute | solution.py:479
  26.1 6.0 %collective-permute-start.9 = (f32[96,128]{1,0:T(8,128)S(1)}, f32[96,128]{1,0:T(8,128)S(1)}, u32[]{:S(2)}, u32[]{:S(2)}) collective-permute-start(f32[96,128]{1,0:T(8,128)S(1)} %get-tuple-element.61), channel_id=1, source_target_pairs={{0,64},{16,80},{32,96},{48,112},{64,0},{80,16},{96,32},{112,48},{1... | collective-permute-start | bytes 147464 | tf_op jit(solution)/shard_map/ppermute | solution.py:489
  26.1 3.9 %collective-permute-start.7 = (f32[48,128]{1,0:T(8,128)S(1)}, f32[48,128]{1,0:T(8,128)S(1)}, u32[]{:S(2)}, u32[]{:S(2)}) collective-permute-start(f32[48,128]{1,0:T(8,128)S(1)} %get-tuple-element.59), channel_id=1, source_target_pairs={{0,16},{16,0},{32,48},{48,32},{64,80},{80,64},{96,112},{112,96},{1... | collective-permute-start | bytes 73736 | tf_op jit(solution)/shard_map/ppermute | solution.py:479
  26.1 6.0 %collective-permute-start.8 = (f32[48,128]{1,0:T(8,128)S(1)}, f32[48,128]{1,0:T(8,128)S(1)}, u32[]{:S(2)}, u32[]{:S(2)}) collective-permute-start(f32[48,128]{1,0:T(8,128)S(1)} %get-tuple-element.60), channel_id=1, source_target_pairs={{0,112},{16,32},{32,16},{48,64},{64,48},{80,96},{96,80},{112,0},{1... | collective-permute-start | bytes 73736 | tf_op jit(solution)/shard_map/ppermute | solution.py:479
  33.0 10.7 %collective-permute-start.10 = (f32[192,128]{1,0:T(8,128)S(1)}, f32[192,128]{1,0:T(8,128)S(1)}, u32[]{:S(2)}, u32[]{:S(2)}) collective-permute-start(f32[192,128]{1,0:T(8,128)S(1)} %get-tuple-element.64), channel_id=1, source_target_pairs={{0,15},{1,0},{2,1},{3,2},{4,3},{5,4},{6,5},{7,6},{8,7},{9,8},{10,9... | collective-permute-start | bytes 294920 | tf_op jit(solution)/shard_map/ppermute | solution.py:484
  35.8 4.0 %collective-permute-start.11 = (f32[48,128]{1,0:T(8,128)S(1)}, f32[48,128]{1,0:T(8,128)S(1)}, u32[]{:S(2)}, u32[]{:S(2)}) collective-permute-start(f32[48,128]{1,0:T(8,128)S(1)} %get-tuple-element.65), channel_id=1, source_target_pairs={{0,112},{16,0},{32,16},{48,32},{64,48},{80,64},{96,80},{112,96},{1... | collective-permute-start | bytes 73736 | tf_op jit(solution)/shard_map/ppermute | solution.py:484
  38.4 5.3 %collective-permute-start.12 = (f32[48,128]{1,0:T(8,128)S(1)}, f32[48,128]{1,0:T(8,128)S(1)}, u32[]{:S(2)}, u32[]{:S(2)}) collective-permute-start(f32[48,128]{1,0:T(8,128)S(1)} %get-tuple-element.66), channel_id=1, source_target_pairs={{0,64},{16,80},{32,96},{48,112},{64,0},{80,16},{96,32},{112,48},{1... | collective-permute-start | bytes 73736 | tf_op jit(solution)/shard_map/ppermute | solution.py:489
  43.7 9.1 %copy-start.1 = (f32[4,2,3,3,4,1,4,128]{7,6,5,4,3,2,1,0:T(4,128)S(1)}, f32[4,2,3,3,4,1,4,128]{7,6,5,4,3,2,1,0:T(4,128)}, u32[]{:S(2)}) copy-start(f32[4,2,3,3,4,1,4,128]{7,6,5,4,3,2,1,0:T(4,128)} %param.6) | copy-start | bytes 1769476
  44.8 8.0 %collective-permute-start.13 = (f32[512,128]{1,0:T(8,128)S(1)}, f32[512,128]{1,0:T(8,128)S(1)}, u32[]{:S(2)}, u32[]{:S(2)}) collective-permute-start(f32[512,128]{1,0:T(8,128)S(1)} %get-tuple-element.68), channel_id=1, source_target_pairs={{0,64},{16,80},{32,96},{48,112},{64,0},{80,16},{96,32},{112,48},{1... | collective-permute-start | bytes 786440 | tf_op jit(solution)/shard_map/ppermute | solution.py:489
  54.0 7.7 %collective-permute-start.14 = (f32[192,128]{1,0:T(8,128)S(1)}, f32[192,128]{1,0:T(8,128)S(1)}, u32[]{:S(2)}, u32[]{:S(2)}) collective-permute-start(f32[192,128]{1,0:T(8,128)S(1)} %get-tuple-element.74), channel_id=1, source_target_pairs={{0,1},{1,2},{2,3},{3,4},{4,5},{5,6},{6,7},{7,8},{8,9},{9,10},{10,1... | collective-permute-start | bytes 294920 | tf_op jit(solution)/shard_map/ppermute | solution.py:484
  54.1 6.0 %collective-permute-start.15 = (f32[48,128]{1,0:T(8,128)S(1)}, f32[48,128]{1,0:T(8,128)S(1)}, u32[]{:S(2)}, u32[]{:S(2)}) collective-permute-start(f32[48,128]{1,0:T(8,128)S(1)} %get-tuple-element.75), channel_id=1, source_target_pairs={{0,16},{16,32},{32,48},{48,64},{64,80},{80,96},{96,112},{112,0},{1... | collective-permute-start | bytes 73736 | tf_op jit(solution)/shard_map/ppermute | solution.py:484
  54.2 5.9 %collective-permute-start.16 = (f32[48,128]{1,0:T(8,128)S(1)}, f32[48,128]{1,0:T(8,128)S(1)}, u32[]{:S(2)}, u32[]{:S(2)}) collective-permute-start(f32[48,128]{1,0:T(8,128)S(1)} %get-tuple-element.76), channel_id=1, source_target_pairs={{0,64},{16,80},{32,96},{48,112},{64,0},{80,16},{96,32},{112,48},{1... | collective-permute-start | bytes 73736 | tf_op jit(solution)/shard_map/ppermute | solution.py:489
  62.6 10.5 %collective-permute-start.17 = (f32[192,128]{1,0:T(8,128)S(1)}, f32[192,128]{1,0:T(8,128)S(1)}, u32[]{:S(2)}, u32[]{:S(2)}) collective-permute-start(f32[192,128]{1,0:T(8,128)S(1)} %get-tuple-element.79), channel_id=1, source_target_pairs={{0,15},{1,0},{2,1},{3,2},{4,3},{5,4},{6,5},{7,6},{8,7},{9,8},{10,9... | collective-permute-start | bytes 294920 | tf_op jit(solution)/shard_map/ppermute | solution.py:484
  65.2 4.2 %collective-permute-start.18 = (f32[48,128]{1,0:T(8,128)S(1)}, f32[48,128]{1,0:T(8,128)S(1)}, u32[]{:S(2)}, u32[]{:S(2)}) collective-permute-start(f32[48,128]{1,0:T(8,128)S(1)} %get-tuple-element.80), channel_id=1, source_target_pairs={{0,112},{16,0},{32,16},{48,32},{64,48},{80,64},{96,80},{112,96},{1... | collective-permute-start | bytes 73736 | tf_op jit(solution)/shard_map/ppermute | solution.py:484
  67.8 5.3 %collective-permute-start.19 = (f32[48,128]{1,0:T(8,128)S(1)}, f32[48,128]{1,0:T(8,128)S(1)}, u32[]{:S(2)}, u32[]{:S(2)}) collective-permute-start(f32[48,128]{1,0:T(8,128)S(1)} %get-tuple-element.81), channel_id=1, source_target_pairs={{0,64},{16,80},{32,96},{48,112},{64,0},{80,16},{96,32},{112,48},{1... | collective-permute-start | bytes 73736 | tf_op jit(solution)/shard_map/ppermute | solution.py:489
  74.3 8.0 %collective-permute-start.20 = (f32[512,128]{1,0:T(8,128)S(1)}, f32[512,128]{1,0:T(8,128)S(1)}, u32[]{:S(2)}, u32[]{:S(2)}) collective-permute-start(f32[512,128]{1,0:T(8,128)S(1)} %get-tuple-element.83), channel_id=1, source_target_pairs={{0,64},{16,80},{32,96},{48,112},{64,0},{80,16},{96,32},{112,48},{1... | collective-permute-start | bytes 786440 | tf_op jit(solution)/shard_map/ppermute | solution.py:489
where the time goes:
time: 84 us; the launch traced here: 83.7 us
  waiting for transfers between devices  38.9 us (46%)
  starting transfers between devices  30.1 us (36%)
  Pallas kernels  11.2 us (13%)
  local copies, waits for them, and re-layouts  2.73 us (3%)
    ppermute x7, waiting for transfers between devices, mirror_swap(): return lax.ppermute(value, 'xd', [(i, i ^ n // 2) for i in range(n)])  23.4 us
    ppermute x8, starting transfers between devices, swap(): return lax.ppermute(value, axis, pairs)  13.8 us
    pallas_call x8, Pallas kernels, call(): pl.pallas_call(kernel, name=name, out_shape=[jax.ShapeDtypeStruct((rows,...  11.2 us
    ppermute x6, starting transfers between devices, shift(): return lax.ppermute(value, axis, [(i, (i + by) % n) for i in range(n)])  10.7 us
    ppermute x6, waiting for transfers between devices, shift(): return lax.ppermute(value, axis, [(i, (i + by) % n) for i in range(n)])  9.07 us
    ppermute x8, waiting for transfers between devices, swap(): return lax.ppermute(value, axis, pairs)  6.51 us
    ppermute x7, starting transfers between devices, mirror_swap(): return lax.ppermute(value, 'xd', [(i, i ^ n // 2) for i in range(n)])  5.57 us
    unnamed x10, local copies, waits for them, and re-layouts  2.73 us
  transfers between devices with their start and end apart: 21, of which 11 were waited for; matrix products, arithmetic and copies ran while one was open for 0% of the time, Pallas kernels for 0%

commit v1 on v0

--- a/solution.py
+++ b/solution.py
@@ -4,6 +4,7 @@
 from jax.experimental import pallas as pl
 from jax.experimental.pallas import tpu as pltpu
 from jax.sharding import PartitionSpec as P
+
 
 HOPPING = 0.13
 STEP = 0.25
@@ -458,10 +459,9 @@
 FACE = 4 * 12
 
 
-def call(kernel, name, n_scalar, args, outs, scratch, limit=4):
+def call(kernel, n_scalar, args, outs, scratch, limit=4):
     return pl.pallas_call(
         kernel,
-        name=name,
         out_shape=[jax.ShapeDtypeStruct((rows, 128), F32) for rows in outs],
         in_specs=[SM] * n_scalar + [VM] * (len(args) - n_scalar),
         out_specs=[VM] * len(outs),
@@ -489,13 +489,48 @@
     return lax.ppermute(value, "xd", [(i, i ^ (n // 2)) for i in range(n)])
 
 
-def exchange(t_a, t_b, x_a, x_b, m):
-    far_t = swap(t_b, "ta", True)
-    mirrored = mirror_swap(m)
-    far_x = swap(x_b, "xd", True)
-    near_x = swap(x_a, "xd", False)
-    near_t = swap(t_a, "ta", False)
-    return near_t, far_t, near_x, far_x, mirrored
+def moved(name, value):
+    if name == "far_t":
+        return swap(value, "ta", True)
+    if name == "near_t":
+        return swap(value, "ta", False)
+    if name == "far_x":
+        return swap(value, "xd", True)
+    if name == "near_x":
+        return swap(value, "xd", False)
+    if name == "back_t":
+        return shift(value, "ta", -1)
+    if name == "back_x":
+        return shift(value, "xd", -1)
+    if name == "on_t":
+        return shift(value, "ta", 1)
+    if name == "on_x":
+        return shift(value, "xd", 1)
+    return mirror_swap(value)
+
+
+SWAP_ORDER = ("far_t", "mirror", "far_x", "near_x", "near_t")
+BACK_ORDER = ("back_t", "mirror", "back_x")
+ON_ORDER = ("on_t", "mirror", "on_x")
+
+
+def exchange(order, **values):
+    return {name: moved(name, values[name]) for name in order}
+
+
+def swap_exchange(t_a, t_b, x_a, x_b, m):
+    got = exchange(SWAP_ORDER, near_t=t_a, far_t=t_b, near_x=x_a, far_x=x_b, mirror=m)
+    return [got[name] for name in ("near_t", "far_t", "near_x", "far_x", "mirror")]
+
+
+def back_exchange(t, x, m):
+    got = exchange(BACK_ORDER, back_t=t, back_x=x, mirror=m)
+    return [got[name] for name in ("back_t", "back_x", "mirror")]
+
+
+def on_exchange(t, x, m):
+    got = exchange(ON_ORDER, on_t=t, on_x=x, mirror=m)
+    return [got[name] for name in ("on_t", "on_x", "mirror")]
 
 
 def per_device(gauge_links, momenta, noise_table, noise_index, partner):
@@ -524,37 +559,23 @@
 
     psi, *rest = call(
         noise_kernel,
-        "noise",
         2,
         (*s, index, table, u),
         [spin] + messages + local,
         [pltpu.VMEM((24, 4096), F32), pltpu.VMEM((384, 768), jnp.bfloat16), FULL, FULL],
         12,
     )
-    arrived = exchange(*rest[:5])
-    phi, *rest = call(
-        phi_kernel, "phi", 2, (*s, psi, u, *rest[5:], *arrived), [spin] + messages + local, halo + [FULL, FULL]
-    )
-    arrived = exchange(*rest[:5])
+    arrived = swap_exchange(*rest[:5])
+    phi, *rest = call(phi_kernel, 2, (*s, psi, u, *rest[5:], *arrived), [spin] + messages + local, halo + [FULL, FULL])
+    arrived = swap_exchange(*rest[:5])
     y, w, o_t, o_x, o_m = call(
-        response_kernel,
-        "response",
-        2,
-        (*s, phi, u, *rest[5:], *arrived),
-        [spin, 4 * FULL, FULL, FACE, FACE],
-        halo + [FULL],
+        response_kernel, 2, (*s, phi, u, *rest[5:], *arrived), [spin, 4 * FULL, FULL, FACE, FACE], halo + [FULL]
     )
     force, sent = call(
-        force_kernel,
-        "force",
-        2,
-        (*s, phi, u, y, w, shift(o_t, "ta", -1), shift(o_x, "xd", -1), mirror_swap(o_m)),
-        [32 * ROWS, 32 * ROWS],
-        [12 * HALO, FULL],
+        force_kernel, 2, (*s, phi, u, y, w, *back_exchange(o_t, o_x, o_m)), [32 * ROWS, 32 * ROWS], [12 * HALO, FULL]
     )
     u, p1, o_t, o_x, o_m, *q = call(
         update_kernel,
-        "update",
         2,
         (*s, phi, u, p, force, mirror_swap(sent)),
         [72 * ROWS, 36 * ROWS, FULL, FACE, FACE] + local,
@@ -562,23 +583,15 @@
     )
     y, w, o_t, o_x, o_m = call(
         response2_kernel,
-        "response2",
         2,
-        (*s, phi, u, *q, *arrived, shift(o_t, "ta", 1), shift(o_x, "xd", 1), mirror_swap(o_m)),
+        (*s, phi, u, *q, *arrived, *on_exchange(o_t, o_x, o_m)),
         [spin, 4 * FULL, FULL, FACE, FACE],
         halo + [FULL],
     )
     force, sent = call(
-        force_kernel,
-        "force2",
-        2,
-        (*s, phi, u, y, w, shift(o_t, "ta", -1), shift(o_x, "xd", -1), mirror_swap(o_m)),
-        [32 * ROWS, 32 * ROWS],
-        [12 * HALO, FULL],
-    )
-    new_u, new_p = call(
-        last_kernel, "last", 0, (u, p1, p, force, mirror_swap(sent)), [72 * ROWS, 72 * ROWS], []
-    )
+        force_kernel, 2, (*s, phi, u, y, w, *back_exchange(o_t, o_x, o_m)), [32 * ROWS, 32 * ROWS], [12 * HALO, FULL]
+    )
+    new_u, new_p = call(last_kernel, 0, (u, p1, p, force, mirror_swap(sent)), [72 * ROWS, 72 * ROWS], [])
     return new_u.reshape(gauge_links.shape), new_p.reshape(momenta.shape)
 
 

time: 84 us -> 84 us (level)
  no operation moved by 1% of the time
where the time goes in v1:
time: 84 us; the launch traced here: 83.7 us
  waiting for transfers between devices  38.9 us (46%)
  starting transfers between devices  30.1 us (36%)
  Pallas kernels  11.2 us (13%)
  local copies, waits for them, and re-layouts  2.73 us (3%)
    ppermute x7, waiting for transfers between devices, mirror_swap(): return lax.ppermute(value, 'xd', [(i, i ^ n // 2) for i in range(n)])  23.4 us
    ppermute x8, starting transfers between devices, swap(): return lax.ppermute(value, axis, pairs)  13.8 us
    pallas_call x8, Pallas kernels, call(): pl.pallas_call(kernel, out_shape=[jax.ShapeDtypeStruct((rows, 128), F32)...  11.2 us
    ppermute x6, starting transfers between devices, shift(): return lax.ppermute(value, axis, [(i, (i + by) % n) for i in range(n)])  10.7 us
    ppermute x6, waiting for transfers between devices, shift(): return lax.ppermute(value, axis, [(i, (i + by) % n) for i in range(n)])  9.07 us
    ppermute x8, waiting for transfers between devices, swap(): return lax.ppermute(value, axis, pairs)  6.51 us
    ppermute x7, starting transfers between devices, mirror_swap(): return lax.ppermute(value, 'xd', [(i, i ^ n // 2) for i in range(n)])  5.57 us
    unnamed x10, local copies, waits for them, and re-layouts  2.73 us
  transfers between devices with their start and end apart: 21, of which 11 were waited for; matrix products, arithmetic and copies ran while one was open for 0% of the time, Pallas kernels for 0%

profile of v1, /device:TPU:0, one launch (start us, length us, event | category | flops | bytes accessed | tf_op | source)
XLA Modules:
  0.0 83.7 jit_solution(15999884607889849832)
XLA Ops:
  1.3 1.1 %copy-done = f32[4,2,3,3,4,1,4,128]{7,6,5,4,3,2,1,0:T(4,128)S(1)} copy-done((f32[4,2,3,3,4,1,4,128]{7,6,5,4,3,2,1,0:T(4,128)S(1)}, f32[4,2,3,3,4,1,4,128]{7,6,5,4,3,2,1,0:T(4,128)}, u32[]{:S(2)}) %copy-start) | copy-done | bytes 589848
  2.4 1.0 %copy-done.2 = f32[2,4,3,4096]{3,1,2,0:T(4,128)S(1)} copy-done((f32[2,4,3,4096]{3,1,2,0:T(4,128)S(1)}, f32[2,4,3,4096]{3,1,2,0:T(4,128)}, u32[]{:S(2)}) %copy-start.2) | copy-done | bytes 393240
  3.4 3.3 %shard_map.68 = (f32[384,128]{1,0:T(8,128)S(1)}, f32[192,128]{1,0:T(8,128)S(1)}, f32[192,128]{1,0:T(8,128)S(1)}, f32[48,128]{1,0:T(8,128)S(1)}, f32[48,128]{1,0:...) custom-call(s32[8]{0:T(128)S(1)} %compare_select_fusion.2.table_i, ...), custom_call_target="tpu_custom_call" | custom-call | tf_op jit(solution)/shard_map/pallas_call | solution.py:463
  6.8 5.6 %collective-permute-start.1 = (f32[192,128]{1,0:T(8,128)S(1)}, f32[192,128]{1,0:T(8,128)S(1)}, u32[]{:S(2)}, u32[]{:S(2)}) collective-permute-start(f32[192,128]{1,0:T(8,128)S(1)} %get-tuple-element.49), channel_id=1, source_target_pairs={{0,15},{1,2},{2,1},{3,4},{4,3},{5,6},{6,5},{7,8},{8,7},{9,10},{10,... | collective-permute-start | bytes 294920 | tf_op jit(solution)/shard_map/ppermute | solution.py:479
  12.5 3.9 %collective-permute-start.4 = (f32[96,128]{1,0:T(8,128)S(1)}, f32[96,128]{1,0:T(8,128)S(1)}, u32[]{:S(2)}, u32[]{:S(2)}) collective-permute-start(f32[96,128]{1,0:T(8,128)S(1)} %get-tuple-element.52), channel_id=1, source_target_pairs={{0,64},{16,80},{32,96},{48,112},{64,0},{80,16},{96,32},{112,48},{1... | collective-permute-start | bytes 147464 | tf_op jit(solution)/shard_map/ppermute | solution.py:489
  16.3 0.7 collective-permute-start.2
  17.0 1.5 %collective-permute-start.3 = (f32[48,128]{1,0:T(8,128)S(1)}, f32[48,128]{1,0:T(8,128)S(1)}, u32[]{:S(2)}, u32[]{:S(2)}) collective-permute-start(f32[48,128]{1,0:T(8,128)S(1)} %get-tuple-element.51), channel_id=1, source_target_pairs={{0,112},{16,32},{32,16},{48,64},{64,48},{80,96},{96,80},{112,0},{1... | collective-permute-start | bytes 73736 | tf_op jit(solution)/shard_map/ppermute | solution.py:479
  18.5 1.7 %collective-permute-done.2.x_a = f32[48,128]{1,0:T(8,128)S(1)} collective-permute-done((f32[48,128]{1,0:T(8,128)S(1)}, f32[48,128]{1,0:T(8,128)S(1)}, u32[]{:S(2)}, u32[]{:S(2)}) %collective-permute-start.2) | collective-permute-done | bytes 24608 | tf_op jit(solution)/shard_map/ppermute | solution.py:479
  20.1 2.8 %collective-permute-done.3.x_b = f32[48,128]{1,0:T(8,128)S(1)} collective-permute-done((f32[48,128]{1,0:T(8,128)S(1)}, f32[48,128]{1,0:T(8,128)S(1)}, u32[]{:S(2)}, u32[]{:S(2)}) %collective-permute-start.3) | collective-permute-done | bytes 24608 | tf_op jit(solution)/shard_map/ppermute | solution.py:479
  22.9 1.1 %shard_map.69 = (f32[384,128]{1,0:T(8,128)S(1)}, f32[192,128]{1,0:T(8,128)S(1)}, f32[192,128]{1,0:T(8,128)S(1)}, f32[48,128]{1,0:T(8,128)S(1)}, f32[48,128]{1,0:...) custom-call(s32[8]{0:T(128)S(1)} %compare_select_fusion.2.table_i, ...), custom_call_target="tpu_custom_call" | custom-call | tf_op jit(solution)/shard_map/pallas_call | solution.py:463
  24.2 1.9 %collective-permute-start.6 = (f32[192,128]{1,0:T(8,128)S(1)}, f32[192,128]{1,0:T(8,128)S(1)}, u32[]{:S(2)}, u32[]{:S(2)}) collective-permute-start(f32[192,128]{1,0:T(8,128)S(1)} %get-tuple-element.58), channel_id=1, source_target_pairs={{0,15},{1,2},{2,1},{3,4},{4,3},{5,6},{6,5},{7,8},{8,7},{9,10},{10,... | collective-permute-start | bytes 294920 | tf_op jit(solution)/shard_map/ppermute | solution.py:479
  26.1 3.9 %collective-permute-start.8 = (f32[48,128]{1,0:T(8,128)S(1)}, f32[48,128]{1,0:T(8,128)S(1)}, u32[]{:S(2)}, u32[]{:S(2)}) collective-permute-start(f32[48,128]{1,0:T(8,128)S(1)} %get-tuple-element.60), channel_id=1, source_target_pairs={{0,112},{16,32},{32,16},{48,64},{64,48},{80,96},{96,80},{112,0},{1... | collective-permute-start | bytes 73736 | tf_op jit(solution)/shard_map/ppermute | solution.py:479
  30.1 2.1 %collective-permute-done.8.x_b = f32[48,128]{1,0:T(8,128)S(1)} collective-permute-done((f32[48,128]{1,0:T(8,128)S(1)}, f32[48,128]{1,0:T(8,128)S(1)}, u32[]{:S(2)}, u32[]{:S(2)}) %collective-permute-start.8) | collective-permute-done | bytes 24608 | tf_op jit(solution)/shard_map/ppermute | solution.py:479
  32.1 0.9 %shard_map.70 = (f32[384,128]{1,0:T(8,128)S(1)}, f32[768,128]{1,0:T(8,128)S(1)}, f32[192,128]{1,0:T(8,128)S(1)}, f32[48,128]{1,0:T(8,128)S(1)}, f32[48,128]{1,0:T(8,128)S(1)}) custom-call(s32[8]{0:T(128)S(1)} %compare_select_fusion.2.table_i, s32[4]{0:T(128)S(1)} %copy-done.3, f32[384,128]{1,0:T(8,128)S(1)} %get-tuple-element.53.phi, ...), custom_call_target="tpu_custom_call" | custom-call | tf_op jit(solution)/shard_map/pallas_call | solution.py:463
  33.0 2.8 %collective-permute-start.10 = (f32[192,128]{1,0:T(8,128)S(1)}, f32[192,128]{1,0:T(8,128)S(1)}, u32[]{:S(2)}, u32[]{:S(2)}) collective-permute-start(f32[192,128]{1,0:T(8,128)S(1)} %get-tuple-element.64), channel_id=1, source_target_pairs={{0,15},{1,0},{2,1},{3,2},{4,3},{5,4},{6,5},{7,6},{8,7},{9,8},{10,9... | collective-permute-start | bytes 294920 | tf_op jit(solution)/shard_map/ppermute | solution.py:484
  35.8 2.5 %collective-permute-start.11 = (f32[48,128]{1,0:T(8,128)S(1)}, f32[48,128]{1,0:T(8,128)S(1)}, u32[]{:S(2)}, u32[]{:S(2)}) collective-permute-start(f32[48,128]{1,0:T(8,128)S(1)} %get-tuple-element.65), channel_id=1, source_target_pairs={{0,112},{16,0},{32,16},{48,32},{64,48},{80,64},{96,80},{112,96},{1... | collective-permute-start | bytes 73736 | tf_op jit(solution)/shard_map/ppermute | solution.py:484
  38.4 1.5 %collective-permute-done.11.r_x = f32[48,128]{1,0:T(8,128)S(1)} collective-permute-done((f32[48,128]{1,0:T(8,128)S(1)}, f32[48,128]{1,0:T(8,128)S(1)}, u32[]{:S(2)}, u32[]{:S(2)}) %collective-permute-start.11) | collective-permute-done | bytes 24608 | tf_op jit(solution)/shard_map/ppermute | solution.py:484
  39.9 3.8 %collective-permute-done.12.r_m = f32[48,128]{1,0:T(8,128)S(1)} collective-permute-done((f32[48,128]{1,0:T(8,128)S(1)}, f32[48,128]{1,0:T(8,128)S(1)}, u32[]{:S(2)}, u32[]{:S(2)}) %collective-permute-start.12) | collective-permute-done | bytes 24608 | tf_op jit(solution)/shard_map/ppermute | solution.py:489
  43.7 1.1 %shard_map.71 = (f32[512,128]{1,0:T(8,128)S(1)}, f32[512,128]{1,0:T(8,128)S(1)}) custom-call(s32[8]{0:T(128)S(1)} %compare_select_fusion.2.table_i, s32[4]{0:T(128)S(1)} %copy-done.3, f32[384,128]{1,0:T(8,128)S(1)} %get-tuple-element.53.phi, f32[1152,128]{1,0:T(8,128)S(1)} %bitcast.13, f32[384,128]{1,0:T(8,128)S(1)} %get-tuple-element.62.y, ...), custom_call_target="tpu_custom_call" | custom-call | tf_op jit(solution)/shard_map/pallas_call | solution.py:463
  44.9 7.9 %collective-permute-done.13.mirrored = f32[512,128]{1,0:T(8,128)S(1)} collective-permute-done((f32[512,128]{1,0:T(8,128)S(1)}, f32[512,128]{1,0:T(8,128)S(1)}, u32[]{:S(2)}, u32[]{:S(2)}) %collective-permute-start.13) | collective-permute-done | bytes 262176 | tf_op jit(solution)/shard_map/ppermute | solution.py:489
  52.7 1.3 %shard_map.72 = (f32[1152,128]{1,0:T(8,128)S(1)}, f32[576,128]{1,0:T(8,128)S(1)}, f32[192,128]{1,0:T(8,128)S(1)}, f32[48,128]{1,0:T(8,128)S(1)}, f32[48,128]{1,0...) custom-call(s32[8]{0:T(128)S(1)} %compare_select_fusion.2.table_i, ...), custom_call_target="tpu_custom_call" | custom-call | tf_op jit(solution)/shard_map/pallas_call | solution.py:463
  54.2 1.5 %collective-permute-start.16 = (f32[48,128]{1,0:T(8,128)S(1)}, f32[48,128]{1,0:T(8,128)S(1)}, u32[]{:S(2)}, u32[]{:S(2)}) collective-permute-start(f32[48,128]{1,0:T(8,128)S(1)} %get-tuple-element.76), channel_id=1, source_target_pairs={{0,64},{16,80},{32,96},{48,112},{64,0},{80,16},{96,32},{112,48},{1... | collective-permute-start | bytes 73736 | tf_op jit(solution)/shard_map/ppermute | solution.py:489
  55.7 4.4 %collective-permute-done.15.b_x = f32[48,128]{1,0:T(8,128)S(1)} collective-permute-done((f32[48,128]{1,0:T(8,128)S(1)}, f32[48,128]{1,0:T(8,128)S(1)}, u32[]{:S(2)}, u32[]{:S(2)}) %collective-permute-start.15) | collective-permute-done | bytes 24608 | tf_op jit(solution)/shard_map/ppermute | solution.py:484
  60.1 1.6 %collective-permute-done.14.b_t = f32[192,128]{1,0:T(8,128)S(1)} collective-permute-done((f32[192,128]{1,0:T(8,128)S(1)}, f32[192,128]{1,0:T(8,128)S(1)}, u32[]{:S(2)}, u32[]{:S(2)}) %collective-permute-start.14) | collective-permute-done | bytes 98336 | tf_op jit(solution)/shard_map/ppermute | solution.py:484
  61.7 0.9 %shard_map.73 = (f32[384,128]{1,0:T(8,128)S(1)}, f32[768,128]{1,0:T(8,128)S(1)}, f32[192,128]{1,0:T(8,128)S(1)}, f32[48,128]{1,0:T(8,128)S(1)}, f32[48,128]{1,0:T(8,128)S(1)}) custom-call(s32[8]{0:T(128)S(1)} %compare_select_fusion.2.table_i, s32[4]{0:T(128)S(1)} %copy-done.3, f32[384,128]{1,0:T(8,128)S(1)} %get-tuple-element.53.phi, ...), custom_call_target="tpu_custom_call" | custom-call | tf_op jit(solution)/shard_map/pallas_call | solution.py:463
  62.6 2.6 %collective-permute-start.17 = (f32[192,128]{1,0:T(8,128)S(1)}, f32[192,128]{1,0:T(8,128)S(1)}, u32[]{:S(2)}, u32[]{:S(2)}) collective-permute-start(f32[192,128]{1,0:T(8,128)S(1)} %get-tuple-element.79), channel_id=1, source_target_pairs={{0,15},{1,0},{2,1},{3,2},{4,3},{5,4},{6,5},{7,6},{8,7},{9,8},{10,9... | collective-permute-start | bytes 294920 | tf_op jit(solution)/shard_map/ppermute | solution.py:484
  65.2 2.6 %collective-permute-start.18 = (f32[48,128]{1,0:T(8,128)S(1)}, f32[48,128]{1,0:T(8,128)S(1)}, u32[]{:S(2)}, u32[]{:S(2)}) collective-permute-start(f32[48,128]{1,0:T(8,128)S(1)} %get-tuple-element.80), channel_id=1, source_target_pairs={{0,112},{16,0},{32,16},{48,32},{64,48},{80,64},{96,80},{112,96},{1... | collective-permute-start | bytes 73736 | tf_op jit(solution)/shard_map/ppermute | solution.py:484
  67.8 1.5 %collective-permute-done.18.r_x = f32[48,128]{1,0:T(8,128)S(1)} collective-permute-done((f32[48,128]{1,0:T(8,128)S(1)}, f32[48,128]{1,0:T(8,128)S(1)}, u32[]{:S(2)}, u32[]{:S(2)}) %collective-permute-start.18) | collective-permute-done | bytes 24608 | tf_op jit(solution)/shard_map/ppermute | solution.py:484
  69.4 3.8 %collective-permute-done.19.r_m = f32[48,128]{1,0:T(8,128)S(1)} collective-permute-done((f32[48,128]{1,0:T(8,128)S(1)}, f32[48,128]{1,0:T(8,128)S(1)}, u32[]{:S(2)}, u32[]{:S(2)}) %collective-permute-start.19) | collective-permute-done | bytes 24608 | tf_op jit(solution)/shard_map/ppermute | solution.py:489
  73.2 1.1 %shard_map.74 = (f32[512,128]{1,0:T(8,128)S(1)}, f32[512,128]{1,0:T(8,128)S(1)}) custom-call(s32[8]{0:T(128)S(1)} %compare_select_fusion.2.table_i, s32[4]{0:T(128)S(1)} %copy-done.3, f32[384,128]{1,0:T(8,128)S(1)} %get-tuple-element.53.phi, f32[1152,128]{1,0:T(8,128)S(1)} %get-tuple-element.69.u, f32[384,128]{1,0:T(8,128)S(1)} %get-tuple-element.77.y, ...), custom_call_target="tpu_custom_call" | custom-call | tf_op jit(solution)/shard_map/pallas_call | solution.py:463
  74.4 7.9 %collective-permute-done.20.mirrored = f32[512,128]{1,0:T(8,128)S(1)} collective-permute-done((f32[512,128]{1,0:T(8,128)S(1)}, f32[512,128]{1,0:T(8,128)S(1)}, u32[]{:S(2)}, u32[]{:S(2)}) %collective-permute-start.20) | collective-permute-done | bytes 262176 | tf_op jit(solution)/shard_map/ppermute | solution.py:489
  82.2 1.5 %shard_map.75 = (f32[1152,128]{1,0:T(8,128)}, f32[1152,128]{1,0:T(8,128)}) custom-call(f32[1152,128]{1,0:T(8,128)S(1)} %get-tuple-element.69.u, f32[576,128]{1,0:T(8,128)S(1)} %get-tuple-element.70.p, f32[1152,128]{1,0:T(8,128)S(1)} %bitcast.16, f32[512,128]{1,0:T(8,128)S(1)} %get-tuple-element.82.force, f32[512,128]{1,0:T(8,128)S(1)} %collective-permute-done.20.mirrored), custom_call_target="tpu_custom_call" | custom-call | tf_op jit(solution)/shard_map/pallas_call | solution.py:463
  (29 shorter events, 1.2 us)
Async XLA Ops:
  0.6 0.7 copy-start.4
  0.7 0.7 copy-start.3
  1.3 1.1 %copy-start = (f32[4,2,3,3,4,1,4,128]{7,6,5,4,3,2,1,0:T(4,128)S(1)}, f32[4,2,3,3,4,1,4,128]{7,6,5,4,3,2,1,0:T(4,128)}, u32[]{:S(2)}) copy-start(f32[4,2,3,3,4,1,4,128]{7,6,5,4,3,2,1,0:T(4,128)} %param.5) | copy-start | bytes 1769476
  2.4 1.0 %copy-start.2 = (f32[2,4,3,4096]{3,1,2,0:T(4,128)S(1)}, f32[2,4,3,4096]{3,1,2,0:T(4,128)}, u32[]{:S(2)}) copy-start(f32[2,4,3,4096]{3,1,2,0:T(4,128)} %param.7) | copy-start | bytes 1179652
  6.8 16.2 %collective-permute-start = (f32[192,128]{1,0:T(8,128)S(1)}, f32[192,128]{1,0:T(8,128)S(1)}, u32[]{:S(2)}, u32[]{:S(2)}) collective-permute-start(f32[192,128]{1,0:T(8,128)S(1)} %get-tuple-element.48), channel_id=1, source_target_pairs={{0,1},{1,0},{2,3},{3,2},{4,5},{5,4},{6,7},{7,6},{8,9},{9,8},{10,11... | collective-permute-start | bytes 294920 | tf_op jit(solution)/shard_map/ppermute | solution.py:479
  6.8 16.1 %collective-permute-start.1 = (f32[192,128]{1,0:T(8,128)S(1)}, f32[192,128]{1,0:T(8,128)S(1)}, u32[]{:S(2)}, u32[]{:S(2)}) collective-permute-start(f32[192,128]{1,0:T(8,128)S(1)} %get-tuple-element.49), channel_id=1, source_target_pairs={{0,15},{1,2},{2,1},{3,4},{4,3},{5,6},{6,5},{7,8},{8,7},{9,10},{10,... | collective-permute-start | bytes 294920 | tf_op jit(solution)/shard_map/ppermute | solution.py:479
  12.5 10.5 %collective-permute-start.4 = (f32[96,128]{1,0:T(8,128)S(1)}, f32[96,128]{1,0:T(8,128)S(1)}, u32[]{:S(2)}, u32[]{:S(2)}) collective-permute-start(f32[96,128]{1,0:T(8,128)S(1)} %get-tuple-element.52), channel_id=1, source_target_pairs={{0,64},{16,80},{32,96},{48,112},{64,0},{80,16},{96,32},{112,48},{1... | collective-permute-start | bytes 147464 | tf_op jit(solution)/shard_map/ppermute | solution.py:489
  16.3 3.8 %collective-permute-start.2 = (f32[48,128]{1,0:T(8,128)S(1)}, f32[48,128]{1,0:T(8,128)S(1)}, u32[]{:S(2)}, u32[]{:S(2)}) collective-permute-start(f32[48,128]{1,0:T(8,128)S(1)} %get-tuple-element.50), channel_id=1, source_target_pairs={{0,16},{16,0},{32,48},{48,32},{64,80},{80,64},{96,112},{112,96},{1... | collective-permute-start | bytes 73736 | tf_op jit(solution)/shard_map/ppermute | solution.py:479
  17.0 5.9 %collective-permute-start.3 = (f32[48,128]{1,0:T(8,128)S(1)}, f32[48,128]{1,0:T(8,128)S(1)}, u32[]{:S(2)}, u32[]{:S(2)}) collective-permute-start(f32[48,128]{1,0:T(8,128)S(1)} %get-tuple-element.51), channel_id=1, source_target_pairs={{0,112},{16,32},{32,16},{48,64},{64,48},{80,96},{96,80},{112,0},{1... | collective-permute-start | bytes 73736 | tf_op jit(solution)/shard_map/ppermute | solution.py:479
  24.1 8.0 %collective-permute-start.5 = (f32[192,128]{1,0:T(8,128)S(1)}, f32[192,128]{1,0:T(8,128)S(1)}, u32[]{:S(2)}, u32[]{:S(2)}) collective-permute-start(f32[192,128]{1,0:T(8,128)S(1)} %get-tuple-element.57), channel_id=1, source_target_pairs={{0,1},{1,0},{2,3},{3,2},{4,5},{5,4},{6,7},{7,6},{8,9},{9,8},{10,11... | collective-permute-start | bytes 294920 | tf_op jit(solution)/shard_map/ppermute | solution.py:479
  24.2 8.0 %collective-permute-start.6 = (f32[192,128]{1,0:T(8,128)S(1)}, f32[192,128]{1,0:T(8,128)S(1)}, u32[]{:S(2)}, u32[]{:S(2)}) collective-permute-start(f32[192,128]{1,0:T(8,128)S(1)} %get-tuple-element.58), channel_id=1, source_target_pairs={{0,15},{1,2},{2,1},{3,4},{4,3},{5,6},{6,5},{7,8},{8,7},{9,10},{10,... | collective-permute-start | bytes 294920 | tf_op jit(solution)/shard_map/ppermute | solution.py:479
  26.1 6.0 %collective-permute-start.9 = (f32[96,128]{1,0:T(8,128)S(1)}, f32[96,128]{1,0:T(8,128)S(1)}, u32[]{:S(2)}, u32[]{:S(2)}) collective-permute-start(f32[96,128]{1,0:T(8,128)S(1)} %get-tuple-element.61), channel_id=1, source_target_pairs={{0,64},{16,80},{32,96},{48,112},{64,0},{80,16},{96,32},{112,48},{1... | collective-permute-start | bytes 147464 | tf_op jit(solution)/shard_map/ppermute | solution.py:489
  26.1 3.9 %collective-permute-start.7 = (f32[48,128]{1,0:T(8,128)S(1)}, f32[48,128]{1,0:T(8,128)S(1)}, u32[]{:S(2)}, u32[]{:S(2)}) collective-permute-start(f32[48,128]{1,0:T(8,128)S(1)} %get-tuple-element.59), channel_id=1, source_target_pairs={{0,16},{16,0},{32,48},{48,32},{64,80},{80,64},{96,112},{112,96},{1... | collective-permute-start | bytes 73736 | tf_op jit(solution)/shard_map/ppermute | solution.py:479
  26.1 6.0 %collective-permute-start.8 = (f32[48,128]{1,0:T(8,128)S(1)}, f32[48,128]{1,0:T(8,128)S(1)}, u32[]{:S(2)}, u32[]{:S(2)}) collective-permute-start(f32[48,128]{1,0:T(8,128)S(1)} %get-tuple-element.60), channel_id=1, source_target_pairs={{0,112},{16,32},{32,16},{48,64},{64,48},{80,96},{96,80},{112,0},{1... | collective-permute-start | bytes 73736 | tf_op jit(solution)/shard_map/ppermute | solution.py:479
  33.0 10.7 %collective-permute-start.10 = (f32[192,128]{1,0:T(8,128)S(1)}, f32[192,128]{1,0:T(8,128)S(1)}, u32[]{:S(2)}, u32[]{:S(2)}) collective-permute-start(f32[192,128]{1,0:T(8,128)S(1)} %get-tuple-element.64), channel_id=1, source_target_pairs={{0,15},{1,0},{2,1},{3,2},{4,3},{5,4},{6,5},{7,6},{8,7},{9,8},{10,9... | collective-permute-start | bytes 294920 | tf_op jit(solution)/shard_map/ppermute | solution.py:484
  35.8 4.0 %collective-permute-start.11 = (f32[48,128]{1,0:T(8,128)S(1)}, f32[48,128]{1,0:T(8,128)S(1)}, u32[]{:S(2)}, u32[]{:S(2)}) collective-permute-start(f32[48,128]{1,0:T(8,128)S(1)} %get-tuple-element.65), channel_id=1, source_target_pairs={{0,112},{16,0},{32,16},{48,32},{64,48},{80,64},{96,80},{112,96},{1... | collective-permute-start | bytes 73736 | tf_op jit(solution)/shard_map/ppermute | solution.py:484
  38.4 5.3 %collective-permute-start.12 = (f32[48,128]{1,0:T(8,128)S(1)}, f32[48,128]{1,0:T(8,128)S(1)}, u32[]{:S(2)}, u32[]{:S(2)}) collective-permute-start(f32[48,128]{1,0:T(8,128)S(1)} %get-tuple-element.66), channel_id=1, source_target_pairs={{0,64},{16,80},{32,96},{48,112},{64,0},{80,16},{96,32},{112,48},{1... | collective-permute-start | bytes 73736 | tf_op jit(solution)/shard_map/ppermute | solution.py:489
  43.7 9.1 %copy-start.1 = (f32[4,2,3,3,4,1,4,128]{7,6,5,4,3,2,1,0:T(4,128)S(1)}, f32[4,2,3,3,4,1,4,128]{7,6,5,4,3,2,1,0:T(4,128)}, u32[]{:S(2)}) copy-start(f32[4,2,3,3,4,1,4,128]{7,6,5,4,3,2,1,0:T(4,128)} %param.6) | copy-start | bytes 1769476
  44.8 8.0 %collective-permute-start.13 = (f32[512,128]{1,0:T(8,128)S(1)}, f32[512,128]{1,0:T(8,128)S(1)}, u32[]{:S(2)}, u32[]{:S(2)}) collective-permute-start(f32[512,128]{1,0:T(8,128)S(1)} %get-tuple-element.68), channel_id=1, source_target_pairs={{0,64},{16,80},{32,96},{48,112},{64,0},{80,16},{96,32},{112,48},{1... | collective-permute-start | bytes 786440 | tf_op jit(solution)/shard_map/ppermute | solution.py:489
  54.0 7.7 %collective-permute-start.14 = (f32[192,128]{1,0:T(8,128)S(1)}, f32[192,128]{1,0:T(8,128)S(1)}, u32[]{:S(2)}, u32[]{:S(2)}) collective-permute-start(f32[192,128]{1,0:T(8,128)S(1)} %get-tuple-element.74), channel_id=1, source_target_pairs={{0,1},{1,2},{2,3},{3,4},{4,5},{5,6},{6,7},{7,8},{8,9},{9,10},{10,1... | collective-permute-start | bytes 294920 | tf_op jit(solution)/shard_map/ppermute | solution.py:484
  54.1 6.0 %collective-permute-start.15 = (f32[48,128]{1,0:T(8,128)S(1)}, f32[48,128]{1,0:T(8,128)S(1)}, u32[]{:S(2)}, u32[]{:S(2)}) collective-permute-start(f32[48,128]{1,0:T(8,128)S(1)} %get-tuple-element.75), channel_id=1, source_target_pairs={{0,16},{16,32},{32,48},{48,64},{64,80},{80,96},{96,112},{112,0},{1... | collective-permute-start | bytes 73736 | tf_op jit(solution)/shard_map/ppermute | solution.py:484
  54.2 5.9 %collective-permute-start.16 = (f32[48,128]{1,0:T(8,128)S(1)}, f32[48,128]{1,0:T(8,128)S(1)}, u32[]{:S(2)}, u32[]{:S(2)}) collective-permute-start(f32[48,128]{1,0:T(8,128)S(1)} %get-tuple-element.76), channel_id=1, source_target_pairs={{0,64},{16,80},{32,96},{48,112},{64,0},{80,16},{96,32},{112,48},{1... | collective-permute-start | bytes 73736 | tf_op jit(solution)/shard_map/ppermute | solution.py:489
  62.6 10.5 %collective-permute-start.17 = (f32[192,128]{1,0:T(8,128)S(1)}, f32[192,128]{1,0:T(8,128)S(1)}, u32[]{:S(2)}, u32[]{:S(2)}) collective-permute-start(f32[192,128]{1,0:T(8,128)S(1)} %get-tuple-element.79), channel_id=1, source_target_pairs={{0,15},{1,0},{2,1},{3,2},{4,3},{5,4},{6,5},{7,6},{8,7},{9,8},{10,9... | collective-permute-start | bytes 294920 | tf_op jit(solution)/shard_map/ppermute | solution.py:484
  65.2 4.2 %collective-permute-start.18 = (f32[48,128]{1,0:T(8,128)S(1)}, f32[48,128]{1,0:T(8,128)S(1)}, u32[]{:S(2)}, u32[]{:S(2)}) collective-permute-start(f32[48,128]{1,0:T(8,128)S(1)} %get-tuple-element.80), channel_id=1, source_target_pairs={{0,112},{16,0},{32,16},{48,32},{64,48},{80,64},{96,80},{112,96},{1... | collective-permute-start | bytes 73736 | tf_op jit(solution)/shard_map/ppermute | solution.py:484
  67.8 5.3 %collective-permute-start.19 = (f32[48,128]{1,0:T(8,128)S(1)}, f32[48,128]{1,0:T(8,128)S(1)}, u32[]{:S(2)}, u32[]{:S(2)}) collective-permute-start(f32[48,128]{1,0:T(8,128)S(1)} %get-tuple-element.81), channel_id=1, source_target_pairs={{0,64},{16,80},{32,96},{48,112},{64,0},{80,16},{96,32},{112,48},{1... | collective-permute-start | bytes 73736 | tf_op jit(solution)/shard_map/ppermute | solution.py:489
  74.3 8.0 %collective-permute-start.20 = (f32[512,128]{1,0:T(8,128)S(1)}, f32[512,128]{1,0:T(8,128)S(1)}, u32[]{:S(2)}, u32[]{:S(2)}) collective-permute-start(f32[512,128]{1,0:T(8,128)S(1)} %get-tuple-element.83), channel_id=1, source_target_pairs={{0,64},{16,80},{32,96},{48,112},{64,0},{80,16},{96,32},{112,48},{1... | collective-permute-start | bytes 786440 | tf_op jit(solution)/shard_map/ppermute | solution.py:489

commit v2 on v1

--- a/solution.py
+++ b/solution.py
@@ -295,11 +295,41 @@
     send_response(y, info, o_t, o_x, o_m, h2)
 
 
-def force_kernel(table_i, partner, phi, u, y, w, r_t, r_x, r_m, force, sent, a0, fa):
+OFF = ((0, 1), (0, 2), (1, 2))
+EARLY = (0, 2, 3)
+
+
+def force_values(left, right):
+    def g_im(i, j):
+        return sum(left[n][i][1] * right[n][j][0] - left[n][i][0] * right[n][j][1] for n in range(4))
+
+    def g_re(i, j):
+        return sum(left[n][i][0] * right[n][j][0] + left[n][i][1] * right[n][j][1] for n in range(4))
+
+    d = [g_im(i, i) for i in range(3)]
+    third = (d[0] + d[1] + d[2]) * (1.0 / 3.0)
+    scale = -2.0 * HOPPING
+    values = [scale * (d[0] - third), scale * (d[1] - third)]
+    for i, j in OFF:
+        values.append((0.5 * scale) * (g_im(i, j) + g_im(j, i)))
+        values.append((0.5 * scale) * (g_re(j, i) - g_re(i, j)))
+    return values
+
+
+def force_at(at, phi, u, y, w, mu, x):
+    ysp = [[(at(y, c * 4 + s), at(y, 12 + c * 4 + s)) for c in range(3)] for s in range(4)]
+    psp = [[(at(phi, c * 4 + s), at(phi, 12 + c * 4 + s)) for c in range(3)] for s in range(4)]
+    link = [[(at(u, mu * 18 + i * 3 + j), at(u, mu * 18 + 9 + i * 3 + j)) for j in range(3)] for i in range(3)]
+    left = mat_half(link, x(ysp)) + get_half(lambda k: at(w, mu * 12 + k))
+    right = project(psp, mu, -1) + project(ysp, mu, 1)
+    return force_values(left, right)
+
+
+def early_force_kernel(table_i, partner, phi, u, y, w, force, sent, a0):
     info = Info(table_i, partner)
+    nothing = jnp.zeros((4, 128), F32)
     for k in range(12):
-        a0[k * HALO + 16 : k * HALO + 20, :] = r_x[k * 4 : k * 4 + 4, :]
-        fa[pl.ds(k * ROWS + 3, 4, stride=4), :] = r_m[k * 4 : k * 4 + 4, :]
+        a0[k * HALO + 16 : k * HALO + 20, :] = nothing
     for h in range(2):
         v = project(spinor(y, h), 0, -1)
         for t in range(2):
@@ -307,57 +337,85 @@
                 for part in range(2):
                     k = half_index(part, t, c)
                     a0[k * HALO + 8 * h : k * HALO + 8 * h + 8, :] = v[t][c][part]
-    x2 = row_in_pair()
-    for h in range(2):
-        ysp = spinor(y, h)
-        psp = spinor(phi, h)
-        for mu in range(4):
+    for h in range(2):
+        for e, mu in enumerate(EARLY):
             if mu == 0:
-                x = get_half(lambda k: a0[k * HALO + 8 * h + 4 : k * HALO + 8 * h + 12, :])
-            elif mu == 1:
-                x = get_half(lambda k: ld(r_t, k, h))
+                x = lambda ysp: get_half(lambda k: a0[k * HALO + 8 * h + 4 : k * HALO + 8 * h + 12, :])
             elif mu == 2:
-                face = get_half(lambda k: ld(fa, k, h))
-                x = map_half(
-                    lambda r, f: jnp.where(x2 == 3, f, pltpu.roll(r, 7, 0)), project(ysp, 2, -1), face
-                )
+                x = lambda ysp: map_half(lambda r: pltpu.roll(r, 7, 0), project(ysp, 2, -1))
             else:
-                x = map_half(lambda r: pltpu.roll(r, 127, 1), project(ysp, 3, -1))
-            left = mat_half(matrix(u, mu, h), x) + get_half(lambda k: ld(w, mu * 12 + k, h))
-            right = project(psp, mu, -1) + project(ysp, mu, 1)
-
-            def g_im(i, j):
-                return sum(left[n][i][1] * right[n][j][0] - left[n][i][0] * right[n][j][1] for n in range(4))
-
-            def g_re(i, j):
-                return sum(left[n][i][0] * right[n][j][0] + left[n][i][1] * right[n][j][1] for n in range(4))
-
-            d = [g_im(i, i) for i in range(3)]
-            third = (d[0] + d[1] + d[2]) * (1.0 / 3.0)
-            scale = -2.0 * HOPPING
-            values = [scale * (d[0] - third), scale * (d[1] - third)]
-            for i, j in ((0, 1), (0, 2), (1, 2)):
-                values.append((0.5 * scale) * (g_im(i, j) + g_im(j, i)))
-                values.append((0.5 * scale) * (g_re(j, i) - g_re(i, j)))
-            for n, value in enumerate(values):
-                st(force, mu * 8 + n, h, value)
-    for k in range(32):
+                x = lambda ysp: map_half(lambda r: pltpu.roll(r, 127, 1), project(ysp, 3, -1))
+            for n, value in enumerate(force_at(lambda ref, k: ld(ref, k, h), phi, u, y, w, mu, x)):
+                st(force, e * 8 + n, h, value)
+    for k in range(24):
+        send_blocks(sent, k, force, k, info)
+
+
+def send_blocks(dst, base, src, k, info):
+    for j in range(4):
+        at = pl.multiple_of(base * ROWS + 4 * info.partner[j], 4)
+        dst[pl.ds(at, 4), :] = src[k * ROWS + 4 * j : k * ROWS + 4 * j + 4, :]
+
+
+def late_force_kernel(table_i, partner, phi, u, y, w, r_t, r_x, r_m, f_t, f_x, f_m, sent):
+    info = Info(table_i, partner)
+    for h in range(2):
+        arrived = get_half(lambda k: ld(r_t, k, h))
+        for n, value in enumerate(force_at(lambda ref, k: ld(ref, k, h), phi, u, y, w, 1, lambda ysp: arrived)):
+            st(f_t, n, h, value)
+    for n in range(8):
+        send_blocks(sent, n, f_t, n, info)
+    face = lambda ref: get_half(lambda k: ref[k * 4 : k * 4 + 4, :])
+    last_x = lambda ref, k: ref[k * ROWS + 12 : k * ROWS + 16, :]
+    for n, value in enumerate(force_at(last_x, phi, u, y, w, 0, lambda ysp: face(r_x))):
+        f_x[n * ROWS + 12 : n * ROWS + 16, :] = value
+        sent[8 * ROWS + n * 4 : 8 * ROWS + n * 4 + 4, :] = value
+    last_m = lambda ref, k: ref[pl.ds(k * ROWS + 3, 4, stride=4), :]
+    for n, value in enumerate(force_at(last_m, phi, u, y, w, 2, lambda ysp: face(r_m))):
+        f_m[pl.ds(n * ROWS + 3, 4, stride=4), :] = value
+    for n in range(8):
         for j in range(4):
-            at = pl.multiple_of(k * ROWS + 4 * info.partner[j], 4)
-            sent[pl.ds(at, 4), :] = force[k * ROWS + 4 * j : k * ROWS + 4 * j + 4, :]
-
-
-OFF = ((0, 1), (0, 2), (1, 2))
-
-
-def updated_momenta(read, force, mirrored, mu, h):
-    diag_force = [ld(force, mu * 8 + n, h) - ld(mirrored, mu * 8 + n, h) for n in range(2)]
+            row = 8 * ROWS + 32 + n * 4 + info.partner[j]
+            sent[pl.ds(row, 1), :] = f_m[n * ROWS + 4 * j + 3 : n * ROWS + 4 * j + 4, :]
+
+
+def place_faces(info, mirrored, m_x, m_m):
+    block = jnp.int32(0)
+    for j in range(4):
+        block = block + jnp.where(info.partner[j] == 3, j, 0)
+    for n in range(8):
+        at = pl.multiple_of(n * ROWS + 4 * block, 4)
+        m_x[pl.ds(at, 4), :] = mirrored[8 * ROWS + n * 4 : 8 * ROWS + n * 4 + 4, :]
+        m_m[pl.ds(n * ROWS + 3, 4, stride=4), :] = mirrored[8 * ROWS + 32 + n * 4 : 8 * ROWS + 32 + n * 4 + 4, :]
+    return block
+
+
+def both_forces(mu, h, block, early, mirror_early, f_t, f_x, f_m, mirrored, m_x, m_m):
+    row = lax.broadcasted_iota(jnp.int32, (8, 128), 0)
+    if mu == 1:
+        return (lambda n: ld(f_t, n, h)), (lambda n: ld(mirrored, n, h))
+    if mu == 2:
+        edge = (row & 3) == 3
+        return (
+            lambda n: jnp.where(edge, ld(f_m, n, h), ld(early, 8 + n, h)),
+            lambda n: jnp.where(edge, ld(m_m, n, h), ld(mirror_early, 8 + n, h)),
+        )
+    edge = (row >> 2) + 2 * h == block
+    if h == 0:
+        here = lambda n: ld(early, n, h)
+    else:
+        here = lambda n: jnp.where(row >= 4, ld(f_x, n, h), ld(early, n, h))
+    return here, (lambda n: jnp.where(edge, ld(m_x, n, h), ld(mirror_early, n, h)))
+
+
+def updated_momenta(read, force, mirrored):
+    diag_force = [force(n) - mirrored(n) for n in range(2)]
     diag_force.append(-(diag_force[0] + diag_force[1]))
     diag = [read(n) + STEP * diag_force[n] for n in range(3)]
     upper = []
     for n in range(3):
-        re = ld(force, mu * 8 + 2 + 2 * n, h) - ld(mirrored, mu * 8 + 2 + 2 * n, h)
-        im = ld(force, mu * 8 + 3 + 2 * n, h) + ld(mirrored, mu * 8 + 3 + 2 * n, h)
+        re = force(2 + 2 * n) - mirrored(2 + 2 * n)
+        im = force(3 + 2 * n) + mirrored(3 + 2 * n)
         upper.append((read(3 + 2 * n) + STEP * re, read(4 + 2 * n) + STEP * im))
     return diag, upper
 
@@ -415,42 +473,84 @@
                 st(ref, mu * 18 + part * 9 + i * 3 + j, h, value[i][j][part])
 
 
-def update_kernel(table_i, partner, phi, u, p, force, mirrored, *rest):
-    new_u, new_p, o_t, o_x, o_m, q0, q2, q3 = rest
+def put_momenta(ref, base, h, diag, upper):
+    for n in range(3):
+        st(ref, base + n, h, diag[n])
+        st(ref, base + 3 + 2 * n, h, upper[n][0])
+        st(ref, base + 4 + 2 * n, h, upper[n][1])
+
+
+def put_full_momenta(new_p, old_p, mu, h, diag, upper):
+    for i in range(3):
+        st(new_p, mu * 18 + 4 * i, h, diag[i])
+        st(new_p, mu * 18 + 9 + 4 * i, h, ld(old_p, mu * 18 + 9 + 4 * i, h))
+    for (i, j), v in zip(OFF, upper):
+        st(new_p, mu * 18 + 3 * i + j, h, v[0])
+        st(new_p, mu * 18 + 3 * j + i, h, v[0])
+        st(new_p, mu * 18 + 9 + 3 * i + j, h, v[1])
+        st(new_p, mu * 18 + 9 + 3 * j + i, h, -v[1])
+
+
+def early_update_kernel(phi, u, p, early, mirror_early, new_u, new_p, q3):
+    for h in range(2):
+        force, mirrored = (lambda n: ld(early, 16 + n, h)), (lambda n: ld(mirror_early, 16 + n, h))
+        diag, upper = updated_momenta(input_momentum(p, 3, h), force, mirrored)
+        put_momenta(new_p, 0, h, diag, upper)
+        link = link_step(diag, upper, matrix(u, 3, h))
+        put_matrix(new_u, 0, h, link)
+        put_half(q3, h, mat_dag_half(link, project(spinor(phi, h), 3, -1)))
+
+
+def early_last_kernel(u, p, early, mirror_early, new_u, new_p):
+    for h in range(2):
+        force, mirrored = (lambda n: ld(early, 16 + n, h)), (lambda n: ld(mirror_early, 16 + n, h))
+        diag, upper = updated_momenta(lambda n: ld(p, 27 + n, h), force, mirrored)
+        put_momenta(new_p, 0, h, diag, upper)
+        put_matrix(new_u, 0, h, link_step(diag, upper, matrix(u, 3, h)))
+
+
+def update_kernel(table_i, partner, phi, u, p, u3, p3, *rest):
+    forces = rest[:6]
+    new_u, new_p, o_t, o_x, o_m, q0, q2, m_x, m_m = rest[6:]
     info = Info(table_i, partner)
+    block = place_faces(info, forces[5], m_x, m_m)
     for h in range(2):
         psi = spinor(phi, h)
-        for mu in range(4):
-            diag, upper = updated_momenta(input_momentum(p, mu, h), force, mirrored, mu, h)
-            for n in range(3):
-                st(new_p, mu * 9 + n, h, diag[n])
-                st(new_p, mu * 9 + 3 + 2 * n, h, upper[n][0])
-                st(new_p, mu * 9 + 4 + 2 * n, h, upper[n][1])
+        for mu in range(3):
+            diag, upper = updated_momenta(
+                input_momentum(p, mu, h), *both_forces(mu, h, block, *forces, m_x, m_m)
+            )
+            put_momenta(new_p, mu * 9, h, diag, upper)
             link = link_step(diag, upper, matrix(u, mu, h))
             put_matrix(new_u, mu, h, link)
             back = mat_dag_half(link, project(psi, mu, -1))
             if mu == 1:
                 put_half(o_t, h, map_half(lambda a: a * info.sign_behind, back))
             else:
-                put_half({0: q0, 2: q2, 3: q3}[mu], h, back)
+                put_half({0: q0, 2: q2}[mu], h, back)
+    new_u[54 * ROWS : 72 * ROWS, :] = u3[...]
+    new_p[27 * ROWS : 36 * ROWS, :] = p3[...]
     for k in range(12):
         o_x[k * 4 : k * 4 + 4, :] = q0[k * ROWS + 12 : k * ROWS + 16, :]
         send_rows(o_m, k, q2, k, info, 3)
 
 
-def last_kernel(u, p, old_p, force, mirrored, new_u, new_p):
-    for h in range(2):
-        for mu in range(4):
-            diag, upper = updated_momenta(lambda n: ld(p, mu * 9 + n, h), force, mirrored, mu, h)
-            for i in range(3):
-                st(new_p, mu * 18 + 4 * i, h, diag[i])
-                st(new_p, mu * 18 + 9 + 4 * i, h, ld(old_p, mu * 18 + 9 + 4 * i, h))
-            for (i, j), v in zip(OFF, upper):
-                st(new_p, mu * 18 + 3 * i + j, h, v[0])
-                st(new_p, mu * 18 + 3 * j + i, h, v[0])
-                st(new_p, mu * 18 + 9 + 3 * i + j, h, v[1])
-                st(new_p, mu * 18 + 9 + 3 * j + i, h, -v[1])
+def last_kernel(table_i, partner, u, p, old_p, u3, p3, *rest):
+    forces = rest[:6]
+    new_u, new_p, m_x, m_m = rest[6:]
+    info = Info(table_i, partner)
+    block = place_faces(info, forces[5], m_x, m_m)
+    for h in range(2):
+        for mu in range(3):
+            diag, upper = updated_momenta(
+                lambda n: ld(p, mu * 9 + n, h), *both_forces(mu, h, block, *forces, m_x, m_m)
+            )
+            put_full_momenta(new_p, old_p, mu, h, diag, upper)
             put_matrix(new_u, mu, h, link_step(diag, upper, matrix(u, mu, h)))
+        diag = [ld(p3, n, h) for n in range(3)]
+        upper = [(ld(p3, 3 + 2 * n, h), ld(p3, 4 + 2 * n, h)) for n in range(3)]
+        put_full_momenta(new_p, old_p, 3, h, diag, upper)
+    new_u[54 * ROWS : 72 * ROWS, :] = u3[...]
 
 
 VM = pl.BlockSpec(memory_space=pltpu.VMEM)
@@ -510,7 +610,7 @@
 
 
 SWAP_ORDER = ("far_t", "mirror", "far_x", "near_x", "near_t")
-BACK_ORDER = ("back_t", "mirror", "back_x")
+BACK_ORDER = ("back_t", "mirror", "back_x", "early")
 ON_ORDER = ("on_t", "mirror", "on_x")
 
 
@@ -523,9 +623,18 @@
     return [got[name] for name in ("near_t", "far_t", "near_x", "far_x", "mirror")]
 
 
-def back_exchange(t, x, m):
-    got = exchange(BACK_ORDER, back_t=t, back_x=x, mirror=m)
-    return [got[name] for name in ("back_t", "back_x", "mirror")]
+def all_forces(s, phi, u, y, w, o_t, o_x, o_m):
+    early, sent = call(early_force_kernel, 2, (*s, phi, u, y, w), [24 * ROWS, 24 * ROWS], [12 * HALO])
+    got = exchange(BACK_ORDER, back_t=o_t, back_x=o_x, mirror=o_m, early=sent)
+    f_t, f_x, f_m, sent = call(
+        late_force_kernel,
+        2,
+        (*s, phi, u, y, w, got["back_t"], got["back_x"], got["mirror"]),
+        [8 * ROWS, 8 * ROWS, 8 * ROWS, 12 * ROWS],
+        [],
+    )
+    late = exchange(("mirror",), mirror=sent)["mirror"]
+    return early, got["early"], f_t, f_x, f_m, late
 
 
 def on_exchange(t, x, m):
@@ -571,27 +680,25 @@
     y, w, o_t, o_x, o_m = call(
         response_kernel, 2, (*s, phi, u, *rest[5:], *arrived), [spin, 4 * FULL, FULL, FACE, FACE], halo + [FULL]
     )
-    force, sent = call(
-        force_kernel, 2, (*s, phi, u, y, w, *back_exchange(o_t, o_x, o_m)), [32 * ROWS, 32 * ROWS], [12 * HALO, FULL]
-    )
-    u, p1, o_t, o_x, o_m, *q = call(
+    forces = all_forces(s, phi, u, y, w, o_t, o_x, o_m)
+    u3, p3, q3 = call(early_update_kernel, 0, (phi, u, p, *forces[:2]), [18 * ROWS, 9 * ROWS, FULL], [])
+    u, p1, o_t, o_x, o_m, q0, q2 = call(
         update_kernel,
         2,
-        (*s, phi, u, p, force, mirror_swap(sent)),
-        [72 * ROWS, 36 * ROWS, FULL, FACE, FACE] + local,
-        [],
+        (*s, phi, u, p, u3, p3, *forces),
+        [72 * ROWS, 36 * ROWS, FULL, FACE, FACE, FULL, FULL],
+        [8 * ROWS, 8 * ROWS],
     )
     y, w, o_t, o_x, o_m = call(
         response2_kernel,
         2,
-        (*s, phi, u, *q, *arrived, *on_exchange(o_t, o_x, o_m)),
+        (*s, phi, u, q0, q2, q3, *arrived, *on_exchange(o_t, o_x, o_m)),
         [spin, 4 * FULL, FULL, FACE, FACE],
         halo + [FULL],
     )
-    force, sent = call(
-        force_kernel, 2, (*s, phi, u, y, w, *back_exchange(o_t, o_x, o_m)), [32 * ROWS, 32 * ROWS], [12 * HALO, FULL]
-    )
-    new_u, new_p = call(last_kernel, 0, (u, p1, p, force, mirror_swap(sent)), [72 * ROWS, 72 * ROWS], [])
+    forces = all_forces(s, phi, u, y, w, o_t, o_x, o_m)
+    u3, p3 = call(early_last_kernel, 0, (u, p1, *forces[:2]), [18 * ROWS, 9 * ROWS], [])
+    new_u, new_p = call(last_kernel, 2, (*s, u, p1, p, u3, p3, *forces), [72 * ROWS, 72 * ROWS], [8 * ROWS, 8 * ROWS])
     return new_u.reshape(gauge_links.shape), new_p.reshape(momenta.shape)
 
 

time: 84 us -> 83.8 us (level)
  waiting for transfers between devices: 38.9 us -> 27.1 us
  starting transfers between devices: 30.1 us -> 39.9 us
  Pallas kernels: 11.2 us -> 13.1 us
    ppermute x7 -> x9, starting transfers between devices: 5.57 us -> 17.4 us  [mirror_swap(): return lax.ppermute(value, 'xd', [(i, i ^ n // 2) for i in range(n)])]
    ppermute x7 -> x9, waiting for transfers between devices: 23.4 us -> 15 us  [mirror_swap(): return lax.ppermute(value, 'xd', [(i, i ^ n // 2) for i in range(n)])]
    ppermute x6, waiting for transfers between devices: 9.07 us -> 5.6 us  [shift(): return lax.ppermute(value, axis, [(i, (i + by) % n) for i in range(n)])]
    ppermute x6, starting transfers between devices: 10.7 us -> 8.67 us  [shift(): return lax.ppermute(value, axis, [(i, (i + by) % n) for i in range(n)])]
    pallas_call x8 -> x12, Pallas kernels: 11.2 us -> 13.1 us  [call(): pl.pallas_call(kernel, out_shape=[jax.ShapeDtypeStruct((rows, 128), F32)...]
  transfers between devices with their start and end apart: 21 -> 23, of which waited for: 11 -> 12; matrix products, arithmetic and copies ran while one was open for 0% -> 0% of each run, Pallas kernels for 0% -> 2%
where the time goes in v2:
time: 83.8 us; the launch traced here: 83.6 us
  starting transfers between devices  39.9 us (48%)
  waiting for transfers between devices  27.1 us (32%)
  Pallas kernels  13.1 us (16%)
  local copies, waits for them, and re-layouts  2.73 us (3%)
    ppermute x9, starting transfers between devices, mirror_swap(): return lax.ppermute(value, 'xd', [(i, i ^ n // 2) for i in range(n)])  17.4 us
    ppermute x9, waiting for transfers between devices, mirror_swap(): return lax.ppermute(value, 'xd', [(i, i ^ n // 2) for i in range(n)])  15 us
    ppermute x8, starting transfers between devices, swap(): return lax.ppermute(value, axis, pairs)  13.8 us
    pallas_call x12, Pallas kernels, call(): pl.pallas_call(kernel, out_shape=[jax.ShapeDtypeStruct((rows, 128), F32)...  13.1 us
    ppermute x6, starting transfers between devices, shift(): return lax.ppermute(value, axis, [(i, (i + by) % n) for i in range(n)])  8.67 us
    ppermute x8, waiting for transfers between devices, swap(): return lax.ppermute(value, axis, pairs)  6.51 us
    ppermute x6, waiting for transfers between devices, shift(): return lax.ppermute(value, axis, [(i, (i + by) % n) for i in range(n)])  5.6 us
    unnamed x10, local copies, waits for them, and re-layouts  2.73 us
  transfers between devices with their start and end apart: 23, of which 12 were waited for; matrix products, arithmetic and copies ran while one was open for 0% of the time, Pallas kernels for 2%

profile of v2, /device:TPU:0, one launch (start us, length us, event | category | flops | bytes accessed | tf_op | source)
XLA Modules:
  0.0 83.6 jit_solution(7015334439505633221)
XLA Ops:
  1.3 1.1 %copy-done = f32[4,2,3,3,4,1,4,128]{7,6,5,4,3,2,1,0:T(4,128)S(1)} copy-done((f32[4,2,3,3,4,1,4,128]{7,6,5,4,3,2,1,0:T(4,128)S(1)}, f32[4,2,3,3,4,1,4,128]{7,6,5,4,3,2,1,0:T(4,128)}, u32[]{:S(2)}) %copy-start) | copy-done | bytes 589848
  2.4 1.0 %copy-done.2 = f32[2,4,3,4096]{3,1,2,0:T(4,128)S(1)} copy-done((f32[2,4,3,4096]{3,1,2,0:T(4,128)S(1)}, f32[2,4,3,4096]{3,1,2,0:T(4,128)}, u32[]{:S(2)}) %copy-start.2) | copy-done | bytes 393240
  3.4 3.3 %shard_map.68 = (f32[384,128]{1,0:T(8,128)S(1)}, f32[192,128]{1,0:T(8,128)S(1)}, f32[192,128]{1,0:T(8,128)S(1)}, f32[48,128]{1,0:T(8,128)S(1)}, f32[48,128]{1,0:...) custom-call(s32[8]{0:T(128)S(1)} %compare_select_fusion.2.table_i, ...), custom_call_target="tpu_custom_call" | custom-call | tf_op jit(solution)/shard_map/pallas_call | solution.py:563
  6.8 5.6 %collective-permute-start.1 = (f32[192,128]{1,0:T(8,128)S(1)}, f32[192,128]{1,0:T(8,128)S(1)}, u32[]{:S(2)}, u32[]{:S(2)}) collective-permute-start(f32[192,128]{1,0:T(8,128)S(1)} %get-tuple-element.61), channel_id=1, source_target_pairs={{0,15},{1,2},{2,1},{3,4},{4,3},{5,6},{6,5},{7,8},{8,7},{9,10},{10,... | collective-permute-start | bytes 294920 | tf_op jit(solution)/shard_map/ppermute | solution.py:579
  12.5 3.9 %collective-permute-start.4 = (f32[96,128]{1,0:T(8,128)S(1)}, f32[96,128]{1,0:T(8,128)S(1)}, u32[]{:S(2)}, u32[]{:S(2)}) collective-permute-start(f32[96,128]{1,0:T(8,128)S(1)} %get-tuple-element.64), channel_id=1, source_target_pairs={{0,64},{16,80},{32,96},{48,112},{64,0},{80,16},{96,32},{112,48},{1... | collective-permute-start | bytes 147464 | tf_op jit(solution)/shard_map/ppermute | solution.py:589
  17.0 1.5 %collective-permute-start.3 = (f32[48,128]{1,0:T(8,128)S(1)}, f32[48,128]{1,0:T(8,128)S(1)}, u32[]{:S(2)}, u32[]{:S(2)}) collective-permute-start(f32[48,128]{1,0:T(8,128)S(1)} %get-tuple-element.63), channel_id=1, source_target_pairs={{0,112},{16,32},{32,16},{48,64},{64,48},{80,96},{96,80},{112,0},{1... | collective-permute-start | bytes 73736 | tf_op jit(solution)/shard_map/ppermute | solution.py:579
  18.5 1.7 %collective-permute-done.2.x_a = f32[48,128]{1,0:T(8,128)S(1)} collective-permute-done((f32[48,128]{1,0:T(8,128)S(1)}, f32[48,128]{1,0:T(8,128)S(1)}, u32[]{:S(2)}, u32[]{:S(2)}) %collective-permute-start.2) | collective-permute-done | bytes 24608 | tf_op jit(solution)/shard_map/ppermute | solution.py:579
  20.1 2.8 %collective-permute-done.3.x_b = f32[48,128]{1,0:T(8,128)S(1)} collective-permute-done((f32[48,128]{1,0:T(8,128)S(1)}, f32[48,128]{1,0:T(8,128)S(1)}, u32[]{:S(2)}, u32[]{:S(2)}) %collective-permute-start.3) | collective-permute-done | bytes 24608 | tf_op jit(solution)/shard_map/ppermute | solution.py:579
  22.9 1.1 %shard_map.69 = (f32[384,128]{1,0:T(8,128)S(1)}, f32[192,128]{1,0:T(8,128)S(1)}, f32[192,128]{1,0:T(8,128)S(1)}, f32[48,128]{1,0:T(8,128)S(1)}, f32[48,128]{1,0:...) custom-call(s32[8]{0:T(128)S(1)} %compare_select_fusion.2.table_i, ...), custom_call_target="tpu_custom_call" | custom-call | tf_op jit(solution)/shard_map/pallas_call | solution.py:563
  24.2 1.9 %collective-permute-start.6 = (f32[192,128]{1,0:T(8,128)S(1)}, f32[192,128]{1,0:T(8,128)S(1)}, u32[]{:S(2)}, u32[]{:S(2)}) collective-permute-start(f32[192,128]{1,0:T(8,128)S(1)} %get-tuple-element.70), channel_id=1, source_target_pairs={{0,15},{1,2},{2,1},{3,4},{4,3},{5,6},{6,5},{7,8},{8,7},{9,10},{10,... | collective-permute-start | bytes 294920 | tf_op jit(solution)/shard_map/ppermute | solution.py:579
  26.1 3.9 %collective-permute-start.8 = (f32[48,128]{1,0:T(8,128)S(1)}, f32[48,128]{1,0:T(8,128)S(1)}, u32[]{:S(2)}, u32[]{:S(2)}) collective-permute-start(f32[48,128]{1,0:T(8,128)S(1)} %get-tuple-element.72), channel_id=1, source_target_pairs={{0,112},{16,32},{32,16},{48,64},{64,48},{80,96},{96,80},{112,0},{1... | collective-permute-start | bytes 73736 | tf_op jit(solution)/shard_map/ppermute | solution.py:579
  30.1 2.1 %collective-permute-done.8.x_b = f32[48,128]{1,0:T(8,128)S(1)} collective-permute-done((f32[48,128]{1,0:T(8,128)S(1)}, f32[48,128]{1,0:T(8,128)S(1)}, u32[]{:S(2)}, u32[]{:S(2)}) %collective-permute-start.8) | collective-permute-done | bytes 24608 | tf_op jit(solution)/shard_map/ppermute | solution.py:579
  34.0 2.3 %collective-permute-start.10 = (f32[384,128]{1,0:T(8,128)S(1)}, f32[384,128]{1,0:T(8,128)S(1)}, u32[]{:S(2)}, u32[]{:S(2)}) collective-permute-start(f32[384,128]{1,0:T(8,128)S(1)} %get-tuple-element.77), channel_id=1, source_target_pairs={{0,64},{16,80},{32,96},{48,112},{64,0},{80,16},{96,32},{112,48},{1... | collective-permute-start | bytes 589832 | tf_op jit(solution)/shard_map/ppermute | solution.py:589
  36.3 2.2 %collective-permute-start.11 = (f32[192,128]{1,0:T(8,128)S(1)}, f32[192,128]{1,0:T(8,128)S(1)}, u32[]{:S(2)}, u32[]{:S(2)}) collective-permute-start(f32[192,128]{1,0:T(8,128)S(1)} %get-tuple-element.80), channel_id=1, source_target_pairs={{0,15},{1,0},{2,1},{3,2},{4,3},{5,4},{6,5},{7,6},{8,7},{9,8},{10,9... | collective-permute-start | bytes 294920 | tf_op jit(solution)/shard_map/ppermute | solution.py:584
  38.5 1.0 %collective-permute-start.12 = (f32[48,128]{1,0:T(8,128)S(1)}, f32[48,128]{1,0:T(8,128)S(1)}, u32[]{:S(2)}, u32[]{:S(2)}) collective-permute-start(f32[48,128]{1,0:T(8,128)S(1)} %get-tuple-element.81), channel_id=1, source_target_pairs={{0,112},{16,0},{32,16},{48,32},{64,48},{80,64},{96,80},{112,96},{1... | collective-permute-start | bytes 73736 | tf_op jit(solution)/shard_map/ppermute | solution.py:584
  39.6 2.4 %collective-permute-start.13 = (f32[48,128]{1,0:T(8,128)S(1)}, f32[48,128]{1,0:T(8,128)S(1)}, u32[]{:S(2)}, u32[]{:S(2)}) collective-permute-start(f32[48,128]{1,0:T(8,128)S(1)} %get-tuple-element.82), channel_id=1, source_target_pairs={{0,64},{16,80},{32,96},{48,112},{64,0},{80,16},{96,32},{112,48},{1... | collective-permute-start | bytes 73736 | tf_op jit(solution)/shard_map/ppermute | solution.py:589
  42.4 2.5 %collective-permute-done.13.r_m = f32[48,128]{1,0:T(8,128)S(1)} collective-permute-done((f32[48,128]{1,0:T(8,128)S(1)}, f32[48,128]{1,0:T(8,128)S(1)}, u32[]{:S(2)}, u32[]{:S(2)}) %collective-permute-start.13) | collective-permute-done | bytes 24608 | tf_op jit(solution)/shard_map/ppermute | solution.py:589
  45.7 2.5 %collective-permute-start.14 = (f32[192,128]{1,0:T(8,128)S(1)}, f32[192,128]{1,0:T(8,128)S(1)}, u32[]{:S(2)}, u32[]{:S(2)}) collective-permute-start(f32[192,128]{1,0:T(8,128)S(1)} %get-tuple-element.86), channel_id=1, source_target_pairs={{0,64},{16,80},{32,96},{48,112},{64,0},{80,16},{96,32},{112,48},{1... | collective-permute-start | bytes 294920 | tf_op jit(solution)/shard_map/ppermute | solution.py:589
  48.4 3.6 %collective-permute-done.14.rest_5_ = f32[192,128]{1,0:T(8,128)S(1)} collective-permute-done((f32[192,128]{1,0:T(8,128)S(1)}, f32[192,128]{1,0:T(8,128)S(1)}, u32[]{:S(2)}, u32[]{:S(2)}) %collective-permute-start.14) | collective-permute-done | bytes 98336 | tf_op jit(solution)/shard_map/ppermute | solution.py:589
  51.9 1.1 %shard_map.74 = (f32[1152,128]{1,0:T(8,128)S(1)}, f32[576,128]{1,0:T(8,128)S(1)}, f32[192,128]{1,0:T(8,128)S(1)}, f32[48,128]{1,0:T(8,128)S(1)}, f32[48,128]{1,0...) custom-call(s32[8]{0:T(128)S(1)} %compare_select_fusion.2.table_i, s32[4]{0:T(128)S(1)} %copy-done.3, ...), custom_call_target="tpu_custom_call" | custom-call | tf_op jit(solution)/shard_map/pallas_call | solution.py:563
  53.1 1.1 %collective-permute-start.16 = (f32[48,128]{1,0:T(8,128)S(1)}, f32[48,128]{1,0:T(8,128)S(1)}, u32[]{:S(2)}, u32[]{:S(2)}) collective-permute-start(f32[48,128]{1,0:T(8,128)S(1)} %get-tuple-element.93), channel_id=1, source_target_pairs={{0,16},{16,32},{32,48},{48,64},{64,80},{80,96},{96,112},{112,0},{1... | collective-permute-start | bytes 73736 | tf_op jit(solution)/shard_map/ppermute | solution.py:584
  54.2 1.5 %collective-permute-start.17 = (f32[48,128]{1,0:T(8,128)S(1)}, f32[48,128]{1,0:T(8,128)S(1)}, u32[]{:S(2)}, u32[]{:S(2)}) collective-permute-start(f32[48,128]{1,0:T(8,128)S(1)} %get-tuple-element.94), channel_id=1, source_target_pairs={{0,64},{16,80},{32,96},{48,112},{64,0},{80,16},{96,32},{112,48},{1... | collective-permute-start | bytes 73736 | tf_op jit(solution)/shard_map/ppermute | solution.py:589
  55.7 3.5 %collective-permute-done.16.b_x = f32[48,128]{1,0:T(8,128)S(1)} collective-permute-done((f32[48,128]{1,0:T(8,128)S(1)}, f32[48,128]{1,0:T(8,128)S(1)}, u32[]{:S(2)}, u32[]{:S(2)}) %collective-permute-start.16) | collective-permute-done | bytes 24608 | tf_op jit(solution)/shard_map/ppermute | solution.py:584
  59.5 1.3 %collective-permute-done.15.b_t = f32[192,128]{1,0:T(8,128)S(1)} collective-permute-done((f32[192,128]{1,0:T(8,128)S(1)}, f32[192,128]{1,0:T(8,128)S(1)}, u32[]{:S(2)}, u32[]{:S(2)}) %collective-permute-start.15) | collective-permute-done | bytes 98336 | tf_op jit(solution)/shard_map/ppermute | solution.py:584
  62.6 2.4 %collective-permute-start.18 = (f32[384,128]{1,0:T(8,128)S(1)}, f32[384,128]{1,0:T(8,128)S(1)}, u32[]{:S(2)}, u32[]{:S(2)}) collective-permute-start(f32[384,128]{1,0:T(8,128)S(1)} %get-tuple-element.98), channel_id=1, source_target_pairs={{0,64},{16,80},{32,96},{48,112},{64,0},{80,16},{96,32},{112,48},{1... | collective-permute-start | bytes 589832 | tf_op jit(solution)/shard_map/ppermute | solution.py:589
  65.0 2.0 %collective-permute-start.19 = (f32[192,128]{1,0:T(8,128)S(1)}, f32[192,128]{1,0:T(8,128)S(1)}, u32[]{:S(2)}, u32[]{:S(2)}) collective-permute-start(f32[192,128]{1,0:T(8,128)S(1)} %get-tuple-element.101), channel_id=1, source_target_pairs={{0,15},{1,0},{2,1},{3,2},{4,3},{5,4},{6,5},{7,6},{8,7},{9,8},{10,9... | collective-permute-start | bytes 294920 | tf_op jit(solution)/shard_map/ppermute | solution.py:584
  67.1 2.2 %collective-permute-start.20 = (f32[48,128]{1,0:T(8,128)S(1)}, f32[48,128]{1,0:T(8,128)S(1)}, u32[]{:S(2)}, u32[]{:S(2)}) collective-permute-start(f32[48,128]{1,0:T(8,128)S(1)} %get-tuple-element.102), channel_id=1, source_target_pairs={{0,112},{16,0},{32,16},{48,32},{64,48},{80,64},{96,80},{112,96},{1... | collective-permute-start | bytes 73736 | tf_op jit(solution)/shard_map/ppermute | solution.py:584
  69.3 1.2 %collective-permute-start.21 = (f32[48,128]{1,0:T(8,128)S(1)}, f32[48,128]{1,0:T(8,128)S(1)}, u32[]{:S(2)}, u32[]{:S(2)}) collective-permute-start(f32[48,128]{1,0:T(8,128)S(1)} %get-tuple-element.103), channel_id=1, source_target_pairs={{0,64},{16,80},{32,96},{48,112},{64,0},{80,16},{96,32},{112,48},{1... | collective-permute-start | bytes 73736 | tf_op jit(solution)/shard_map/ppermute | solution.py:589
  70.9 3.7 %collective-permute-done.21.r_m = f32[48,128]{1,0:T(8,128)S(1)} collective-permute-done((f32[48,128]{1,0:T(8,128)S(1)}, f32[48,128]{1,0:T(8,128)S(1)}, u32[]{:S(2)}, u32[]{:S(2)}) %collective-permute-start.21) | collective-permute-done | bytes 24608 | tf_op jit(solution)/shard_map/ppermute | solution.py:589
  75.5 1.2 %collective-permute-start.22 = (f32[192,128]{1,0:T(8,128)S(1)}, f32[192,128]{1,0:T(8,128)S(1)}, u32[]{:S(2)}, u32[]{:S(2)}) collective-permute-start(f32[192,128]{1,0:T(8,128)S(1)} %get-tuple-element.107), channel_id=1, source_target_pairs={{0,64},{16,80},{32,96},{48,112},{64,0},{80,16},{96,32},{112,48},{1... | collective-permute-start | bytes 294920 | tf_op jit(solution)/shard_map/ppermute | solution.py:589
  76.9 4.8 %collective-permute-done.22.rest_5_ = f32[192,128]{1,0:T(8,128)S(1)} collective-permute-done((f32[192,128]{1,0:T(8,128)S(1)}, f32[192,128]{1,0:T(8,128)S(1)}, u32[]{:S(2)}, u32[]{:S(2)}) %collective-permute-start.22) | collective-permute-done | bytes 98336 | tf_op jit(solution)/shard_map/ppermute | solution.py:589
  81.7 1.9 %shard_map.79 = (f32[1152,128]{1,0:T(8,128)}, f32[1152,128]{1,0:T(8,128)}) custom-call(s32[8]{0:T(128)S(1)} %compare_select_fusion.2.table_i, s32[4]{0:T(128)S(1)} %copy-done.3, f32[1152,128]{1,0:T(8,128)S(1)} %get-tuple-element.87.u, f32[576,128]{1,0:T(8,128)S(1)} %get-tuple-element.88.p, f32[1152,128]{1,0:T(8,128)S(1)} %bitcast.19, ...), custom_call_target="tpu_custom_call" | custom-call | tf_op jit(solution)/shard_map/pallas_call | solution.py:563
  (37 shorter events, 8.5 us)
Async XLA Ops:
  0.6 0.7 copy-start.4
  0.7 0.7 copy-start.3
  1.3 1.1 %copy-start = (f32[4,2,3,3,4,1,4,128]{7,6,5,4,3,2,1,0:T(4,128)S(1)}, f32[4,2,3,3,4,1,4,128]{7,6,5,4,3,2,1,0:T(4,128)}, u32[]{:S(2)}) copy-start(f32[4,2,3,3,4,1,4,128]{7,6,5,4,3,2,1,0:T(4,128)} %param.5) | copy-start | bytes 1769476
  2.4 1.0 %copy-start.2 = (f32[2,4,3,4096]{3,1,2,0:T(4,128)S(1)}, f32[2,4,3,4096]{3,1,2,0:T(4,128)}, u32[]{:S(2)}) copy-start(f32[2,4,3,4096]{3,1,2,0:T(4,128)} %param.7) | copy-start | bytes 1179652
  6.8 16.2 %collective-permute-start = (f32[192,128]{1,0:T(8,128)S(1)}, f32[192,128]{1,0:T(8,128)S(1)}, u32[]{:S(2)}, u32[]{:S(2)}) collective-permute-start(f32[192,128]{1,0:T(8,128)S(1)} %get-tuple-element.60), channel_id=1, source_target_pairs={{0,1},{1,0},{2,3},{3,2},{4,5},{5,4},{6,7},{7,6},{8,9},{9,8},{10,11... | collective-permute-start | bytes 294920 | tf_op jit(solution)/shard_map/ppermute | solution.py:579
  6.8 16.1 %collective-permute-start.1 = (f32[192,128]{1,0:T(8,128)S(1)}, f32[192,128]{1,0:T(8,128)S(1)}, u32[]{:S(2)}, u32[]{:S(2)}) collective-permute-start(f32[192,128]{1,0:T(8,128)S(1)} %get-tuple-element.61), channel_id=1, source_target_pairs={{0,15},{1,2},{2,1},{3,4},{4,3},{5,6},{6,5},{7,8},{8,7},{9,10},{10,... | collective-permute-start | bytes 294920 | tf_op jit(solution)/shard_map/ppermute | solution.py:579
  12.5 10.5 %collective-permute-start.4 = (f32[96,128]{1,0:T(8,128)S(1)}, f32[96,128]{1,0:T(8,128)S(1)}, u32[]{:S(2)}, u32[]{:S(2)}) collective-permute-start(f32[96,128]{1,0:T(8,128)S(1)} %get-tuple-element.64), channel_id=1, source_target_pairs={{0,64},{16,80},{32,96},{48,112},{64,0},{80,16},{96,32},{112,48},{1... | collective-permute-start | bytes 147464 | tf_op jit(solution)/shard_map/ppermute | solution.py:589
  16.3 3.8 %collective-permute-start.2 = (f32[48,128]{1,0:T(8,128)S(1)}, f32[48,128]{1,0:T(8,128)S(1)}, u32[]{:S(2)}, u32[]{:S(2)}) collective-permute-start(f32[48,128]{1,0:T(8,128)S(1)} %get-tuple-element.62), channel_id=1, source_target_pairs={{0,16},{16,0},{32,48},{48,32},{64,80},{80,64},{96,112},{112,96},{1... | collective-permute-start | bytes 73736 | tf_op jit(solution)/shard_map/ppermute | solution.py:579
  17.0 5.9 %collective-permute-start.3 = (f32[48,128]{1,0:T(8,128)S(1)}, f32[48,128]{1,0:T(8,128)S(1)}, u32[]{:S(2)}, u32[]{:S(2)}) collective-permute-start(f32[48,128]{1,0:T(8,128)S(1)} %get-tuple-element.63), channel_id=1, source_target_pairs={{0,112},{16,32},{32,16},{48,64},{64,48},{80,96},{96,80},{112,0},{1... | collective-permute-start | bytes 73736 | tf_op jit(solution)/shard_map/ppermute | solution.py:579
  24.1 8.0 %collective-permute-start.5 = (f32[192,128]{1,0:T(8,128)S(1)}, f32[192,128]{1,0:T(8,128)S(1)}, u32[]{:S(2)}, u32[]{:S(2)}) collective-permute-start(f32[192,128]{1,0:T(8,128)S(1)} %get-tuple-element.69), channel_id=1, source_target_pairs={{0,1},{1,0},{2,3},{3,2},{4,5},{5,4},{6,7},{7,6},{8,9},{9,8},{10,11... | collective-permute-start | bytes 294920 | tf_op jit(solution)/shard_map/ppermute | solution.py:579
  24.2 8.0 %collective-permute-start.6 = (f32[192,128]{1,0:T(8,128)S(1)}, f32[192,128]{1,0:T(8,128)S(1)}, u32[]{:S(2)}, u32[]{:S(2)}) collective-permute-start(f32[192,128]{1,0:T(8,128)S(1)} %get-tuple-element.70), channel_id=1, source_target_pairs={{0,15},{1,2},{2,1},{3,4},{4,3},{5,6},{6,5},{7,8},{8,7},{9,10},{10,... | collective-permute-start | bytes 294920 | tf_op jit(solution)/shard_map/ppermute | solution.py:579
  26.1 6.0 %collective-permute-start.9 = (f32[96,128]{1,0:T(8,128)S(1)}, f32[96,128]{1,0:T(8,128)S(1)}, u32[]{:S(2)}, u32[]{:S(2)}) collective-permute-start(f32[96,128]{1,0:T(8,128)S(1)} %get-tuple-element.73), channel_id=1, source_target_pairs={{0,64},{16,80},{32,96},{48,112},{64,0},{80,16},{96,32},{112,48},{1... | collective-permute-start | bytes 147464 | tf_op jit(solution)/shard_map/ppermute | solution.py:589
  26.1 3.9 %collective-permute-start.7 = (f32[48,128]{1,0:T(8,128)S(1)}, f32[48,128]{1,0:T(8,128)S(1)}, u32[]{:S(2)}, u32[]{:S(2)}) collective-permute-start(f32[48,128]{1,0:T(8,128)S(1)} %get-tuple-element.71), channel_id=1, source_target_pairs={{0,16},{16,0},{32,48},{48,32},{64,80},{80,64},{96,112},{112,96},{1... | collective-permute-start | bytes 73736 | tf_op jit(solution)/shard_map/ppermute | solution.py:579
  26.1 6.0 %collective-permute-start.8 = (f32[48,128]{1,0:T(8,128)S(1)}, f32[48,128]{1,0:T(8,128)S(1)}, u32[]{:S(2)}, u32[]{:S(2)}) collective-permute-start(f32[48,128]{1,0:T(8,128)S(1)} %get-tuple-element.72), channel_id=1, source_target_pairs={{0,112},{16,32},{32,16},{48,64},{64,48},{80,96},{96,80},{112,0},{1... | collective-permute-start | bytes 73736 | tf_op jit(solution)/shard_map/ppermute | solution.py:579
  34.0 14.2 %collective-permute-start.10 = (f32[384,128]{1,0:T(8,128)S(1)}, f32[384,128]{1,0:T(8,128)S(1)}, u32[]{:S(2)}, u32[]{:S(2)}) collective-permute-start(f32[384,128]{1,0:T(8,128)S(1)} %get-tuple-element.77), channel_id=1, source_target_pairs={{0,64},{16,80},{32,96},{48,112},{64,0},{80,16},{96,32},{112,48},{1... | collective-permute-start | bytes 589832 | tf_op jit(solution)/shard_map/ppermute | solution.py:589
  36.3 8.6 %collective-permute-start.11 = (f32[192,128]{1,0:T(8,128)S(1)}, f32[192,128]{1,0:T(8,128)S(1)}, u32[]{:S(2)}, u32[]{:S(2)}) collective-permute-start(f32[192,128]{1,0:T(8,128)S(1)} %get-tuple-element.80), channel_id=1, source_target_pairs={{0,15},{1,0},{2,1},{3,2},{4,3},{5,4},{6,5},{7,6},{8,7},{9,8},{10,9... | collective-permute-start | bytes 294920 | tf_op jit(solution)/shard_map/ppermute | solution.py:584
  38.5 3.8 %collective-permute-start.12 = (f32[48,128]{1,0:T(8,128)S(1)}, f32[48,128]{1,0:T(8,128)S(1)}, u32[]{:S(2)}, u32[]{:S(2)}) collective-permute-start(f32[48,128]{1,0:T(8,128)S(1)} %get-tuple-element.81), channel_id=1, source_target_pairs={{0,112},{16,0},{32,16},{48,32},{64,48},{80,64},{96,80},{112,96},{1... | collective-permute-start | bytes 73736 | tf_op jit(solution)/shard_map/ppermute | solution.py:584
  39.6 8.6 %copy-start.1 = (f32[4,2,3,3,4,1,4,128]{7,6,5,4,3,2,1,0:T(4,128)S(1)}, f32[4,2,3,3,4,1,4,128]{7,6,5,4,3,2,1,0:T(4,128)}, u32[]{:S(2)}) copy-start(f32[4,2,3,3,4,1,4,128]{7,6,5,4,3,2,1,0:T(4,128)} %param.6) | copy-start | bytes 1769476
  39.6 5.3 %collective-permute-start.13 = (f32[48,128]{1,0:T(8,128)S(1)}, f32[48,128]{1,0:T(8,128)S(1)}, u32[]{:S(2)}, u32[]{:S(2)}) collective-permute-start(f32[48,128]{1,0:T(8,128)S(1)} %get-tuple-element.82), channel_id=1, source_target_pairs={{0,64},{16,80},{32,96},{48,112},{64,0},{80,16},{96,32},{112,48},{1... | collective-permute-start | bytes 73736 | tf_op jit(solution)/shard_map/ppermute | solution.py:589
  45.7 6.2 %collective-permute-start.14 = (f32[192,128]{1,0:T(8,128)S(1)}, f32[192,128]{1,0:T(8,128)S(1)}, u32[]{:S(2)}, u32[]{:S(2)}) collective-permute-start(f32[192,128]{1,0:T(8,128)S(1)} %get-tuple-element.86), channel_id=1, source_target_pairs={{0,64},{16,80},{32,96},{48,112},{64,0},{80,16},{96,32},{112,48},{1... | collective-permute-start | bytes 294920 | tf_op jit(solution)/shard_map/ppermute | solution.py:589
  53.1 7.7 %collective-permute-start.15 = (f32[192,128]{1,0:T(8,128)S(1)}, f32[192,128]{1,0:T(8,128)S(1)}, u32[]{:S(2)}, u32[]{:S(2)}) collective-permute-start(f32[192,128]{1,0:T(8,128)S(1)} %get-tuple-element.92), channel_id=1, source_target_pairs={{0,1},{1,2},{2,3},{3,4},{4,5},{5,6},{6,7},{7,8},{8,9},{9,10},{10,1... | collective-permute-start | bytes 294920 | tf_op jit(solution)/shard_map/ppermute | solution.py:584
  53.1 6.0 %collective-permute-start.16 = (f32[48,128]{1,0:T(8,128)S(1)}, f32[48,128]{1,0:T(8,128)S(1)}, u32[]{:S(2)}, u32[]{:S(2)}) collective-permute-start(f32[48,128]{1,0:T(8,128)S(1)} %get-tuple-element.93), channel_id=1, source_target_pairs={{0,16},{16,32},{32,48},{48,64},{64,80},{80,96},{96,112},{112,0},{1... | collective-permute-start | bytes 73736 | tf_op jit(solution)/shard_map/ppermute | solution.py:584
  54.2 5.3 %collective-permute-start.17 = (f32[48,128]{1,0:T(8,128)S(1)}, f32[48,128]{1,0:T(8,128)S(1)}, u32[]{:S(2)}, u32[]{:S(2)}) collective-permute-start(f32[48,128]{1,0:T(8,128)S(1)} %get-tuple-element.94), channel_id=1, source_target_pairs={{0,64},{16,80},{32,96},{48,112},{64,0},{80,16},{96,32},{112,48},{1... | collective-permute-start | bytes 73736 | tf_op jit(solution)/shard_map/ppermute | solution.py:589
  62.6 14.1 %collective-permute-start.18 = (f32[384,128]{1,0:T(8,128)S(1)}, f32[384,128]{1,0:T(8,128)S(1)}, u32[]{:S(2)}, u32[]{:S(2)}) collective-permute-start(f32[384,128]{1,0:T(8,128)S(1)} %get-tuple-element.98), channel_id=1, source_target_pairs={{0,64},{16,80},{32,96},{48,112},{64,0},{80,16},{96,32},{112,48},{1... | collective-permute-start | bytes 589832 | tf_op jit(solution)/shard_map/ppermute | solution.py:589
  65.0 9.6 %collective-permute-start.19 = (f32[192,128]{1,0:T(8,128)S(1)}, f32[192,128]{1,0:T(8,128)S(1)}, u32[]{:S(2)}, u32[]{:S(2)}) collective-permute-start(f32[192,128]{1,0:T(8,128)S(1)} %get-tuple-element.101), channel_id=1, source_target_pairs={{0,15},{1,0},{2,1},{3,2},{4,3},{5,4},{6,5},{7,6},{8,7},{9,8},{10,9... | collective-permute-start | bytes 294920 | tf_op jit(solution)/shard_map/ppermute | solution.py:584
  67.1 3.8 %collective-permute-start.20 = (f32[48,128]{1,0:T(8,128)S(1)}, f32[48,128]{1,0:T(8,128)S(1)}, u32[]{:S(2)}, u32[]{:S(2)}) collective-permute-start(f32[48,128]{1,0:T(8,128)S(1)} %get-tuple-element.102), channel_id=1, source_target_pairs={{0,112},{16,0},{32,16},{48,32},{64,48},{80,64},{96,80},{112,96},{1... | collective-permute-start | bytes 73736 | tf_op jit(solution)/shard_map/ppermute | solution.py:584
  69.3 5.3 %collective-permute-start.21 = (f32[48,128]{1,0:T(8,128)S(1)}, f32[48,128]{1,0:T(8,128)S(1)}, u32[]{:S(2)}, u32[]{:S(2)}) collective-permute-start(f32[48,128]{1,0:T(8,128)S(1)} %get-tuple-element.103), channel_id=1, source_target_pairs={{0,64},{16,80},{32,96},{48,112},{64,0},{80,16},{96,32},{112,48},{1... | collective-permute-start | bytes 73736 | tf_op jit(solution)/shard_map/ppermute | solution.py:589
  75.5 6.2 %collective-permute-start.22 = (f32[192,128]{1,0:T(8,128)S(1)}, f32[192,128]{1,0:T(8,128)S(1)}, u32[]{:S(2)}, u32[]{:S(2)}) collective-permute-start(f32[192,128]{1,0:T(8,128)S(1)} %get-tuple-element.107), channel_id=1, source_target_pairs={{0,64},{16,80},{32,96},{48,112},{64,0},{80,16},{96,32},{112,48},{1... | collective-permute-start | bytes 294920 | tf_op jit(solution)/shard_map/ppermute | solution.py:589

commit v3 on v2

--- a/solution.py
+++ b/solution.py
@@ -113,13 +113,45 @@
     return [[tuple(fn(*(v[t][c][part] for v in vs)) for part in range(2)) for c in range(3)] for t in range(2)]
 
 
+INFO_ROWS = 64
+
+
 class Info:
-    def __init__(self, table, partner):
-        self.even_t = table[0] == 0
-        self.even_x = table[1] == 0
-        self.sign_ahead = table[2].astype(F32)
-        self.sign_behind = table[3].astype(F32)
-        self.partner = [partner[j] & 3 for j in range(4)]
+    def __init__(self, info):
+        self.even_t = info[24:32, :] == 0
+        self.even_x = info[32:36, :] == 0
+        self.sign_ahead = info[40:48, :].astype(F32)
+        self.sign_behind = info[48:56, :].astype(F32)
+        self.face_source = [info[16:20, :] == j for j in range(4)]
+        self.edge_block = info[56:64, :]
+        half = row_block()
+        self.block_source = []
+        for h in range(2):
+            source = info[8 * h : 8 * h + 8, :]
+            self.block_source.append((source == half, source == 1 - half, source == 2 + half))
+
+
+def row_block():
+    return lax.broadcasted_iota(jnp.int32, (8, 128), 0) >> 2
+
+
+def write_info(info, odd_t, odd_x, sign_ahead, sign_behind, partner):
+    row = lax.broadcasted_iota(jnp.int32, (8, 128), 0)
+
+    def source_of(target):
+        value = jnp.zeros((8, 128), jnp.int32)
+        for j in range(4):
+            value = jnp.where(target == partner[j], j, value)
+        return value
+
+    info[0:8, :] = source_of(row >> 2)
+    info[8:16, :] = source_of(2 + (row >> 2))
+    info[16:24, :] = source_of(row & 3)
+    edge = jnp.int32(0)
+    for j in range(4):
+        edge = edge + jnp.where(partner[j] == 3, j, 0)
+    for n, value in enumerate((odd_t, odd_x, sign_ahead, sign_behind, edge)):
+        info[24 + 8 * n : 32 + 8 * n, :] = jnp.full((8, 128), value, jnp.int32)
 
 
 def row_in_pair():
@@ -127,8 +159,14 @@
 
 
 def send_rows(dst, base, src, k, info, row):
-    for j in range(4):
-        dst[pl.ds(base * 4 + info.partner[j], 1), :] = src[k * ROWS + 4 * j + row : k * ROWS + 4 * j + row + 1, :]
+    def spread(j):
+        at = k * ROWS + 4 * j + row
+        return jnp.broadcast_to(src[at : at + 1, :], (4, 128))
+
+    value = spread(0)
+    for j in range(1, 4):
+        value = jnp.where(info.face_source[j], spread(j), value)
+    dst[base * 4 : base * 4 + 4, :] = value
 
 
 def send_both(psi_ref, u_ref, info, t_a, t_b, x_a, x_b, mirror, q0, q2, q3, h0, h2):
@@ -224,9 +262,24 @@
     )
 
 
-def noise_kernel(table_i, partner, index, table, u, *rest):
-    psi, t_a, t_b, x_a, x_b, mirror, q0, q2, q3, flat, parts, h0, h2 = rest
-    info = Info(table_i, partner)
+def noise_kernel(table_i_hbm, partner_hbm, index_hbm, table_hbm, u_hbm, *rest):
+    psi, t_a, t_b, x_a, x_b, mirror, q0, q2, q3, info_ref = rest[:10]
+    flat, parts, h0, h2, table, u, index, table_i, partner, sems = rest[10:]
+    copies = [
+        pltpu.make_async_copy(src, dst, sems.at[n])
+        for n, (src, dst) in enumerate(
+            (
+                (index_hbm, index),
+                (table_hbm, table),
+                (table_i_hbm, table_i),
+                (partner_hbm, partner),
+                (u_hbm, u),
+            )
+        )
+    ]
+    for copy in copies:
+        copy.start()
+    copies[1].wait()
     for part in range(2):
         for c in range(3):
             flat[(part * 3 + c) * 4 : (part * 3 + c) * 4 + 4, :] = table[part, c]
@@ -238,23 +291,32 @@
         third = (left - second.astype(F32)).astype(jnp.bfloat16)
         for n, value in enumerate((first, second, third)):
             parts[hi * 24 : hi * 24 + 24, n * 256 : n * 256 + 256] = value
+    copies[0].wait()
     low_iota = lax.broadcasted_iota(jnp.int32, (256, 128), 0)
     table_parts = parts[...]
-    for r in range(16):
-        wanted = index[r : r + 1, :]
-        hot = jnp.where(low_iota == (wanted & 255), 1.0, 0.0).astype(jnp.bfloat16)
+    for r in range(0, 16, 2):
+        wanted = [index[r + n : r + n + 1, :] for n in range(2)]
+        hot = jnp.concatenate(
+            [jnp.where(low_iota == (w & 255), 1.0, 0.0).astype(jnp.bfloat16) for w in wanted], axis=1
+        )
         found = jnp.dot(table_parts, jnp.concatenate([hot, hot, hot], axis=0), preferred_element_type=F32)
-        high = jnp.broadcast_to(wanted >> 8, (24, 128))
-        value = found[0:24]
-        for hi in range(1, 16):
-            value = jnp.where(high == hi, found[hi * 24 : hi * 24 + 24], value)
-        psi[pl.ds(r, 24, stride=16), :] = value
+        for n in range(2):
+            high = jnp.broadcast_to(wanted[n] >> 8, (24, 128))
+            value = found[0:24, 128 * n : 128 * n + 128]
+            for hi in range(1, 16):
+                value = jnp.where(high == hi, found[hi * 24 : hi * 24 + 24, 128 * n : 128 * n + 128], value)
+            psi[pl.ds(r + n, 24, stride=16), :] = value
+    copies[2].wait()
+    copies[3].wait()
+    write_info(info_ref, *(table_i[n] for n in range(4)), [partner[j] & 3 for j in range(4)])
+    info = Info(info_ref)
+    copies[4].wait()
     send_both(psi, u, info, t_a, t_b, x_a, x_b, mirror, q0, q2, q3, h0, h2)
 
 
-def phi_kernel(table_i, partner, psi, u, q0, q2, q3, t_a, t_b, x_a, x_b, mirror, *rest):
+def phi_kernel(info_ref, psi, u, q0, q2, q3, t_a, t_b, x_a, x_b, mirror, *rest):
     phi, o_ta, o_tb, o_xa, o_xb, o_m, o_q0, o_q2, o_q3, a0, b0, fa, fb, h0, h2 = rest
-    info = Info(table_i, partner)
+    info = Info(info_ref)
     arrived = arrived_swap(info, t_a, t_b, x_a, x_b, mirror)
     dirac(psi, u, arrived, q0, q2, q3, (a0, b0, fa, fb), phi, None)
     send_both(phi, u, info, o_ta, o_tb, o_xa, o_xb, o_m, o_q0, o_q2, o_q3, h0, h2)
@@ -276,17 +338,17 @@
         send_rows(o_m, k, h2, k, info, 0)
 
 
-def response_kernel(table_i, partner, phi, u, q0, q2, q3, t_a, t_b, x_a, x_b, mirror, *rest):
+def response_kernel(info_ref, phi, u, q0, q2, q3, t_a, t_b, x_a, x_b, mirror, *rest):
     y, w, o_t, o_x, o_m, a0, b0, fa, fb, h2 = rest
-    info = Info(table_i, partner)
+    info = Info(info_ref)
     arrived = arrived_swap(info, t_a, t_b, x_a, x_b, mirror)
     dirac(phi, u, arrived, q0, q2, q3, (a0, b0, fa, fb), y, w)
     send_response(y, info, o_t, o_x, o_m, h2)
 
 
-def response2_kernel(table_i, partner, phi, u, q0, q2, q3, t_a, t_b, x_a, x_b, mirror, b_t, b_x, b_m, *rest):
+def response2_kernel(info_ref, phi, u, q0, q2, q3, t_a, t_b, x_a, x_b, mirror, b_t, b_x, b_m, *rest):
     y, w, o_t, o_x, o_m, a0, b0, fa, fb, h2 = rest
-    info = Info(table_i, partner)
+    info = Info(info_ref)
     arrived = list(arrived_swap(info, t_a, t_b, x_a, x_b, mirror))
     arrived[1] = lambda k, h: ld(b_t, k, h)
     arrived[3] = lambda k: b_x[k * 4 : k * 4 + 4, :]
@@ -325,8 +387,8 @@
     return force_values(left, right)
 
 
-def early_force_kernel(table_i, partner, phi, u, y, w, force, sent, a0):
-    info = Info(table_i, partner)
+def early_force_kernel(info_ref, phi, u, y, w, force, sent, a0):
+    info = Info(info_ref)
     nothing = jnp.zeros((4, 128), F32)
     for k in range(12):
         a0[k * HALO + 16 : k * HALO + 20, :] = nothing
@@ -352,13 +414,17 @@
 
 
 def send_blocks(dst, base, src, k, info):
-    for j in range(4):
-        at = pl.multiple_of(base * ROWS + 4 * info.partner[j], 4)
-        dst[pl.ds(at, 4), :] = src[k * ROWS + 4 * j : k * ROWS + 4 * j + 4, :]
-
-
-def late_force_kernel(table_i, partner, phi, u, y, w, r_t, r_x, r_m, f_t, f_x, f_m, sent):
-    info = Info(table_i, partner)
+    low, high = ld(src, k, 0), ld(src, k, 1)
+    low_turned, high_turned = pltpu.roll(low, 4, 0), pltpu.roll(high, 4, 0)
+    for h in range(2):
+        first, second, third = info.block_source[h]
+        value = jnp.where(third, high, high_turned)
+        value = jnp.where(second, low_turned, value)
+        st(dst, base, h, jnp.where(first, low, value))
+
+
+def late_force_kernel(info_ref, phi, u, y, w, r_t, r_x, r_m, f_t, f_x, f_m, sent):
+    info = Info(info_ref)
     for h in range(2):
         arrived = get_half(lambda k: ld(r_t, k, h))
         for n, value in enumerate(force_at(lambda ref, k: ld(ref, k, h), phi, u, y, w, 1, lambda ysp: arrived)):
@@ -374,20 +440,15 @@
     for n, value in enumerate(force_at(last_m, phi, u, y, w, 2, lambda ysp: face(r_m))):
         f_m[pl.ds(n * ROWS + 3, 4, stride=4), :] = value
     for n in range(8):
+        send_rows(sent, 40 + n, f_m, n, info, 3)
+
+
+def place_faces(mirrored, m_x, m_m):
+    for n in range(8):
+        face = mirrored[8 * ROWS + n * 4 : 8 * ROWS + n * 4 + 4, :]
         for j in range(4):
-            row = 8 * ROWS + 32 + n * 4 + info.partner[j]
-            sent[pl.ds(row, 1), :] = f_m[n * ROWS + 4 * j + 3 : n * ROWS + 4 * j + 4, :]
-
-
-def place_faces(info, mirrored, m_x, m_m):
-    block = jnp.int32(0)
-    for j in range(4):
-        block = block + jnp.where(info.partner[j] == 3, j, 0)
-    for n in range(8):
-        at = pl.multiple_of(n * ROWS + 4 * block, 4)
-        m_x[pl.ds(at, 4), :] = mirrored[8 * ROWS + n * 4 : 8 * ROWS + n * 4 + 4, :]
+            m_x[n * ROWS + 4 * j : n * ROWS + 4 * j + 4, :] = face
         m_m[pl.ds(n * ROWS + 3, 4, stride=4), :] = mirrored[8 * ROWS + 32 + n * 4 : 8 * ROWS + 32 + n * 4 + 4, :]
-    return block
 
 
 def both_forces(mu, h, block, early, mirror_early, f_t, f_x, f_m, mirrored, m_x, m_m):
@@ -480,15 +541,15 @@
         st(ref, base + 4 + 2 * n, h, upper[n][1])
 
 
-def put_full_momenta(new_p, old_p, mu, h, diag, upper):
+def put_full_momenta(new_p, old_p, at, mu, h, diag, upper):
     for i in range(3):
-        st(new_p, mu * 18 + 4 * i, h, diag[i])
-        st(new_p, mu * 18 + 9 + 4 * i, h, ld(old_p, mu * 18 + 9 + 4 * i, h))
+        st(new_p, at * 18 + 4 * i, h, diag[i])
+        st(new_p, at * 18 + 9 + 4 * i, h, ld(old_p, mu * 18 + 9 + 4 * i, h))
     for (i, j), v in zip(OFF, upper):
-        st(new_p, mu * 18 + 3 * i + j, h, v[0])
-        st(new_p, mu * 18 + 3 * j + i, h, v[0])
-        st(new_p, mu * 18 + 9 + 3 * i + j, h, v[1])
-        st(new_p, mu * 18 + 9 + 3 * j + i, h, -v[1])
+        st(new_p, at * 18 + 3 * i + j, h, v[0])
+        st(new_p, at * 18 + 3 * j + i, h, v[0])
+        st(new_p, at * 18 + 9 + 3 * i + j, h, v[1])
+        st(new_p, at * 18 + 9 + 3 * j + i, h, -v[1])
 
 
 def early_update_kernel(phi, u, p, early, mirror_early, new_u, new_p, q3):
@@ -501,24 +562,24 @@
         put_half(q3, h, mat_dag_half(link, project(spinor(phi, h), 3, -1)))
 
 
-def early_last_kernel(u, p, early, mirror_early, new_u, new_p):
+def early_last_kernel(u, p, old_p, early, mirror_early, new_u, new_p):
     for h in range(2):
         force, mirrored = (lambda n: ld(early, 16 + n, h)), (lambda n: ld(mirror_early, 16 + n, h))
         diag, upper = updated_momenta(lambda n: ld(p, 27 + n, h), force, mirrored)
-        put_momenta(new_p, 0, h, diag, upper)
+        put_full_momenta(new_p, old_p, 0, 3, h, diag, upper)
         put_matrix(new_u, 0, h, link_step(diag, upper, matrix(u, 3, h)))
 
 
-def update_kernel(table_i, partner, phi, u, p, u3, p3, *rest):
+def update_kernel(info_ref, phi, u, p, u3, p3, *rest):
     forces = rest[:6]
     new_u, new_p, o_t, o_x, o_m, q0, q2, m_x, m_m = rest[6:]
-    info = Info(table_i, partner)
-    block = place_faces(info, forces[5], m_x, m_m)
+    info = Info(info_ref)
+    place_faces(forces[5], m_x, m_m)
     for h in range(2):
         psi = spinor(phi, h)
         for mu in range(3):
             diag, upper = updated_momenta(
-                input_momentum(p, mu, h), *both_forces(mu, h, block, *forces, m_x, m_m)
+                input_momentum(p, mu, h), *both_forces(mu, h, info.edge_block, *forces, m_x, m_m)
             )
             put_momenta(new_p, mu * 9, h, diag, upper)
             link = link_step(diag, upper, matrix(u, mu, h))
@@ -535,36 +596,45 @@
         send_rows(o_m, k, q2, k, info, 3)
 
 
-def last_kernel(table_i, partner, u, p, old_p, u3, p3, *rest):
+def last_kernel(info_ref, u, p, old_p, u3, p3, *rest):
     forces = rest[:6]
-    new_u, new_p, m_x, m_m = rest[6:]
-    info = Info(table_i, partner)
-    block = place_faces(info, forces[5], m_x, m_m)
-    for h in range(2):
-        for mu in range(3):
+    out_u, out_p, new_u, new_p, m_x, m_m, sems = rest[6:]
+    info = Info(info_ref)
+    size = 18 * ROWS
+    copies = []
+
+    def send(src, dst, mu):
+        copies.append(pltpu.make_async_copy(src, dst.at[mu * size : mu * size + size, :], sems.at[len(copies)]))
+        copies[-1].start()
+
+    send(u3, out_u, 3)
+    send(p3, out_p, 3)
+    place_faces(forces[5], m_x, m_m)
+    for mu in range(3):
+        for h in range(2):
             diag, upper = updated_momenta(
-                lambda n: ld(p, mu * 9 + n, h), *both_forces(mu, h, block, *forces, m_x, m_m)
+                lambda n: ld(p, mu * 9 + n, h), *both_forces(mu, h, info.edge_block, *forces, m_x, m_m)
             )
-            put_full_momenta(new_p, old_p, mu, h, diag, upper)
+            put_full_momenta(new_p, old_p, mu, mu, h, diag, upper)
             put_matrix(new_u, mu, h, link_step(diag, upper, matrix(u, mu, h)))
-        diag = [ld(p3, n, h) for n in range(3)]
-        upper = [(ld(p3, 3 + 2 * n, h), ld(p3, 4 + 2 * n, h)) for n in range(3)]
-        put_full_momenta(new_p, old_p, 3, h, diag, upper)
-    new_u[54 * ROWS : 72 * ROWS, :] = u3[...]
+        send(new_p.at[mu * size : mu * size + size, :], out_p, mu)
+        send(new_u.at[mu * size : mu * size + size, :], out_u, mu)
+    for copy in copies:
+        copy.wait()
 
 
 VM = pl.BlockSpec(memory_space=pltpu.VMEM)
-SM = pl.BlockSpec(memory_space=pltpu.SMEM)
+HBM = pl.BlockSpec(memory_space=pltpu.HBM)
 FULL = ROWS * 12
 FACE = 4 * 12
 
 
-def call(kernel, n_scalar, args, outs, scratch, limit=4):
+def call(kernel, args, outs, scratch, limit=4, from_hbm=False, to_hbm=False):
     return pl.pallas_call(
         kernel,
-        out_shape=[jax.ShapeDtypeStruct((rows, 128), F32) for rows in outs],
-        in_specs=[SM] * n_scalar + [VM] * (len(args) - n_scalar),
-        out_specs=[VM] * len(outs),
+        out_shape=[jax.ShapeDtypeStruct((s, 128), F32) if isinstance(s, int) else s for s in outs],
+        in_specs=[HBM if from_hbm else VM] * len(args),
+        out_specs=[HBM if to_hbm else VM] * len(outs),
         scratch_shapes=[s if not isinstance(s, int) else pltpu.VMEM((s, 128), F32) for s in scratch],
         compiler_params=pltpu.CompilerParams(vmem_limit_bytes=limit << 20),
     )(*args)
@@ -623,13 +693,12 @@
     return [got[name] for name in ("near_t", "far_t", "near_x", "far_x", "mirror")]
 
 
-def all_forces(s, phi, u, y, w, o_t, o_x, o_m):
-    early, sent = call(early_force_kernel, 2, (*s, phi, u, y, w), [24 * ROWS, 24 * ROWS], [12 * HALO])
+def all_forces(masks, phi, u, y, w, o_t, o_x, o_m):
+    early, sent = call(early_force_kernel, (masks, phi, u, y, w), [24 * ROWS, 24 * ROWS], [12 * HALO])
     got = exchange(BACK_ORDER, back_t=o_t, back_x=o_x, mirror=o_m, early=sent)
     f_t, f_x, f_m, sent = call(
         late_force_kernel,
-        2,
-        (*s, phi, u, y, w, got["back_t"], got["back_x"], got["mirror"]),
+        (masks, phi, u, y, w, got["back_t"], got["back_x"], got["mirror"]),
         [8 * ROWS, 8 * ROWS, 8 * ROWS, 12 * ROWS],
         [],
     )
@@ -656,7 +725,6 @@
             jnp.where(lane == 2, jnp.where(ta == 0, -1, 1), jnp.where(ta == last, -1, 1)),
         ),
     ).astype(jnp.int32)
-    s = (info, partner)
     u = gauge_links.reshape(72 * ROWS, 128)
     p = momenta.reshape(72 * ROWS, 128)
     table = jnp.transpose(noise_table, (0, 2, 1, 3))
@@ -666,39 +734,54 @@
     halo = [12 * HALO, 12 * HALO, FULL, FULL]
     spin = 24 * ROWS
 
-    psi, *rest = call(
+    psi, *rest, masks = call(
         noise_kernel,
-        2,
-        (*s, index, table, u),
-        [spin] + messages + local,
-        [pltpu.VMEM((24, 4096), F32), pltpu.VMEM((384, 768), jnp.bfloat16), FULL, FULL],
+        [pltpu.with_memory_space_constraint(v, pltpu.HBM) for v in (info, partner, index, table, u)],
+        [spin] + messages + local + [jax.ShapeDtypeStruct((INFO_ROWS, 128), jnp.int32)],
+        [
+            pltpu.VMEM((24, 4096), F32),
+            pltpu.VMEM((384, 768), jnp.bfloat16),
+            FULL,
+            FULL,
+            pltpu.VMEM((2, 3, 4, 4096), F32),
+            72 * ROWS,
+            pltpu.VMEM((ROWS, 128), jnp.int32),
+            pltpu.SMEM((8,), jnp.int32),
+            pltpu.SMEM((4,), jnp.int32),
+            pltpu.SemaphoreType.DMA((5,)),
+        ],
         12,
+        from_hbm=True,
     )
     arrived = swap_exchange(*rest[:5])
-    phi, *rest = call(phi_kernel, 2, (*s, psi, u, *rest[5:], *arrived), [spin] + messages + local, halo + [FULL, FULL])
+    phi, *rest = call(phi_kernel, (masks, psi, u, *rest[5:], *arrived), [spin] + messages + local, halo + [FULL, FULL])
     arrived = swap_exchange(*rest[:5])
     y, w, o_t, o_x, o_m = call(
-        response_kernel, 2, (*s, phi, u, *rest[5:], *arrived), [spin, 4 * FULL, FULL, FACE, FACE], halo + [FULL]
+        response_kernel, (masks, phi, u, *rest[5:], *arrived), [spin, 4 * FULL, FULL, FACE, FACE], halo + [FULL]
     )
-    forces = all_forces(s, phi, u, y, w, o_t, o_x, o_m)
-    u3, p3, q3 = call(early_update_kernel, 0, (phi, u, p, *forces[:2]), [18 * ROWS, 9 * ROWS, FULL], [])
+    forces = all_forces(masks, phi, u, y, w, o_t, o_x, o_m)
+    u3, p3, q3 = call(early_update_kernel, (phi, u, p, *forces[:2]), [18 * ROWS, 9 * ROWS, FULL], [])
     u, p1, o_t, o_x, o_m, q0, q2 = call(
         update_kernel,
-        2,
-        (*s, phi, u, p, u3, p3, *forces),
+        (masks, phi, u, p, u3, p3, *forces),
         [72 * ROWS, 36 * ROWS, FULL, FACE, FACE, FULL, FULL],
         [8 * ROWS, 8 * ROWS],
     )
     y, w, o_t, o_x, o_m = call(
         response2_kernel,
-        2,
-        (*s, phi, u, q0, q2, q3, *arrived, *on_exchange(o_t, o_x, o_m)),
+        (masks, phi, u, q0, q2, q3, *arrived, *on_exchange(o_t, o_x, o_m)),
         [spin, 4 * FULL, FULL, FACE, FACE],
         halo + [FULL],
     )
-    forces = all_forces(s, phi, u, y, w, o_t, o_x, o_m)
-    u3, p3 = call(early_last_kernel, 0, (u, p1, *forces[:2]), [18 * ROWS, 9 * ROWS], [])
-    new_u, new_p = call(last_kernel, 2, (*s, u, p1, p, u3, p3, *forces), [72 * ROWS, 72 * ROWS], [8 * ROWS, 8 * ROWS])
+    forces = all_forces(masks, phi, u, y, w, o_t, o_x, o_m)
+    u3, p3 = call(early_last_kernel, (u, p1, p, *forces[:2]), [18 * ROWS, 18 * ROWS], [])
+    new_u, new_p = call(
+        last_kernel,
+        (masks, u, p1, p, u3, p3, *forces),
+        [72 * ROWS, 72 * ROWS],
+        [54 * ROWS, 54 * ROWS, 8 * ROWS, 8 * ROWS, pltpu.SemaphoreType.DMA((8,))],
+        to_hbm=True,
+    )
     return new_u.reshape(gauge_links.shape), new_p.reshape(momenta.shape)
 
 

time: 83.8 us -> 76 us (0.907)
  Pallas kernels: 13.1 us -> 7.56 us
  local copies, waits for them, and re-layouts: 2.73 us -> 0.01 us
    pallas_call x12, Pallas kernels: 13.1 us -> 7.56 us  [call(): pl.pallas_call(kernel, out_shape=[jax.ShapeDtypeStruct((s, 128), F32) if...]
    unnamed x10 -> x4, local copies, waits for them, and re-layouts: 2.73 us -> 0.01 us
  transfers between devices with their start and end apart: 23 -> 23, of which waited for: 12 -> 12; matrix products, arithmetic and copies ran while one was open for 0% -> 0% of each run, Pallas kernels for 2% -> 1%
where the time goes in v3:
time: 76 us; the launch traced here: 75.8 us
  starting transfers between devices  39.9 us (52%)
  waiting for transfers between devices  27.1 us (36%)
  Pallas kernels  7.56 us (10%)
    ppermute x9, starting transfers between devices, mirror_swap(): return lax.ppermute(value, 'xd', [(i, i ^ n // 2) for i in range(n)])  17.4 us
    ppermute x9, waiting for transfers between devices, mirror_swap(): return lax.ppermute(value, 'xd', [(i, i ^ n // 2) for i in range(n)])  15 us
    ppermute x8, starting transfers between devices, swap(): return lax.ppermute(value, axis, pairs)  13.8 us
    ppermute x6, starting transfers between devices, shift(): return lax.ppermute(value, axis, [(i, (i + by) % n) for i in range(n)])  8.67 us
    pallas_call x12, Pallas kernels, call(): pl.pallas_call(kernel, out_shape=[jax.ShapeDtypeStruct((s, 128), F32) if...  7.56 us
    ppermute x8, waiting for transfers between devices, swap(): return lax.ppermute(value, axis, pairs)  6.51 us
    ppermute x6, waiting for transfers between devices, shift(): return lax.ppermute(value, axis, [(i, (i + by) % n) for i in range(n)])  5.6 us
  transfers between devices with their start and end apart: 23, of which 12 were waited for; matrix products, arithmetic and copies ran while one was open for 0% of the time, Pallas kernels for 1%

profile of v3, /device:TPU:0, one launch (start us, length us, event | category | flops | bytes accessed | tf_op | source)
XLA Modules:
  0.0 75.8 jit_solution(303965660684166143)
XLA Ops:
  0.7 0.5 compare_select_fusion.2.table_i_hbm
  1.2 2.9 %shard_map.68 = (f32[384,128]{1,0:T(8,128)S(1)}, f32[192,128]{1,0:T(8,128)S(1)}, f32[192,128]{1,0:T(8,128)S(1)}, f32[48,128]{1,0:T(8,128)S(1)}, f32[48,128]{1,0:...) custom-call(s32[8]{0:T(128)} %compare_select_fusion.2.table_i_hbm, ...), custom_call_target="tpu_custom_call" | custom-call | tf_op jit(solution)/shard_map/pallas_call | solution.py:633
  4.1 5.6 %collective-permute-start.1 = (f32[192,128]{1,0:T(8,128)S(1)}, f32[192,128]{1,0:T(8,128)S(1)}, u32[]{:S(2)}, u32[]{:S(2)}) collective-permute-start(f32[192,128]{1,0:T(8,128)S(1)} %get-tuple-element.63), channel_id=1, source_target_pairs={{0,15},{1,2},{2,1},{3,4},{4,3},{5,6},{6,5},{7,8},{8,7},{9,10},{10,... | collective-permute-start | bytes 294920 | tf_op jit(solution)/shard_map/ppermute | solution.py:649
  9.8 3.9 %collective-permute-start.4 = (f32[96,128]{1,0:T(8,128)S(1)}, f32[96,128]{1,0:T(8,128)S(1)}, u32[]{:S(2)}, u32[]{:S(2)}) collective-permute-start(f32[96,128]{1,0:T(8,128)S(1)} %get-tuple-element.66), channel_id=1, source_target_pairs={{0,64},{16,80},{32,96},{48,112},{64,0},{80,16},{96,32},{112,48},{1... | collective-permute-start | bytes 147464 | tf_op jit(solution)/shard_map/ppermute | solution.py:659
  13.6 0.7 collective-permute-start.2
  14.3 1.5 %collective-permute-start.3 = (f32[48,128]{1,0:T(8,128)S(1)}, f32[48,128]{1,0:T(8,128)S(1)}, u32[]{:S(2)}, u32[]{:S(2)}) collective-permute-start(f32[48,128]{1,0:T(8,128)S(1)} %get-tuple-element.65), channel_id=1, source_target_pairs={{0,112},{16,32},{32,16},{48,64},{64,48},{80,96},{96,80},{112,0},{1... | collective-permute-start | bytes 73736 | tf_op jit(solution)/shard_map/ppermute | solution.py:649
  15.8 1.6 %collective-permute-done.2.x_a = f32[48,128]{1,0:T(8,128)S(1)} collective-permute-done((f32[48,128]{1,0:T(8,128)S(1)}, f32[48,128]{1,0:T(8,128)S(1)}, u32[]{:S(2)}, u32[]{:S(2)}) %collective-permute-start.2) | collective-permute-done | bytes 24608 | tf_op jit(solution)/shard_map/ppermute | solution.py:649
  17.5 2.8 %collective-permute-done.3.x_b = f32[48,128]{1,0:T(8,128)S(1)} collective-permute-done((f32[48,128]{1,0:T(8,128)S(1)}, f32[48,128]{1,0:T(8,128)S(1)}, u32[]{:S(2)}, u32[]{:S(2)}) %collective-permute-start.3) | collective-permute-done | bytes 24608 | tf_op jit(solution)/shard_map/ppermute | solution.py:649
  20.3 0.5 shard_map.69
  20.9 1.9 %collective-permute-start.6 = (f32[192,128]{1,0:T(8,128)S(1)}, f32[192,128]{1,0:T(8,128)S(1)}, u32[]{:S(2)}, u32[]{:S(2)}) collective-permute-start(f32[192,128]{1,0:T(8,128)S(1)} %get-tuple-element.72), channel_id=1, source_target_pairs={{0,15},{1,2},{2,1},{3,4},{4,3},{5,6},{6,5},{7,8},{8,7},{9,10},{10,... | collective-permute-start | bytes 294920 | tf_op jit(solution)/shard_map/ppermute | solution.py:649
  22.9 3.9 %collective-permute-start.8 = (f32[48,128]{1,0:T(8,128)S(1)}, f32[48,128]{1,0:T(8,128)S(1)}, u32[]{:S(2)}, u32[]{:S(2)}) collective-permute-start(f32[48,128]{1,0:T(8,128)S(1)} %get-tuple-element.74), channel_id=1, source_target_pairs={{0,112},{16,32},{32,16},{48,64},{64,48},{80,96},{96,80},{112,0},{1... | collective-permute-start | bytes 73736 | tf_op jit(solution)/shard_map/ppermute | solution.py:649
  26.8 2.1 %collective-permute-done.8.x_b = f32[48,128]{1,0:T(8,128)S(1)} collective-permute-done((f32[48,128]{1,0:T(8,128)S(1)}, f32[48,128]{1,0:T(8,128)S(1)}, u32[]{:S(2)}, u32[]{:S(2)}) %collective-permute-start.8) | collective-permute-done | bytes 24608 | tf_op jit(solution)/shard_map/ppermute | solution.py:649
  29.6 2.3 %collective-permute-start.10 = (f32[384,128]{1,0:T(8,128)S(1)}, f32[384,128]{1,0:T(8,128)S(1)}, u32[]{:S(2)}, u32[]{:S(2)}) collective-permute-start(f32[384,128]{1,0:T(8,128)S(1)} %get-tuple-element.79), channel_id=1, source_target_pairs={{0,64},{16,80},{32,96},{48,112},{64,0},{80,16},{96,32},{112,48},{1... | collective-permute-start | bytes 589832 | tf_op jit(solution)/shard_map/ppermute | solution.py:659
  32.0 2.2 %collective-permute-start.11 = (f32[192,128]{1,0:T(8,128)S(1)}, f32[192,128]{1,0:T(8,128)S(1)}, u32[]{:S(2)}, u32[]{:S(2)}) collective-permute-start(f32[192,128]{1,0:T(8,128)S(1)} %get-tuple-element.82), channel_id=1, source_target_pairs={{0,15},{1,0},{2,1},{3,2},{4,3},{5,4},{6,5},{7,6},{8,7},{9,8},{10,9... | collective-permute-start | bytes 294920 | tf_op jit(solution)/shard_map/ppermute | solution.py:654
  34.2 1.0 %collective-permute-start.12 = (f32[48,128]{1,0:T(8,128)S(1)}, f32[48,128]{1,0:T(8,128)S(1)}, u32[]{:S(2)}, u32[]{:S(2)}) collective-permute-start(f32[48,128]{1,0:T(8,128)S(1)} %get-tuple-element.83), channel_id=1, source_target_pairs={{0,112},{16,0},{32,16},{48,32},{64,48},{80,64},{96,80},{112,96},{1... | collective-permute-start | bytes 73736 | tf_op jit(solution)/shard_map/ppermute | solution.py:654
  35.2 2.4 %collective-permute-start.13 = (f32[48,128]{1,0:T(8,128)S(1)}, f32[48,128]{1,0:T(8,128)S(1)}, u32[]{:S(2)}, u32[]{:S(2)}) collective-permute-start(f32[48,128]{1,0:T(8,128)S(1)} %get-tuple-element.84), channel_id=1, source_target_pairs={{0,64},{16,80},{32,96},{48,112},{64,0},{80,16},{96,32},{112,48},{1... | collective-permute-start | bytes 73736 | tf_op jit(solution)/shard_map/ppermute | solution.py:659
  38.0 2.5 %collective-permute-done.13.r_m = f32[48,128]{1,0:T(8,128)S(1)} collective-permute-done((f32[48,128]{1,0:T(8,128)S(1)}, f32[48,128]{1,0:T(8,128)S(1)}, u32[]{:S(2)}, u32[]{:S(2)}) %collective-permute-start.13) | collective-permute-done | bytes 24608 | tf_op jit(solution)/shard_map/ppermute | solution.py:659
  40.9 2.5 %collective-permute-start.14 = (f32[192,128]{1,0:T(8,128)S(1)}, f32[192,128]{1,0:T(8,128)S(1)}, u32[]{:S(2)}, u32[]{:S(2)}) collective-permute-start(f32[192,128]{1,0:T(8,128)S(1)} %get-tuple-element.88), channel_id=1, source_target_pairs={{0,64},{16,80},{32,96},{48,112},{64,0},{80,16},{96,32},{112,48},{1... | collective-permute-start | bytes 294920 | tf_op jit(solution)/shard_map/ppermute | solution.py:659
  43.5 3.6 %collective-permute-done.14.rest_5_ = f32[192,128]{1,0:T(8,128)S(1)} collective-permute-done((f32[192,128]{1,0:T(8,128)S(1)}, f32[192,128]{1,0:T(8,128)S(1)}, u32[]{:S(2)}, u32[]{:S(2)}) %collective-permute-start.14) | collective-permute-done | bytes 98336 | tf_op jit(solution)/shard_map/ppermute | solution.py:659
  47.1 0.6 shard_map.74
  47.7 1.1 %collective-permute-start.16 = (f32[48,128]{1,0:T(8,128)S(1)}, f32[48,128]{1,0:T(8,128)S(1)}, u32[]{:S(2)}, u32[]{:S(2)}) collective-permute-start(f32[48,128]{1,0:T(8,128)S(1)} %get-tuple-element.95), channel_id=1, source_target_pairs={{0,16},{16,32},{32,48},{48,64},{64,80},{80,96},{96,112},{112,0},{1... | collective-permute-start | bytes 73736 | tf_op jit(solution)/shard_map/ppermute | solution.py:654
  48.8 1.5 %collective-permute-start.17 = (f32[48,128]{1,0:T(8,128)S(1)}, f32[48,128]{1,0:T(8,128)S(1)}, u32[]{:S(2)}, u32[]{:S(2)}) collective-permute-start(f32[48,128]{1,0:T(8,128)S(1)} %get-tuple-element.96), channel_id=1, source_target_pairs={{0,64},{16,80},{32,96},{48,112},{64,0},{80,16},{96,32},{112,48},{1... | collective-permute-start | bytes 73736 | tf_op jit(solution)/shard_map/ppermute | solution.py:659
  50.3 3.5 %collective-permute-done.16.b_x = f32[48,128]{1,0:T(8,128)S(1)} collective-permute-done((f32[48,128]{1,0:T(8,128)S(1)}, f32[48,128]{1,0:T(8,128)S(1)}, u32[]{:S(2)}, u32[]{:S(2)}) %collective-permute-start.16) | collective-permute-done | bytes 24608 | tf_op jit(solution)/shard_map/ppermute | solution.py:654
  54.1 1.3 %collective-permute-done.15.b_t = f32[192,128]{1,0:T(8,128)S(1)} collective-permute-done((f32[192,128]{1,0:T(8,128)S(1)}, f32[192,128]{1,0:T(8,128)S(1)}, u32[]{:S(2)}, u32[]{:S(2)}) %collective-permute-start.15) | collective-permute-done | bytes 98336 | tf_op jit(solution)/shard_map/ppermute | solution.py:654
  56.1 2.5 %collective-permute-start.18 = (f32[384,128]{1,0:T(8,128)S(1)}, f32[384,128]{1,0:T(8,128)S(1)}, u32[]{:S(2)}, u32[]{:S(2)}) collective-permute-start(f32[384,128]{1,0:T(8,128)S(1)} %get-tuple-element.100), channel_id=1, source_target_pairs={{0,64},{16,80},{32,96},{48,112},{64,0},{80,16},{96,32},{112,48},{1... | collective-permute-start | bytes 589832 | tf_op jit(solution)/shard_map/ppermute | solution.py:659
  58.6 2.0 %collective-permute-start.19 = (f32[192,128]{1,0:T(8,128)S(1)}, f32[192,128]{1,0:T(8,128)S(1)}, u32[]{:S(2)}, u32[]{:S(2)}) collective-permute-start(f32[192,128]{1,0:T(8,128)S(1)} %get-tuple-element.103), channel_id=1, source_target_pairs={{0,15},{1,0},{2,1},{3,2},{4,3},{5,4},{6,5},{7,6},{8,7},{9,8},{10,9... | collective-permute-start | bytes 294920 | tf_op jit(solution)/shard_map/ppermute | solution.py:654
  60.6 2.2 %collective-permute-start.20 = (f32[48,128]{1,0:T(8,128)S(1)}, f32[48,128]{1,0:T(8,128)S(1)}, u32[]{:S(2)}, u32[]{:S(2)}) collective-permute-start(f32[48,128]{1,0:T(8,128)S(1)} %get-tuple-element.104), channel_id=1, source_target_pairs={{0,112},{16,0},{32,16},{48,32},{64,48},{80,64},{96,80},{112,96},{1... | collective-permute-start | bytes 73736 | tf_op jit(solution)/shard_map/ppermute | solution.py:654
  62.8 1.2 %collective-permute-start.21 = (f32[48,128]{1,0:T(8,128)S(1)}, f32[48,128]{1,0:T(8,128)S(1)}, u32[]{:S(2)}, u32[]{:S(2)}) collective-permute-start(f32[48,128]{1,0:T(8,128)S(1)} %get-tuple-element.105), channel_id=1, source_target_pairs={{0,64},{16,80},{32,96},{48,112},{64,0},{80,16},{96,32},{112,48},{1... | collective-permute-start | bytes 73736 | tf_op jit(solution)/shard_map/ppermute | solution.py:659
  64.4 3.7 %collective-permute-done.21.r_m = f32[48,128]{1,0:T(8,128)S(1)} collective-permute-done((f32[48,128]{1,0:T(8,128)S(1)}, f32[48,128]{1,0:T(8,128)S(1)}, u32[]{:S(2)}, u32[]{:S(2)}) %collective-permute-start.21) | collective-permute-done | bytes 24608 | tf_op jit(solution)/shard_map/ppermute | solution.py:659
  68.4 1.2 %collective-permute-start.22 = (f32[192,128]{1,0:T(8,128)S(1)}, f32[192,128]{1,0:T(8,128)S(1)}, u32[]{:S(2)}, u32[]{:S(2)}) collective-permute-start(f32[192,128]{1,0:T(8,128)S(1)} %get-tuple-element.109), channel_id=1, source_target_pairs={{0,64},{16,80},{32,96},{48,112},{64,0},{80,16},{96,32},{112,48},{1... | collective-permute-start | bytes 294920 | tf_op jit(solution)/shard_map/ppermute | solution.py:659
  69.8 4.8 %collective-permute-done.22.rest_5_ = f32[192,128]{1,0:T(8,128)S(1)} collective-permute-done((f32[192,128]{1,0:T(8,128)S(1)}, f32[192,128]{1,0:T(8,128)S(1)}, u32[]{:S(2)}, u32[]{:S(2)}) %collective-permute-start.22) | collective-permute-done | bytes 98336 | tf_op jit(solution)/shard_map/ppermute | solution.py:659
  74.6 1.2 %shard_map.79 = (f32[1152,128]{1,0:T(8,128)}, f32[1152,128]{1,0:T(8,128)}) custom-call(s32[64,128]{1,0:T(8,128)S(1)} %get-tuple-element.57.info_ref, f32[1152,128]{1,0:T(8,128)S(1)} %get-tuple-element.89.u, f32[576,128]{1,0:T(8,128)S(1)} %get-tuple-element.90.p, f32[1152,128]{1,0:T(8,128)S(1)} %bitcast.20, f32[288,128]{1,0:T(8,128)S(1)} %get-tuple-element.101.u3, ...), custom_call_target="tpu_custom_call" | custom-call | tf_op jit(solution)/shard_map/pallas_call | solution.py:633
  (31 shorter events, 3.9 us)
Async XLA Ops:
  0.6 19.6 %copy-start = (f32[4,2,3,3,4,1,4,128]{7,6,5,4,3,2,1,0:T(4,128)S(1)}, f32[4,2,3,3,4,1,4,128]{7,6,5,4,3,2,1,0:T(4,128)}, u32[]{:S(2)}) copy-start(f32[4,2,3,3,4,1,4,128]{7,6,5,4,3,2,1,0:T(4,128)} %param.5) | copy-start | bytes 1769476
  4.1 16.2 %collective-permute-start = (f32[192,128]{1,0:T(8,128)S(1)}, f32[192,128]{1,0:T(8,128)S(1)}, u32[]{:S(2)}, u32[]{:S(2)}) collective-permute-start(f32[192,128]{1,0:T(8,128)S(1)} %get-tuple-element.62), channel_id=1, source_target_pairs={{0,1},{1,0},{2,3},{3,2},{4,5},{5,4},{6,7},{7,6},{8,9},{9,8},{10,11... | collective-permute-start | bytes 294920 | tf_op jit(solution)/shard_map/ppermute | solution.py:649
  4.1 16.1 %collective-permute-start.1 = (f32[192,128]{1,0:T(8,128)S(1)}, f32[192,128]{1,0:T(8,128)S(1)}, u32[]{:S(2)}, u32[]{:S(2)}) collective-permute-start(f32[192,128]{1,0:T(8,128)S(1)} %get-tuple-element.63), channel_id=1, source_target_pairs={{0,15},{1,2},{2,1},{3,4},{4,3},{5,6},{6,5},{7,8},{8,7},{9,10},{10,... | collective-permute-start | bytes 294920 | tf_op jit(solution)/shard_map/ppermute | solution.py:649
  9.8 10.5 %collective-permute-start.4 = (f32[96,128]{1,0:T(8,128)S(1)}, f32[96,128]{1,0:T(8,128)S(1)}, u32[]{:S(2)}, u32[]{:S(2)}) collective-permute-start(f32[96,128]{1,0:T(8,128)S(1)} %get-tuple-element.66), channel_id=1, source_target_pairs={{0,64},{16,80},{32,96},{48,112},{64,0},{80,16},{96,32},{112,48},{1... | collective-permute-start | bytes 147464 | tf_op jit(solution)/shard_map/ppermute | solution.py:659
  13.6 3.8 %collective-permute-start.2 = (f32[48,128]{1,0:T(8,128)S(1)}, f32[48,128]{1,0:T(8,128)S(1)}, u32[]{:S(2)}, u32[]{:S(2)}) collective-permute-start(f32[48,128]{1,0:T(8,128)S(1)} %get-tuple-element.64), channel_id=1, source_target_pairs={{0,16},{16,0},{32,48},{48,32},{64,80},{80,64},{96,112},{112,96},{1... | collective-permute-start | bytes 73736 | tf_op jit(solution)/shard_map/ppermute | solution.py:649
  14.3 5.9 %collective-permute-start.3 = (f32[48,128]{1,0:T(8,128)S(1)}, f32[48,128]{1,0:T(8,128)S(1)}, u32[]{:S(2)}, u32[]{:S(2)}) collective-permute-start(f32[48,128]{1,0:T(8,128)S(1)} %get-tuple-element.65), channel_id=1, source_target_pairs={{0,112},{16,32},{32,16},{48,64},{64,48},{80,96},{96,80},{112,0},{1... | collective-permute-start | bytes 73736 | tf_op jit(solution)/shard_map/ppermute | solution.py:649
  20.8 8.0 %collective-permute-start.5 = (f32[192,128]{1,0:T(8,128)S(1)}, f32[192,128]{1,0:T(8,128)S(1)}, u32[]{:S(2)}, u32[]{:S(2)}) collective-permute-start(f32[192,128]{1,0:T(8,128)S(1)} %get-tuple-element.71), channel_id=1, source_target_pairs={{0,1},{1,0},{2,3},{3,2},{4,5},{5,4},{6,7},{7,6},{8,9},{9,8},{10,11... | collective-permute-start | bytes 294920 | tf_op jit(solution)/shard_map/ppermute | solution.py:649
  20.9 8.0 %collective-permute-start.6 = (f32[192,128]{1,0:T(8,128)S(1)}, f32[192,128]{1,0:T(8,128)S(1)}, u32[]{:S(2)}, u32[]{:S(2)}) collective-permute-start(f32[192,128]{1,0:T(8,128)S(1)} %get-tuple-element.72), channel_id=1, source_target_pairs={{0,15},{1,2},{2,1},{3,4},{4,3},{5,6},{6,5},{7,8},{8,7},{9,10},{10,... | collective-permute-start | bytes 294920 | tf_op jit(solution)/shard_map/ppermute | solution.py:649
  22.8 6.0 %collective-permute-start.9 = (f32[96,128]{1,0:T(8,128)S(1)}, f32[96,128]{1,0:T(8,128)S(1)}, u32[]{:S(2)}, u32[]{:S(2)}) collective-permute-start(f32[96,128]{1,0:T(8,128)S(1)} %get-tuple-element.75), channel_id=1, source_target_pairs={{0,64},{16,80},{32,96},{48,112},{64,0},{80,16},{96,32},{112,48},{1... | collective-permute-start | bytes 147464 | tf_op jit(solution)/shard_map/ppermute | solution.py:659
  22.9 3.9 %collective-permute-start.7 = (f32[48,128]{1,0:T(8,128)S(1)}, f32[48,128]{1,0:T(8,128)S(1)}, u32[]{:S(2)}, u32[]{:S(2)}) collective-permute-start(f32[48,128]{1,0:T(8,128)S(1)} %get-tuple-element.73), channel_id=1, source_target_pairs={{0,16},{16,0},{32,48},{48,32},{64,80},{80,64},{96,112},{112,96},{1... | collective-permute-start | bytes 73736 | tf_op jit(solution)/shard_map/ppermute | solution.py:649
  22.9 6.0 %collective-permute-start.8 = (f32[48,128]{1,0:T(8,128)S(1)}, f32[48,128]{1,0:T(8,128)S(1)}, u32[]{:S(2)}, u32[]{:S(2)}) collective-permute-start(f32[48,128]{1,0:T(8,128)S(1)} %get-tuple-element.74), channel_id=1, source_target_pairs={{0,112},{16,32},{32,16},{48,64},{64,48},{80,96},{96,80},{112,0},{1... | collective-permute-start | bytes 73736 | tf_op jit(solution)/shard_map/ppermute | solution.py:649
  29.6 13.7 %collective-permute-start.10 = (f32[384,128]{1,0:T(8,128)S(1)}, f32[384,128]{1,0:T(8,128)S(1)}, u32[]{:S(2)}, u32[]{:S(2)}) collective-permute-start(f32[384,128]{1,0:T(8,128)S(1)} %get-tuple-element.79), channel_id=1, source_target_pairs={{0,64},{16,80},{32,96},{48,112},{64,0},{80,16},{96,32},{112,48},{1... | collective-permute-start | bytes 589832 | tf_op jit(solution)/shard_map/ppermute | solution.py:659
  32.0 8.6 %collective-permute-start.11 = (f32[192,128]{1,0:T(8,128)S(1)}, f32[192,128]{1,0:T(8,128)S(1)}, u32[]{:S(2)}, u32[]{:S(2)}) collective-permute-start(f32[192,128]{1,0:T(8,128)S(1)} %get-tuple-element.82), channel_id=1, source_target_pairs={{0,15},{1,0},{2,1},{3,2},{4,3},{5,4},{6,5},{7,6},{8,7},{9,8},{10,9... | collective-permute-start | bytes 294920 | tf_op jit(solution)/shard_map/ppermute | solution.py:654
  34.2 3.8 %collective-permute-start.12 = (f32[48,128]{1,0:T(8,128)S(1)}, f32[48,128]{1,0:T(8,128)S(1)}, u32[]{:S(2)}, u32[]{:S(2)}) collective-permute-start(f32[48,128]{1,0:T(8,128)S(1)} %get-tuple-element.83), channel_id=1, source_target_pairs={{0,112},{16,0},{32,16},{48,32},{64,48},{80,64},{96,80},{112,96},{1... | collective-permute-start | bytes 73736 | tf_op jit(solution)/shard_map/ppermute | solution.py:654
  35.2 8.1 %copy-start.1 = (f32[4,2,3,3,4,1,4,128]{7,6,5,4,3,2,1,0:T(4,128)S(1)}, f32[4,2,3,3,4,1,4,128]{7,6,5,4,3,2,1,0:T(4,128)}, u32[]{:S(2)}) copy-start(f32[4,2,3,3,4,1,4,128]{7,6,5,4,3,2,1,0:T(4,128)} %param.6) | copy-start | bytes 1769476
  35.2 5.3 %collective-permute-start.13 = (f32[48,128]{1,0:T(8,128)S(1)}, f32[48,128]{1,0:T(8,128)S(1)}, u32[]{:S(2)}, u32[]{:S(2)}) collective-permute-start(f32[48,128]{1,0:T(8,128)S(1)} %get-tuple-element.84), channel_id=1, source_target_pairs={{0,64},{16,80},{32,96},{48,112},{64,0},{80,16},{96,32},{112,48},{1... | collective-permute-start | bytes 73736 | tf_op jit(solution)/shard_map/ppermute | solution.py:659
  40.9 6.2 %collective-permute-start.14 = (f32[192,128]{1,0:T(8,128)S(1)}, f32[192,128]{1,0:T(8,128)S(1)}, u32[]{:S(2)}, u32[]{:S(2)}) collective-permute-start(f32[192,128]{1,0:T(8,128)S(1)} %get-tuple-element.88), channel_id=1, source_target_pairs={{0,64},{16,80},{32,96},{48,112},{64,0},{80,16},{96,32},{112,48},{1... | collective-permute-start | bytes 294920 | tf_op jit(solution)/shard_map/ppermute | solution.py:659
  47.6 7.7 %collective-permute-start.15 = (f32[192,128]{1,0:T(8,128)S(1)}, f32[192,128]{1,0:T(8,128)S(1)}, u32[]{:S(2)}, u32[]{:S(2)}) collective-permute-start(f32[192,128]{1,0:T(8,128)S(1)} %get-tuple-element.94), channel_id=1, source_target_pairs={{0,1},{1,2},{2,3},{3,4},{4,5},{5,6},{6,7},{7,8},{8,9},{9,10},{10,1... | collective-permute-start | bytes 294920 | tf_op jit(solution)/shard_map/ppermute | solution.py:654
  47.7 6.0 %collective-permute-start.16 = (f32[48,128]{1,0:T(8,128)S(1)}, f32[48,128]{1,0:T(8,128)S(1)}, u32[]{:S(2)}, u32[]{:S(2)}) collective-permute-start(f32[48,128]{1,0:T(8,128)S(1)} %get-tuple-element.95), channel_id=1, source_target_pairs={{0,16},{16,32},{32,48},{48,64},{64,80},{80,96},{96,112},{112,0},{1... | collective-permute-start | bytes 73736 | tf_op jit(solution)/shard_map/ppermute | solution.py:654
  48.8 5.3 %collective-permute-start.17 = (f32[48,128]{1,0:T(8,128)S(1)}, f32[48,128]{1,0:T(8,128)S(1)}, u32[]{:S(2)}, u32[]{:S(2)}) collective-permute-start(f32[48,128]{1,0:T(8,128)S(1)} %get-tuple-element.96), channel_id=1, source_target_pairs={{0,64},{16,80},{32,96},{48,112},{64,0},{80,16},{96,32},{112,48},{1... | collective-permute-start | bytes 73736 | tf_op jit(solution)/shard_map/ppermute | solution.py:659
  56.1 13.6 %collective-permute-start.18 = (f32[384,128]{1,0:T(8,128)S(1)}, f32[384,128]{1,0:T(8,128)S(1)}, u32[]{:S(2)}, u32[]{:S(2)}) collective-permute-start(f32[384,128]{1,0:T(8,128)S(1)} %get-tuple-element.100), channel_id=1, source_target_pairs={{0,64},{16,80},{32,96},{48,112},{64,0},{80,16},{96,32},{112,48},{1... | collective-permute-start | bytes 589832 | tf_op jit(solution)/shard_map/ppermute | solution.py:659
  58.6 9.6 %collective-permute-start.19 = (f32[192,128]{1,0:T(8,128)S(1)}, f32[192,128]{1,0:T(8,128)S(1)}, u32[]{:S(2)}, u32[]{:S(2)}) collective-permute-start(f32[192,128]{1,0:T(8,128)S(1)} %get-tuple-element.103), channel_id=1, source_target_pairs={{0,15},{1,0},{2,1},{3,2},{4,3},{5,4},{6,5},{7,6},{8,7},{9,8},{10,9... | collective-permute-start | bytes 294920 | tf_op jit(solution)/shard_map/ppermute | solution.py:654
  60.6 3.8 %collective-permute-start.20 = (f32[48,128]{1,0:T(8,128)S(1)}, f32[48,128]{1,0:T(8,128)S(1)}, u32[]{:S(2)}, u32[]{:S(2)}) collective-permute-start(f32[48,128]{1,0:T(8,128)S(1)} %get-tuple-element.104), channel_id=1, source_target_pairs={{0,112},{16,0},{32,16},{48,32},{64,48},{80,64},{96,80},{112,96},{1... | collective-permute-start | bytes 73736 | tf_op jit(solution)/shard_map/ppermute | solution.py:654
  62.8 5.3 %collective-permute-start.21 = (f32[48,128]{1,0:T(8,128)S(1)}, f32[48,128]{1,0:T(8,128)S(1)}, u32[]{:S(2)}, u32[]{:S(2)}) collective-permute-start(f32[48,128]{1,0:T(8,128)S(1)} %get-tuple-element.105), channel_id=1, source_target_pairs={{0,64},{16,80},{32,96},{48,112},{64,0},{80,16},{96,32},{112,48},{1... | collective-permute-start | bytes 73736 | tf_op jit(solution)/shard_map/ppermute | solution.py:659
  68.4 6.2 %collective-permute-start.22 = (f32[192,128]{1,0:T(8,128)S(1)}, f32[192,128]{1,0:T(8,128)S(1)}, u32[]{:S(2)}, u32[]{:S(2)}) collective-permute-start(f32[192,128]{1,0:T(8,128)S(1)} %get-tuple-element.109), channel_id=1, source_target_pairs={{0,64},{16,80},{32,96},{48,112},{64,0},{80,16},{96,32},{112,48},{1... | collective-permute-start | bytes 294920 | tf_op jit(solution)/shard_map/ppermute | solution.py:659

commit v4 on v3

--- a/solution.py
+++ b/solution.py
@@ -262,16 +262,15 @@
     )
 
 
-def noise_kernel(table_i_hbm, partner_hbm, index_hbm, table_hbm, u_hbm, *rest):
+def noise_kernel(partner_hbm, index_hbm, table_hbm, u_hbm, *rest):
     psi, t_a, t_b, x_a, x_b, mirror, q0, q2, q3, info_ref = rest[:10]
-    flat, parts, h0, h2, table, u, index, table_i, partner, sems = rest[10:]
+    flat, parts, h0, h2, table, u, index, partner, sems = rest[10:]
     copies = [
         pltpu.make_async_copy(src, dst, sems.at[n])
         for n, (src, dst) in enumerate(
             (
                 (index_hbm, index),
                 (table_hbm, table),
-                (table_i_hbm, table_i),
                 (partner_hbm, partner),
                 (u_hbm, u),
             )
@@ -307,10 +306,12 @@
                 value = jnp.where(high == hi, found[hi * 24 : hi * 24 + 24, 128 * n : 128 * n + 128], value)
             psi[pl.ds(r + n, 24, stride=16), :] = value
     copies[2].wait()
+    ta, xd = lax.axis_index("ta"), lax.axis_index("xd")
+    sign_ahead = jnp.where(ta == 0, -1, 1)
+    sign_behind = jnp.where(ta == lax.axis_size("ta") - 1, -1, 1)
+    write_info(info_ref, ta & 1, xd & 1, sign_ahead, sign_behind, [partner[j] & 3 for j in range(4)])
+    info = Info(info_ref)
     copies[3].wait()
-    write_info(info_ref, *(table_i[n] for n in range(4)), [partner[j] & 3 for j in range(4)])
-    info = Info(info_ref)
-    copies[4].wait()
     send_both(psi, u, info, t_a, t_b, x_a, x_b, mirror, q0, q2, q3, h0, h2)
 
 
@@ -680,7 +681,7 @@
 
 
 SWAP_ORDER = ("far_t", "mirror", "far_x", "near_x", "near_t")
-BACK_ORDER = ("back_t", "mirror", "back_x", "early")
+BACK_ORDER = ("mirror", "back_t", "back_x", "early")
 ON_ORDER = ("on_t", "mirror", "on_x")
 
 
@@ -712,19 +713,6 @@
 
 
 def per_device(gauge_links, momenta, noise_table, noise_index, partner):
-    ta = lax.axis_index("ta")
-    xd = lax.axis_index("xd")
-    lane = lax.iota(jnp.int32, 8)
-    last = lax.axis_size("ta") - 1
-    info = jnp.where(
-        lane == 0,
-        ta & 1,
-        jnp.where(
-            lane == 1,
-            xd & 1,
-            jnp.where(lane == 2, jnp.where(ta == 0, -1, 1), jnp.where(ta == last, -1, 1)),
-        ),
-    ).astype(jnp.int32)
     u = gauge_links.reshape(72 * ROWS, 128)
     p = momenta.reshape(72 * ROWS, 128)
     table = jnp.transpose(noise_table, (0, 2, 1, 3))
@@ -736,7 +724,7 @@
 
     psi, *rest, masks = call(
         noise_kernel,
-        [pltpu.with_memory_space_constraint(v, pltpu.HBM) for v in (info, partner, index, table, u)],
+        [pltpu.with_memory_space_constraint(v, pltpu.HBM) for v in (partner, index, table, u)],
         [spin] + messages + local + [jax.ShapeDtypeStruct((INFO_ROWS, 128), jnp.int32)],
         [
             pltpu.VMEM((24, 4096), F32),
@@ -746,9 +734,8 @@
             pltpu.VMEM((2, 3, 4, 4096), F32),
             72 * ROWS,
             pltpu.VMEM((ROWS, 128), jnp.int32),
-            pltpu.SMEM((8,), jnp.int32),
             pltpu.SMEM((4,), jnp.int32),
-            pltpu.SemaphoreType.DMA((5,)),
+            pltpu.SemaphoreType.DMA((4,)),
         ],
         12,
         from_hbm=True,

time: 76 us -> 75.5 us (level)
  no operation moved by 1% of the time
where the time goes in v4:
time: 75.5 us; the launch traced here: 75.3 us
  starting transfers between devices  39.9 us (53%)
  waiting for transfers between devices  27.1 us (36%)
  Pallas kernels  7.62 us (10%)
    ppermute x9, starting transfers between devices, mirror_swap(): return lax.ppermute(value, 'xd', [(i, i ^ n // 2) for i in range(n)])  17.4 us
    ppermute x9, waiting for transfers between devices, mirror_swap(): return lax.ppermute(value, 'xd', [(i, i ^ n // 2) for i in range(n)])  15 us
    ppermute x8, starting transfers between devices, swap(): return lax.ppermute(value, axis, pairs)  13.8 us
    ppermute x6, starting transfers between devices, shift(): return lax.ppermute(value, axis, [(i, (i + by) % n) for i in range(n)])  8.67 us
    pallas_call x12, Pallas kernels, call(): pl.pallas_call(kernel, out_shape=[jax.ShapeDtypeStruct((s, 128), F32) if...  7.62 us
    ppermute x8, waiting for transfers between devices, swap(): return lax.ppermute(value, axis, pairs)  6.51 us
    ppermute x6, waiting for transfers between devices, shift(): return lax.ppermute(value, axis, [(i, (i + by) % n) for i in range(n)])  5.6 us
  transfers between devices with their start and end apart: 23, of which 12 were waited for; matrix products, arithmetic and copies ran while one was open for 0% of the time, Pallas kernels for 1%

profile of v4, /device:TPU:0, one launch (start us, length us, event | category | flops | bytes accessed | tf_op | source)
XLA Modules:
  0.0 75.3 jit_solution(4076072261788358488)
XLA Ops:
  0.6 2.9 %shard_map.68 = (f32[384,128]{1,0:T(8,128)S(1)}, f32[192,128]{1,0:T(8,128)S(1)}, f32[192,128]{1,0:T(8,128)S(1)}, f32[48,128]{1,0:T(8,128)S(1)}, f32[48,128]{1,0:...) custom-call(s32[4]{0:T(128)} %partner_hbm.1, ...), custom_call_target="tpu_custom_call" | custom-call | tf_op jit(solution)/shard_map/pallas_call | solution.py:634
  3.7 5.6 %collective-permute-start.1 = (f32[192,128]{1,0:T(8,128)S(1)}, f32[192,128]{1,0:T(8,128)S(1)}, u32[]{:S(2)}, u32[]{:S(2)}) collective-permute-start(f32[192,128]{1,0:T(8,128)S(1)} %get-tuple-element.63), channel_id=1, source_target_pairs={{0,15},{1,2},{2,1},{3,4},{4,3},{5,6},{6,5},{7,8},{8,7},{9,10},{10,... | collective-permute-start | bytes 294920 | tf_op jit(solution)/shard_map/ppermute | solution.py:650
  9.3 3.9 %collective-permute-start.4 = (f32[96,128]{1,0:T(8,128)S(1)}, f32[96,128]{1,0:T(8,128)S(1)}, u32[]{:S(2)}, u32[]{:S(2)}) collective-permute-start(f32[96,128]{1,0:T(8,128)S(1)} %get-tuple-element.66), channel_id=1, source_target_pairs={{0,64},{16,80},{32,96},{48,112},{64,0},{80,16},{96,32},{112,48},{1... | collective-permute-start | bytes 147464 | tf_op jit(solution)/shard_map/ppermute | solution.py:660
  13.2 0.7 collective-permute-start.2
  13.8 1.5 %collective-permute-start.3 = (f32[48,128]{1,0:T(8,128)S(1)}, f32[48,128]{1,0:T(8,128)S(1)}, u32[]{:S(2)}, u32[]{:S(2)}) collective-permute-start(f32[48,128]{1,0:T(8,128)S(1)} %get-tuple-element.65), channel_id=1, source_target_pairs={{0,112},{16,32},{32,16},{48,64},{64,48},{80,96},{96,80},{112,0},{1... | collective-permute-start | bytes 73736 | tf_op jit(solution)/shard_map/ppermute | solution.py:650
  15.3 1.7 %collective-permute-done.2.x_a = f32[48,128]{1,0:T(8,128)S(1)} collective-permute-done((f32[48,128]{1,0:T(8,128)S(1)}, f32[48,128]{1,0:T(8,128)S(1)}, u32[]{:S(2)}, u32[]{:S(2)}) %collective-permute-start.2) | collective-permute-done | bytes 24608 | tf_op jit(solution)/shard_map/ppermute | solution.py:650
  17.0 2.8 %collective-permute-done.3.x_b = f32[48,128]{1,0:T(8,128)S(1)} collective-permute-done((f32[48,128]{1,0:T(8,128)S(1)}, f32[48,128]{1,0:T(8,128)S(1)}, u32[]{:S(2)}, u32[]{:S(2)}) %collective-permute-start.3) | collective-permute-done | bytes 24608 | tf_op jit(solution)/shard_map/ppermute | solution.py:650
  19.8 0.5 shard_map.69
  20.4 1.9 %collective-permute-start.6 = (f32[192,128]{1,0:T(8,128)S(1)}, f32[192,128]{1,0:T(8,128)S(1)}, u32[]{:S(2)}, u32[]{:S(2)}) collective-permute-start(f32[192,128]{1,0:T(8,128)S(1)} %get-tuple-element.72), channel_id=1, source_target_pairs={{0,15},{1,2},{2,1},{3,4},{4,3},{5,6},{6,5},{7,8},{8,7},{9,10},{10,... | collective-permute-start | bytes 294920 | tf_op jit(solution)/shard_map/ppermute | solution.py:650
  22.4 3.9 %collective-permute-start.8 = (f32[48,128]{1,0:T(8,128)S(1)}, f32[48,128]{1,0:T(8,128)S(1)}, u32[]{:S(2)}, u32[]{:S(2)}) collective-permute-start(f32[48,128]{1,0:T(8,128)S(1)} %get-tuple-element.74), channel_id=1, source_target_pairs={{0,112},{16,32},{32,16},{48,64},{64,48},{80,96},{96,80},{112,0},{1... | collective-permute-start | bytes 73736 | tf_op jit(solution)/shard_map/ppermute | solution.py:650
  26.3 2.1 %collective-permute-done.8.x_b = f32[48,128]{1,0:T(8,128)S(1)} collective-permute-done((f32[48,128]{1,0:T(8,128)S(1)}, f32[48,128]{1,0:T(8,128)S(1)}, u32[]{:S(2)}, u32[]{:S(2)}) %collective-permute-start.8) | collective-permute-done | bytes 24608 | tf_op jit(solution)/shard_map/ppermute | solution.py:650
  29.1 2.3 %collective-permute-start.10 = (f32[384,128]{1,0:T(8,128)S(1)}, f32[384,128]{1,0:T(8,128)S(1)}, u32[]{:S(2)}, u32[]{:S(2)}) collective-permute-start(f32[384,128]{1,0:T(8,128)S(1)} %get-tuple-element.79), channel_id=1, source_target_pairs={{0,64},{16,80},{32,96},{48,112},{64,0},{80,16},{96,32},{112,48},{1... | collective-permute-start | bytes 589832 | tf_op jit(solution)/shard_map/ppermute | solution.py:660
  31.5 2.2 %collective-permute-start.11 = (f32[192,128]{1,0:T(8,128)S(1)}, f32[192,128]{1,0:T(8,128)S(1)}, u32[]{:S(2)}, u32[]{:S(2)}) collective-permute-start(f32[192,128]{1,0:T(8,128)S(1)} %get-tuple-element.82), channel_id=1, source_target_pairs={{0,15},{1,0},{2,1},{3,2},{4,3},{5,4},{6,5},{7,6},{8,7},{9,8},{10,9... | collective-permute-start | bytes 294920 | tf_op jit(solution)/shard_map/ppermute | solution.py:655
  33.7 1.0 %collective-permute-start.12 = (f32[48,128]{1,0:T(8,128)S(1)}, f32[48,128]{1,0:T(8,128)S(1)}, u32[]{:S(2)}, u32[]{:S(2)}) collective-permute-start(f32[48,128]{1,0:T(8,128)S(1)} %get-tuple-element.83), channel_id=1, source_target_pairs={{0,112},{16,0},{32,16},{48,32},{64,48},{80,64},{96,80},{112,96},{1... | collective-permute-start | bytes 73736 | tf_op jit(solution)/shard_map/ppermute | solution.py:655
  34.8 2.4 %collective-permute-start.13 = (f32[48,128]{1,0:T(8,128)S(1)}, f32[48,128]{1,0:T(8,128)S(1)}, u32[]{:S(2)}, u32[]{:S(2)}) collective-permute-start(f32[48,128]{1,0:T(8,128)S(1)} %get-tuple-element.84), channel_id=1, source_target_pairs={{0,64},{16,80},{32,96},{48,112},{64,0},{80,16},{96,32},{112,48},{1... | collective-permute-start | bytes 73736 | tf_op jit(solution)/shard_map/ppermute | solution.py:660
  37.6 2.5 %collective-permute-done.13.r_m = f32[48,128]{1,0:T(8,128)S(1)} collective-permute-done((f32[48,128]{1,0:T(8,128)S(1)}, f32[48,128]{1,0:T(8,128)S(1)}, u32[]{:S(2)}, u32[]{:S(2)}) %collective-permute-start.13) | collective-permute-done | bytes 24608 | tf_op jit(solution)/shard_map/ppermute | solution.py:660
  40.4 2.5 %collective-permute-start.14 = (f32[192,128]{1,0:T(8,128)S(1)}, f32[192,128]{1,0:T(8,128)S(1)}, u32[]{:S(2)}, u32[]{:S(2)}) collective-permute-start(f32[192,128]{1,0:T(8,128)S(1)} %get-tuple-element.88), channel_id=1, source_target_pairs={{0,64},{16,80},{32,96},{48,112},{64,0},{80,16},{96,32},{112,48},{1... | collective-permute-start | bytes 294920 | tf_op jit(solution)/shard_map/ppermute | solution.py:660
  43.0 3.6 %collective-permute-done.14.rest_5_ = f32[192,128]{1,0:T(8,128)S(1)} collective-permute-done((f32[192,128]{1,0:T(8,128)S(1)}, f32[192,128]{1,0:T(8,128)S(1)}, u32[]{:S(2)}, u32[]{:S(2)}) %collective-permute-start.14) | collective-permute-done | bytes 98336 | tf_op jit(solution)/shard_map/ppermute | solution.py:660
  46.6 0.6 shard_map.74
  47.2 1.1 %collective-permute-start.16 = (f32[48,128]{1,0:T(8,128)S(1)}, f32[48,128]{1,0:T(8,128)S(1)}, u32[]{:S(2)}, u32[]{:S(2)}) collective-permute-start(f32[48,128]{1,0:T(8,128)S(1)} %get-tuple-element.95), channel_id=1, source_target_pairs={{0,16},{16,32},{32,48},{48,64},{64,80},{80,96},{96,112},{112,0},{1... | collective-permute-start | bytes 73736 | tf_op jit(solution)/shard_map/ppermute | solution.py:655
  48.3 1.5 %collective-permute-start.17 = (f32[48,128]{1,0:T(8,128)S(1)}, f32[48,128]{1,0:T(8,128)S(1)}, u32[]{:S(2)}, u32[]{:S(2)}) collective-permute-start(f32[48,128]{1,0:T(8,128)S(1)} %get-tuple-element.96), channel_id=1, source_target_pairs={{0,64},{16,80},{32,96},{48,112},{64,0},{80,16},{96,32},{112,48},{1... | collective-permute-start | bytes 73736 | tf_op jit(solution)/shard_map/ppermute | solution.py:660
  49.8 3.5 %collective-permute-done.16.b_x = f32[48,128]{1,0:T(8,128)S(1)} collective-permute-done((f32[48,128]{1,0:T(8,128)S(1)}, f32[48,128]{1,0:T(8,128)S(1)}, u32[]{:S(2)}, u32[]{:S(2)}) %collective-permute-start.16) | collective-permute-done | bytes 24608 | tf_op jit(solution)/shard_map/ppermute | solution.py:655
  53.6 1.3 %collective-permute-done.15.b_t = f32[192,128]{1,0:T(8,128)S(1)} collective-permute-done((f32[192,128]{1,0:T(8,128)S(1)}, f32[192,128]{1,0:T(8,128)S(1)}, u32[]{:S(2)}, u32[]{:S(2)}) %collective-permute-start.15) | collective-permute-done | bytes 98336 | tf_op jit(solution)/shard_map/ppermute | solution.py:655
  55.6 2.5 %collective-permute-start.18 = (f32[384,128]{1,0:T(8,128)S(1)}, f32[384,128]{1,0:T(8,128)S(1)}, u32[]{:S(2)}, u32[]{:S(2)}) collective-permute-start(f32[384,128]{1,0:T(8,128)S(1)} %get-tuple-element.100), channel_id=1, source_target_pairs={{0,64},{16,80},{32,96},{48,112},{64,0},{80,16},{96,32},{112,48},{1... | collective-permute-start | bytes 589832 | tf_op jit(solution)/shard_map/ppermute | solution.py:660
  58.1 2.0 %collective-permute-start.19 = (f32[192,128]{1,0:T(8,128)S(1)}, f32[192,128]{1,0:T(8,128)S(1)}, u32[]{:S(2)}, u32[]{:S(2)}) collective-permute-start(f32[192,128]{1,0:T(8,128)S(1)} %get-tuple-element.103), channel_id=1, source_target_pairs={{0,15},{1,0},{2,1},{3,2},{4,3},{5,4},{6,5},{7,6},{8,7},{9,8},{10,9... | collective-permute-start | bytes 294920 | tf_op jit(solution)/shard_map/ppermute | solution.py:655
  60.1 2.2 %collective-permute-start.20 = (f32[48,128]{1,0:T(8,128)S(1)}, f32[48,128]{1,0:T(8,128)S(1)}, u32[]{:S(2)}, u32[]{:S(2)}) collective-permute-start(f32[48,128]{1,0:T(8,128)S(1)} %get-tuple-element.104), channel_id=1, source_target_pairs={{0,112},{16,0},{32,16},{48,32},{64,48},{80,64},{96,80},{112,96},{1... | collective-permute-start | bytes 73736 | tf_op jit(solution)/shard_map/ppermute | solution.py:655
  62.4 1.2 %collective-permute-start.21 = (f32[48,128]{1,0:T(8,128)S(1)}, f32[48,128]{1,0:T(8,128)S(1)}, u32[]{:S(2)}, u32[]{:S(2)}) collective-permute-start(f32[48,128]{1,0:T(8,128)S(1)} %get-tuple-element.105), channel_id=1, source_target_pairs={{0,64},{16,80},{32,96},{48,112},{64,0},{80,16},{96,32},{112,48},{1... | collective-permute-start | bytes 73736 | tf_op jit(solution)/shard_map/ppermute | solution.py:660
  63.5 0.5 collective-permute-done.20.r_x
  64.0 3.7 %collective-permute-done.21.r_m = f32[48,128]{1,0:T(8,128)S(1)} collective-permute-done((f32[48,128]{1,0:T(8,128)S(1)}, f32[48,128]{1,0:T(8,128)S(1)}, u32[]{:S(2)}, u32[]{:S(2)}) %collective-permute-start.21) | collective-permute-done | bytes 24608 | tf_op jit(solution)/shard_map/ppermute | solution.py:660
  68.0 1.2 %collective-permute-start.22 = (f32[192,128]{1,0:T(8,128)S(1)}, f32[192,128]{1,0:T(8,128)S(1)}, u32[]{:S(2)}, u32[]{:S(2)}) collective-permute-start(f32[192,128]{1,0:T(8,128)S(1)} %get-tuple-element.109), channel_id=1, source_target_pairs={{0,64},{16,80},{32,96},{48,112},{64,0},{80,16},{96,32},{112,48},{1... | collective-permute-start | bytes 294920 | tf_op jit(solution)/shard_map/ppermute | solution.py:660
  69.4 4.8 %collective-permute-done.22.rest_5_ = f32[192,128]{1,0:T(8,128)S(1)} collective-permute-done((f32[192,128]{1,0:T(8,128)S(1)}, f32[192,128]{1,0:T(8,128)S(1)}, u32[]{:S(2)}, u32[]{:S(2)}) %collective-permute-start.22) | collective-permute-done | bytes 98336 | tf_op jit(solution)/shard_map/ppermute | solution.py:660
  74.2 1.2 %shard_map.79 = (f32[1152,128]{1,0:T(8,128)}, f32[1152,128]{1,0:T(8,128)}) custom-call(s32[64,128]{1,0:T(8,128)S(1)} %get-tuple-element.57.info_ref, f32[1152,128]{1,0:T(8,128)S(1)} %get-tuple-element.89.u, f32[576,128]{1,0:T(8,128)S(1)} %get-tuple-element.90.p, f32[1152,128]{1,0:T(8,128)S(1)} %bitcast.20, f32[288,128]{1,0:T(8,128)S(1)} %get-tuple-element.101.u3, ...), custom_call_target="tpu_custom_call" | custom-call | tf_op jit(solution)/shard_map/pallas_call | solution.py:634
  (30 shorter events, 3.5 us)
Async XLA Ops:
  0.6 19.1 %copy-start = (f32[4,2,3,3,4,1,4,128]{7,6,5,4,3,2,1,0:T(4,128)S(1)}, f32[4,2,3,3,4,1,4,128]{7,6,5,4,3,2,1,0:T(4,128)}, u32[]{:S(2)}) copy-start(f32[4,2,3,3,4,1,4,128]{7,6,5,4,3,2,1,0:T(4,128)} %param.5) | copy-start | bytes 1769476
  3.6 16.2 %collective-permute-start = (f32[192,128]{1,0:T(8,128)S(1)}, f32[192,128]{1,0:T(8,128)S(1)}, u32[]{:S(2)}, u32[]{:S(2)}) collective-permute-start(f32[192,128]{1,0:T(8,128)S(1)} %get-tuple-element.62), channel_id=1, source_target_pairs={{0,1},{1,0},{2,3},{3,2},{4,5},{5,4},{6,7},{7,6},{8,9},{9,8},{10,11... | collective-permute-start | bytes 294920 | tf_op jit(solution)/shard_map/ppermute | solution.py:650
  3.7 16.1 %collective-permute-start.1 = (f32[192,128]{1,0:T(8,128)S(1)}, f32[192,128]{1,0:T(8,128)S(1)}, u32[]{:S(2)}, u32[]{:S(2)}) collective-permute-start(f32[192,128]{1,0:T(8,128)S(1)} %get-tuple-element.63), channel_id=1, source_target_pairs={{0,15},{1,2},{2,1},{3,4},{4,3},{5,6},{6,5},{7,8},{8,7},{9,10},{10,... | collective-permute-start | bytes 294920 | tf_op jit(solution)/shard_map/ppermute | solution.py:650
  9.3 10.5 %collective-permute-start.4 = (f32[96,128]{1,0:T(8,128)S(1)}, f32[96,128]{1,0:T(8,128)S(1)}, u32[]{:S(2)}, u32[]{:S(2)}) collective-permute-start(f32[96,128]{1,0:T(8,128)S(1)} %get-tuple-element.66), channel_id=1, source_target_pairs={{0,64},{16,80},{32,96},{48,112},{64,0},{80,16},{96,32},{112,48},{1... | collective-permute-start | bytes 147464 | tf_op jit(solution)/shard_map/ppermute | solution.py:660
  13.2 3.8 %collective-permute-start.2 = (f32[48,128]{1,0:T(8,128)S(1)}, f32[48,128]{1,0:T(8,128)S(1)}, u32[]{:S(2)}, u32[]{:S(2)}) collective-permute-start(f32[48,128]{1,0:T(8,128)S(1)} %get-tuple-element.64), channel_id=1, source_target_pairs={{0,16},{16,0},{32,48},{48,32},{64,80},{80,64},{96,112},{112,96},{1... | collective-permute-start | bytes 73736 | tf_op jit(solution)/shard_map/ppermute | solution.py:650
  13.8 5.9 %collective-permute-start.3 = (f32[48,128]{1,0:T(8,128)S(1)}, f32[48,128]{1,0:T(8,128)S(1)}, u32[]{:S(2)}, u32[]{:S(2)}) collective-permute-start(f32[48,128]{1,0:T(8,128)S(1)} %get-tuple-element.65), channel_id=1, source_target_pairs={{0,112},{16,32},{32,16},{48,64},{64,48},{80,96},{96,80},{112,0},{1... | collective-permute-start | bytes 73736 | tf_op jit(solution)/shard_map/ppermute | solution.py:650
  20.3 8.0 %collective-permute-start.5 = (f32[192,128]{1,0:T(8,128)S(1)}, f32[192,128]{1,0:T(8,128)S(1)}, u32[]{:S(2)}, u32[]{:S(2)}) collective-permute-start(f32[192,128]{1,0:T(8,128)S(1)} %get-tuple-element.71), channel_id=1, source_target_pairs={{0,1},{1,0},{2,3},{3,2},{4,5},{5,4},{6,7},{7,6},{8,9},{9,8},{10,11... | collective-permute-start | bytes 294920 | tf_op jit(solution)/shard_map/ppermute | solution.py:650
  20.4 8.0 %collective-permute-start.6 = (f32[192,128]{1,0:T(8,128)S(1)}, f32[192,128]{1,0:T(8,128)S(1)}, u32[]{:S(2)}, u32[]{:S(2)}) collective-permute-start(f32[192,128]{1,0:T(8,128)S(1)} %get-tuple-element.72), channel_id=1, source_target_pairs={{0,15},{1,2},{2,1},{3,4},{4,3},{5,6},{6,5},{7,8},{8,7},{9,10},{10,... | collective-permute-start | bytes 294920 | tf_op jit(solution)/shard_map/ppermute | solution.py:650
  22.4 6.0 %collective-permute-start.9 = (f32[96,128]{1,0:T(8,128)S(1)}, f32[96,128]{1,0:T(8,128)S(1)}, u32[]{:S(2)}, u32[]{:S(2)}) collective-permute-start(f32[96,128]{1,0:T(8,128)S(1)} %get-tuple-element.75), channel_id=1, source_target_pairs={{0,64},{16,80},{32,96},{48,112},{64,0},{80,16},{96,32},{112,48},{1... | collective-permute-start | bytes 147464 | tf_op jit(solution)/shard_map/ppermute | solution.py:660
  22.4 3.9 %collective-permute-start.7 = (f32[48,128]{1,0:T(8,128)S(1)}, f32[48,128]{1,0:T(8,128)S(1)}, u32[]{:S(2)}, u32[]{:S(2)}) collective-permute-start(f32[48,128]{1,0:T(8,128)S(1)} %get-tuple-element.73), channel_id=1, source_target_pairs={{0,16},{16,0},{32,48},{48,32},{64,80},{80,64},{96,112},{112,96},{1... | collective-permute-start | bytes 73736 | tf_op jit(solution)/shard_map/ppermute | solution.py:650
  22.4 6.0 %collective-permute-start.8 = (f32[48,128]{1,0:T(8,128)S(1)}, f32[48,128]{1,0:T(8,128)S(1)}, u32[]{:S(2)}, u32[]{:S(2)}) collective-permute-start(f32[48,128]{1,0:T(8,128)S(1)} %get-tuple-element.74), channel_id=1, source_target_pairs={{0,112},{16,32},{32,16},{48,64},{64,48},{80,96},{96,80},{112,0},{1... | collective-permute-start | bytes 73736 | tf_op jit(solution)/shard_map/ppermute | solution.py:650
  29.1 13.7 %collective-permute-start.10 = (f32[384,128]{1,0:T(8,128)S(1)}, f32[384,128]{1,0:T(8,128)S(1)}, u32[]{:S(2)}, u32[]{:S(2)}) collective-permute-start(f32[384,128]{1,0:T(8,128)S(1)} %get-tuple-element.79), channel_id=1, source_target_pairs={{0,64},{16,80},{32,96},{48,112},{64,0},{80,16},{96,32},{112,48},{1... | collective-permute-start | bytes 589832 | tf_op jit(solution)/shard_map/ppermute | solution.py:660
  31.5 8.6 %collective-permute-start.11 = (f32[192,128]{1,0:T(8,128)S(1)}, f32[192,128]{1,0:T(8,128)S(1)}, u32[]{:S(2)}, u32[]{:S(2)}) collective-permute-start(f32[192,128]{1,0:T(8,128)S(1)} %get-tuple-element.82), channel_id=1, source_target_pairs={{0,15},{1,0},{2,1},{3,2},{4,3},{5,4},{6,5},{7,6},{8,7},{9,8},{10,9... | collective-permute-start | bytes 294920 | tf_op jit(solution)/shard_map/ppermute | solution.py:655
  33.7 3.8 %collective-permute-start.12 = (f32[48,128]{1,0:T(8,128)S(1)}, f32[48,128]{1,0:T(8,128)S(1)}, u32[]{:S(2)}, u32[]{:S(2)}) collective-permute-start(f32[48,128]{1,0:T(8,128)S(1)} %get-tuple-element.83), channel_id=1, source_target_pairs={{0,112},{16,0},{32,16},{48,32},{64,48},{80,64},{96,80},{112,96},{1... | collective-permute-start | bytes 73736 | tf_op jit(solution)/shard_map/ppermute | solution.py:655
  34.8 8.1 %copy-start.1 = (f32[4,2,3,3,4,1,4,128]{7,6,5,4,3,2,1,0:T(4,128)S(1)}, f32[4,2,3,3,4,1,4,128]{7,6,5,4,3,2,1,0:T(4,128)}, u32[]{:S(2)}) copy-start(f32[4,2,3,3,4,1,4,128]{7,6,5,4,3,2,1,0:T(4,128)} %param.6) | copy-start | bytes 1769476
  34.8 5.3 %collective-permute-start.13 = (f32[48,128]{1,0:T(8,128)S(1)}, f32[48,128]{1,0:T(8,128)S(1)}, u32[]{:S(2)}, u32[]{:S(2)}) collective-permute-start(f32[48,128]{1,0:T(8,128)S(1)} %get-tuple-element.84), channel_id=1, source_target_pairs={{0,64},{16,80},{32,96},{48,112},{64,0},{80,16},{96,32},{112,48},{1... | collective-permute-start | bytes 73736 | tf_op jit(solution)/shard_map/ppermute | solution.py:660
  40.4 6.2 %collective-permute-start.14 = (f32[192,128]{1,0:T(8,128)S(1)}, f32[192,128]{1,0:T(8,128)S(1)}, u32[]{:S(2)}, u32[]{:S(2)}) collective-permute-start(f32[192,128]{1,0:T(8,128)S(1)} %get-tuple-element.88), channel_id=1, source_target_pairs={{0,64},{16,80},{32,96},{48,112},{64,0},{80,16},{96,32},{112,48},{1... | collective-permute-start | bytes 294920 | tf_op jit(solution)/shard_map/ppermute | solution.py:660
  47.2 7.7 %collective-permute-start.15 = (f32[192,128]{1,0:T(8,128)S(1)}, f32[192,128]{1,0:T(8,128)S(1)}, u32[]{:S(2)}, u32[]{:S(2)}) collective-permute-start(f32[192,128]{1,0:T(8,128)S(1)} %get-tuple-element.94), channel_id=1, source_target_pairs={{0,1},{1,2},{2,3},{3,4},{4,5},{5,6},{6,7},{7,8},{8,9},{9,10},{10,1... | collective-permute-start | bytes 294920 | tf_op jit(solution)/shard_map/ppermute | solution.py:655
  47.2 6.0 %collective-permute-start.16 = (f32[48,128]{1,0:T(8,128)S(1)}, f32[48,128]{1,0:T(8,128)S(1)}, u32[]{:S(2)}, u32[]{:S(2)}) collective-permute-start(f32[48,128]{1,0:T(8,128)S(1)} %get-tuple-element.95), channel_id=1, source_target_pairs={{0,16},{16,32},{32,48},{48,64},{64,80},{80,96},{96,112},{112,0},{1... | collective-permute-start | bytes 73736 | tf_op jit(solution)/shard_map/ppermute | solution.py:655
  48.3 5.3 %collective-permute-start.17 = (f32[48,128]{1,0:T(8,128)S(1)}, f32[48,128]{1,0:T(8,128)S(1)}, u32[]{:S(2)}, u32[]{:S(2)}) collective-permute-start(f32[48,128]{1,0:T(8,128)S(1)} %get-tuple-element.96), channel_id=1, source_target_pairs={{0,64},{16,80},{32,96},{48,112},{64,0},{80,16},{96,32},{112,48},{1... | collective-permute-start | bytes 73736 | tf_op jit(solution)/shard_map/ppermute | solution.py:660
  55.6 13.6 %collective-permute-start.18 = (f32[384,128]{1,0:T(8,128)S(1)}, f32[384,128]{1,0:T(8,128)S(1)}, u32[]{:S(2)}, u32[]{:S(2)}) collective-permute-start(f32[384,128]{1,0:T(8,128)S(1)} %get-tuple-element.100), channel_id=1, source_target_pairs={{0,64},{16,80},{32,96},{48,112},{64,0},{80,16},{96,32},{112,48},{1... | collective-permute-start | bytes 589832 | tf_op jit(solution)/shard_map/ppermute | solution.py:660
  58.1 9.6 %collective-permute-start.19 = (f32[192,128]{1,0:T(8,128)S(1)}, f32[192,128]{1,0:T(8,128)S(1)}, u32[]{:S(2)}, u32[]{:S(2)}) collective-permute-start(f32[192,128]{1,0:T(8,128)S(1)} %get-tuple-element.103), channel_id=1, source_target_pairs={{0,15},{1,0},{2,1},{3,2},{4,3},{5,4},{6,5},{7,6},{8,7},{9,8},{10,9... | collective-permute-start | bytes 294920 | tf_op jit(solution)/shard_map/ppermute | solution.py:655
  60.1 3.8 %collective-permute-start.20 = (f32[48,128]{1,0:T(8,128)S(1)}, f32[48,128]{1,0:T(8,128)S(1)}, u32[]{:S(2)}, u32[]{:S(2)}) collective-permute-start(f32[48,128]{1,0:T(8,128)S(1)} %get-tuple-element.104), channel_id=1, source_target_pairs={{0,112},{16,0},{32,16},{48,32},{64,48},{80,64},{96,80},{112,96},{1... | collective-permute-start | bytes 73736 | tf_op jit(solution)/shard_map/ppermute | solution.py:655
  62.4 5.3 %collective-permute-start.21 = (f32[48,128]{1,0:T(8,128)S(1)}, f32[48,128]{1,0:T(8,128)S(1)}, u32[]{:S(2)}, u32[]{:S(2)}) collective-permute-start(f32[48,128]{1,0:T(8,128)S(1)} %get-tuple-element.105), channel_id=1, source_target_pairs={{0,64},{16,80},{32,96},{48,112},{64,0},{80,16},{96,32},{112,48},{1... | collective-permute-start | bytes 73736 | tf_op jit(solution)/shard_map/ppermute | solution.py:660
  68.0 6.2 %collective-permute-start.22 = (f32[192,128]{1,0:T(8,128)S(1)}, f32[192,128]{1,0:T(8,128)S(1)}, u32[]{:S(2)}, u32[]{:S(2)}) collective-permute-start(f32[192,128]{1,0:T(8,128)S(1)} %get-tuple-element.109), channel_id=1, source_target_pairs={{0,64},{16,80},{32,96},{48,112},{64,0},{80,16},{96,32},{112,48},{1... | collective-permute-start | bytes 294920 | tf_op jit(solution)/shard_map/ppermute | solution.py:660

commit v5 on v4

--- a/solution.py
+++ b/solution.py
@@ -191,31 +191,16 @@
         send_rows(mirror, 12 + k, q2, k, info, 3)
 
 
-def dirac(psi_ref, u_ref, arrived, q0, q2, q3, scratch, out_ref, w_ref):
-    ahead_t, behind_t, ahead_x, behind_x, ahead_m, behind_m = arrived
-    a0, b0, fa, fb = scratch
+def dirac_rest(psi_ref, u_ref, ahead_t, behind_t, ahead_m, behind_m, q2, q3, fa, fb, acc_ref, w_ref):
     for k in range(12):
-        a0[k * HALO + 16 : k * HALO + 20, :] = ahead_x(k)
-        b0[k * HALO : k * HALO + 4, :] = behind_x(k)
-        b0[k * HALO + 4 : k * HALO + 20, :] = q0[k * ROWS : k * ROWS + 16, :]
         fa[pl.ds(k * ROWS + 3, 4, stride=4), :] = ahead_m(k)
         fb[pl.ds(k * ROWS, 4, stride=4), :] = behind_m(k)
-    for h in range(2):
-        v = project(spinor(psi_ref, h), 0, 1)
-        for t in range(2):
-            for c in range(3):
-                for part in range(2):
-                    k = half_index(part, t, c)
-                    a0[k * HALO + 8 * h : k * HALO + 8 * h + 8, :] = v[t][c][part]
     x2 = row_in_pair()
     for h in range(2):
         psi = spinor(psi_ref, h)
         acc = None
-        for mu in range(4):
-            if mu == 0:
-                ahead = get_half(lambda k: a0[k * HALO + 8 * h + 4 : k * HALO + 8 * h + 12, :])
-                behind = get_half(lambda k: b0[k * HALO + 8 * h : k * HALO + 8 * h + 8, :])
-            elif mu == 1:
+        for mu in (1, 2, 3):
+            if mu == 1:
                 ahead = get_half(lambda k: ahead_t(k, h))
                 behind = get_half(lambda k: behind_t(k, h))
             elif mu == 2:
@@ -226,39 +211,97 @@
             else:
                 ahead = map_half(lambda r: pltpu.roll(r, 127, 1), project(psi, 3, 1))
                 behind = get_half(lambda k: pltpu.roll(ld(q3, k, h), 1, 1))
-            w = mat_half(matrix(u_ref, mu, h), ahead)
-            if w_ref is not None:
-                put_half(w_ref, h, w, mu * 12)
-            total = map_half(lambda a, b: a + b, w, behind)
-            delta = map_half(lambda a, b: a - b, w, behind)
-            source, coef = GAMMA[mu]
-            if acc is None:
-                zero = jnp.zeros((8, 128), F32)
-                acc = [total[0], total[1]] + [
-                    [add_unit((zero, zero), delta[source[s]][c], coef[s], 1) for c in range(3)] for s in (2, 3)
-                ]
-            else:
-                for s in range(2):
-                    acc[s] = [cadd(acc[s][c], total[s][c]) for c in range(3)]
-                for s in (2, 3):
-                    acc[s] = [add_unit(acc[s][c], delta[source[s]][c], coef[s], 1) for c in range(3)]
+            acc = add_direction(acc, u_ref, w_ref, mu, h, ahead, behind)
+        for s in range(4):
+            for c in range(3):
+                for part in range(2):
+                    st(acc_ref, part * 12 + c * 4 + s, h, acc[s][c][part])
+
+
+def add_direction(acc, u_ref, w_ref, mu, h, ahead, behind):
+    w = mat_half(matrix(u_ref, mu, h), ahead)
+    if w_ref is not None:
+        put_half(w_ref, h, w, (mu - 1) * 12 if mu else 0)
+    total = map_half(lambda a, b: a + b, w, behind)
+    delta = map_half(lambda a, b: a - b, w, behind)
+    source, coef = GAMMA[mu]
+    if acc is None:
+        zero = jnp.zeros((8, 128), F32)
+        acc = [[(zero, zero)] * 3] * 4
+    upper = [[cadd(acc[s][c], total[s][c]) for c in range(3)] for s in range(2)]
+    lower = [[add_unit(acc[s][c], delta[source[s]][c], coef[s], 1) for c in range(3)] for s in (2, 3)]
+    return upper + lower
+
+
+def dirac_rows(psi_ref, u_ref, acc_ref, ahead_x, behind_x, q0, a0, b0, out_ref, w_ref):
+    for k in range(12):
+        a0[k * HALO + 16 : k * HALO + 20, :] = ahead_x(k)
+        b0[k * HALO : k * HALO + 4, :] = behind_x(k)
+        b0[k * HALO + 4 : k * HALO + 20, :] = q0[k * ROWS : k * ROWS + 16, :]
+    for h in range(2):
+        v = project(spinor(psi_ref, h), 0, 1)
+        for t in range(2):
+            for c in range(3):
+                for part in range(2):
+                    k = half_index(part, t, c)
+                    a0[k * HALO + 8 * h : k * HALO + 8 * h + 8, :] = v[t][c][part]
+    for h in range(2):
+        psi = spinor(psi_ref, h)
+        ahead = get_half(lambda k: a0[k * HALO + 8 * h + 4 : k * HALO + 8 * h + 12, :])
+        behind = get_half(lambda k: b0[k * HALO + 8 * h : k * HALO + 8 * h + 8, :])
+        acc = add_direction(spinor(acc_ref, h), u_ref, w_ref, 0, h, ahead, behind)
         for s in range(4):
             for c in range(3):
                 for part in range(2):
                     st(out_ref, part * 12 + c * 4 + s, h, psi[s][c][part] - HOPPING * acc[s][c][part])
 
 
-def arrived_swap(info, t_a, t_b, x_a, x_b, mirror):
-    def rows(ref, k):
-        return ref[k * 4 : k * 4 + 4, :]
-
-    return (
+def rows_of(ref, k):
+    return ref[k * 4 : k * 4 + 4, :]
+
+
+def rest_kernel(info_ref, psi, u, q2, q3, t_a, t_b, mirror, acc, *scratch, w=None):
+    info = Info(info_ref)
+    dirac_rest(
+        psi,
+        u,
         lambda k, h: jnp.where(info.even_t, ld(t_a, k, h), ld(t_b, k, h)),
         lambda k, h: jnp.where(info.even_t, ld(t_b, k, h), ld(t_a, k, h)),
-        lambda k: jnp.where(info.even_x, rows(x_a, k), rows(x_b, k)),
-        lambda k: jnp.where(info.even_x, rows(x_b, k), rows(x_a, k)),
-        lambda k: rows(mirror, k),
-        lambda k: rows(mirror, 12 + k),
+        lambda k: rows_of(mirror, k),
+        lambda k: rows_of(mirror, 12 + k),
+        q2,
+        q3,
+        *scratch,
+        acc,
+        w,
+    )
+
+
+def rest_w_kernel(info_ref, psi, u, q2, q3, t_a, t_b, mirror, acc, w, *scratch):
+    rest_kernel(info_ref, psi, u, q2, q3, t_a, t_b, mirror, acc, *scratch, w=w)
+
+
+def rest2_kernel(info_ref, psi, u, q2, q3, t_a, t_b, mirror, b_t, b_m, acc, w, *scratch):
+    info = Info(info_ref)
+    dirac_rest(
+        psi,
+        u,
+        lambda k, h: jnp.where(info.even_t, ld(t_a, k, h), ld(t_b, k, h)),
+        lambda k, h: ld(b_t, k, h),
+        lambda k: rows_of(mirror, k),
+        lambda k: rows_of(b_m, k),
+        q2,
+        q3,
+        *scratch,
+        acc,
+        w,
+    )
+
+
+def arrived_rows(info, x_a, x_b):
+    return (
+        lambda k: jnp.where(info.even_x, rows_of(x_a, k), rows_of(x_b, k)),
+        lambda k: jnp.where(info.even_x, rows_of(x_b, k), rows_of(x_a, k)),
     )
 
 
@@ -315,11 +358,10 @@
     send_both(psi, u, info, t_a, t_b, x_a, x_b, mirror, q0, q2, q3, h0, h2)
 
 
-def phi_kernel(info_ref, psi, u, q0, q2, q3, t_a, t_b, x_a, x_b, mirror, *rest):
-    phi, o_ta, o_tb, o_xa, o_xb, o_m, o_q0, o_q2, o_q3, a0, b0, fa, fb, h0, h2 = rest
-    info = Info(info_ref)
-    arrived = arrived_swap(info, t_a, t_b, x_a, x_b, mirror)
-    dirac(psi, u, arrived, q0, q2, q3, (a0, b0, fa, fb), phi, None)
+def phi_kernel(info_ref, psi, u, acc, q0, x_a, x_b, *rest):
+    phi, o_ta, o_tb, o_xa, o_xb, o_m, o_q0, o_q2, o_q3, a0, b0, h0, h2 = rest
+    info = Info(info_ref)
+    dirac_rows(psi, u, acc, *arrived_rows(info, x_a, x_b), q0, a0, b0, phi, None)
     send_both(phi, u, info, o_ta, o_tb, o_xa, o_xb, o_m, o_q0, o_q2, o_q3, h0, h2)
 
 
@@ -339,22 +381,18 @@
         send_rows(o_m, k, h2, k, info, 0)
 
 
-def response_kernel(info_ref, phi, u, q0, q2, q3, t_a, t_b, x_a, x_b, mirror, *rest):
-    y, w, o_t, o_x, o_m, a0, b0, fa, fb, h2 = rest
-    info = Info(info_ref)
-    arrived = arrived_swap(info, t_a, t_b, x_a, x_b, mirror)
-    dirac(phi, u, arrived, q0, q2, q3, (a0, b0, fa, fb), y, w)
+def response_kernel(info_ref, phi, u, acc, q0, x_a, x_b, *rest):
+    y, w, o_t, o_x, o_m, a0, b0, h2 = rest
+    info = Info(info_ref)
+    dirac_rows(phi, u, acc, *arrived_rows(info, x_a, x_b), q0, a0, b0, y, w)
     send_response(y, info, o_t, o_x, o_m, h2)
 
 
-def response2_kernel(info_ref, phi, u, q0, q2, q3, t_a, t_b, x_a, x_b, mirror, b_t, b_x, b_m, *rest):
-    y, w, o_t, o_x, o_m, a0, b0, fa, fb, h2 = rest
-    info = Info(info_ref)
-    arrived = list(arrived_swap(info, t_a, t_b, x_a, x_b, mirror))
-    arrived[1] = lambda k, h: ld(b_t, k, h)
-    arrived[3] = lambda k: b_x[k * 4 : k * 4 + 4, :]
-    arrived[5] = lambda k: b_m[k * 4 : k * 4 + 4, :]
-    dirac(phi, u, arrived, q0, q2, q3, (a0, b0, fa, fb), y, w)
+def response2_kernel(info_ref, phi, u, acc, q0, x_a, x_b, b_x, *rest):
+    y, w, o_t, o_x, o_m, a0, b0, h2 = rest
+    info = Info(info_ref)
+    ahead_x = arrived_rows(info, x_a, x_b)[0]
+    dirac_rows(phi, u, acc, ahead_x, lambda k: rows_of(b_x, k), q0, a0, b0, y, w)
     send_response(y, info, o_t, o_x, o_m, h2)
 
 
@@ -383,12 +421,14 @@
     ysp = [[(at(y, c * 4 + s), at(y, 12 + c * 4 + s)) for c in range(3)] for s in range(4)]
     psp = [[(at(phi, c * 4 + s), at(phi, 12 + c * 4 + s)) for c in range(3)] for s in range(4)]
     link = [[(at(u, mu * 18 + i * 3 + j), at(u, mu * 18 + 9 + i * 3 + j)) for j in range(3)] for i in range(3)]
-    left = mat_half(link, x(ysp)) + get_half(lambda k: at(w, mu * 12 + k))
+    ref, base = (w[1], (mu - 1) * 12) if mu else (w[0], 0)
+    left = mat_half(link, x(ysp)) + get_half(lambda k: at(ref, base + k))
     right = project(psp, mu, -1) + project(ysp, mu, 1)
     return force_values(left, right)
 
 
-def early_force_kernel(info_ref, phi, u, y, w, force, sent, a0):
+def early_force_kernel(info_ref, phi, u, y, w0, w1, force, sent, a0):
+    w = (w0, w1)
     info = Info(info_ref)
     nothing = jnp.zeros((4, 128), F32)
     for k in range(12):
@@ -424,7 +464,8 @@
         st(dst, base, h, jnp.where(first, low, value))
 
 
-def late_force_kernel(info_ref, phi, u, y, w, r_t, r_x, r_m, f_t, f_x, f_m, sent):
+def late_force_kernel(info_ref, phi, u, y, w0, w1, r_t, r_x, r_m, f_t, f_x, f_m, sent):
+    w = (w0, w1)
     info = Info(info_ref)
     for h in range(2):
         arrived = get_half(lambda k: ld(r_t, k, h))
@@ -695,11 +736,11 @@
 
 
 def all_forces(masks, phi, u, y, w, o_t, o_x, o_m):
-    early, sent = call(early_force_kernel, (masks, phi, u, y, w), [24 * ROWS, 24 * ROWS], [12 * HALO])
+    early, sent = call(early_force_kernel, (masks, phi, u, y, *w), [24 * ROWS, 24 * ROWS], [12 * HALO])
     got = exchange(BACK_ORDER, back_t=o_t, back_x=o_x, mirror=o_m, early=sent)
     f_t, f_x, f_m, sent = call(
         late_force_kernel,
-        (masks, phi, u, y, w, got["back_t"], got["back_x"], got["mirror"]),
+        (masks, phi, u, y, *w, got["back_t"], got["back_x"], got["mirror"]),
         [8 * ROWS, 8 * ROWS, 8 * ROWS, 12 * ROWS],
         [],
     )
@@ -719,7 +760,7 @@
     index = noise_index.reshape(ROWS, 128)
     messages = [FULL, FULL, FACE, FACE, 2 * FACE]
     local = [FULL, FULL, FULL]
-    halo = [12 * HALO, 12 * HALO, FULL, FULL]
+    halo = [12 * HALO, 12 * HALO]
     spin = 24 * ROWS
 
     psi, *rest, masks = call(
@@ -740,12 +781,17 @@
         12,
         from_hbm=True,
     )
-    arrived = swap_exchange(*rest[:5])
-    phi, *rest = call(phi_kernel, (masks, psi, u, *rest[5:], *arrived), [spin] + messages + local, halo + [FULL, FULL])
-    arrived = swap_exchange(*rest[:5])
-    y, w, o_t, o_x, o_m = call(
-        response_kernel, (masks, phi, u, *rest[5:], *arrived), [spin, 4 * FULL, FULL, FACE, FACE], halo + [FULL]
-    )
+    t_a, t_b, x_a, x_b, m = swap_exchange(*rest[:5])
+    q0, q2, q3 = rest[5:]
+    (acc,) = call(rest_kernel, (masks, psi, u, q2, q3, t_a, t_b, m), [spin], [FULL, FULL])
+    phi, *rest = call(phi_kernel, (masks, psi, u, acc, q0, x_a, x_b), [spin] + messages + local, halo + [FULL, FULL])
+    t_a, t_b, x_a, x_b, m = swap_exchange(*rest[:5])
+    q0, q2, q3 = rest[5:]
+    acc, w1 = call(rest_w_kernel, (masks, phi, u, q2, q3, t_a, t_b, m), [spin, 3 * FULL], [FULL, FULL])
+    y, w0, o_t, o_x, o_m = call(
+        response_kernel, (masks, phi, u, acc, q0, x_a, x_b), [spin, FULL, FULL, FACE, FACE], halo + [FULL]
+    )
+    w = (w0, w1)
     forces = all_forces(masks, phi, u, y, w, o_t, o_x, o_m)
     u3, p3, q3 = call(early_update_kernel, (phi, u, p, *forces[:2]), [18 * ROWS, 9 * ROWS, FULL], [])
     u, p1, o_t, o_x, o_m, q0, q2 = call(
@@ -754,12 +800,12 @@
         [72 * ROWS, 36 * ROWS, FULL, FACE, FACE, FULL, FULL],
         [8 * ROWS, 8 * ROWS],
     )
-    y, w, o_t, o_x, o_m = call(
-        response2_kernel,
-        (masks, phi, u, q0, q2, q3, *arrived, *on_exchange(o_t, o_x, o_m)),
-        [spin, 4 * FULL, FULL, FACE, FACE],
-        halo + [FULL],
-    )
+    b_t, b_x, b_m = on_exchange(o_t, o_x, o_m)
+    acc, w1 = call(rest2_kernel, (masks, phi, u, q2, q3, t_a, t_b, m, b_t, b_m), [spin, 3 * FULL], [FULL, FULL])
+    y, w0, o_t, o_x, o_m = call(
+        response2_kernel, (masks, phi, u, acc, q0, x_a, x_b, b_x), [spin, FULL, FULL, FACE, FACE], halo + [FULL]
+    )
+    w = (w0, w1)
     forces = all_forces(masks, phi, u, y, w, o_t, o_x, o_m)
     u3, p3 = call(early_last_kernel, (u, p1, p, *forces[:2]), [18 * ROWS, 18 * ROWS], [])
     new_u, new_p = call(

time: 75.5 us -> 74.1 us (0.981)
  waiting for transfers between devices: 27.1 us -> 25.9 us
    ppermute x9, waiting for transfers between devices: 15 us -> 17.6 us  [mirror_swap(): return lax.ppermute(value, 'xd', [(i, i ^ n // 2) for i in range(n)])]
    ppermute x8, waiting for transfers between devices: 6.51 us -> 4.39 us  [swap(): return lax.ppermute(value, axis, pairs)]
    ppermute x6, starting transfers between devices: 8.67 us -> 6.82 us  [shift(): return lax.ppermute(value, axis, [(i, (i + by) % n) for i in range(n)])]
    ppermute x9, starting transfers between devices: 17.4 us -> 19.2 us  [mirror_swap(): return lax.ppermute(value, 'xd', [(i, i ^ n // 2) for i in range(n)])]
    ppermute x6, waiting for transfers between devices: 5.6 us -> 3.84 us  [shift(): return lax.ppermute(value, axis, [(i, (i + by) % n) for i in range(n)])]
    pallas_call x12 -> x15, Pallas kernels: 7.62 us -> 7.54 us  [call(): pl.pallas_call(kernel, out_shape=[jax.ShapeDtypeStruct((s, 128), F32) if...]
  transfers between devices with their start and end apart: 23 -> 23, of which waited for: 12 -> 14; matrix products, arithmetic and copies ran while one was open for 0% -> 0% of each run, Pallas kernels for 1% -> 2%
where the time goes in v5:
time: 74.1 us; the launch traced here: 74 us
  starting transfers between devices  39.8 us (54%)
  waiting for transfers between devices  25.9 us (35%)
  Pallas kernels  7.54 us (10%)
  between operations  0.76 us (1%)
    ppermute x9, starting transfers between devices, mirror_swap(): return lax.ppermute(value, 'xd', [(i, i ^ n // 2) for i in range(n)])  19.2 us
    ppermute x9, waiting for transfers between devices, mirror_swap(): return lax.ppermute(value, 'xd', [(i, i ^ n // 2) for i in range(n)])  17.6 us
    ppermute x8, starting transfers between devices, swap(): return lax.ppermute(value, axis, pairs)  13.8 us
    pallas_call x15, Pallas kernels, call(): pl.pallas_call(kernel, out_shape=[jax.ShapeDtypeStruct((s, 128), F32) if...  7.54 us
    ppermute x6, starting transfers between devices, shift(): return lax.ppermute(value, axis, [(i, (i + by) % n) for i in range(n)])  6.82 us
    ppermute x8, waiting for transfers between devices, swap(): return lax.ppermute(value, axis, pairs)  4.39 us
    ppermute x6, waiting for transfers between devices, shift(): return lax.ppermute(value, axis, [(i, (i + by) % n) for i in range(n)])  3.84 us
  transfers between devices with their start and end apart: 23, of which 14 were waited for; matrix products, arithmetic and copies ran while one was open for 0% of the time, Pallas kernels for 2%

profile of v5, /device:TPU:0, one launch (start us, length us, event | category | flops | bytes accessed | tf_op | source)
XLA Modules:
  0.0 74.0 jit_solution(18063770618230779310)
XLA Ops:
  0.6 2.9 %shard_map.68 = (f32[384,128]{1,0:T(8,128)S(1)}, f32[192,128]{1,0:T(8,128)S(1)}, f32[192,128]{1,0:T(8,128)S(1)}, f32[48,128]{1,0:T(8,128)S(1)}, f32[48,128]{1,0:...) custom-call(s32[4]{0:T(128)} %partner_hbm.1, ...), custom_call_target="tpu_custom_call" | custom-call | tf_op jit(solution)/shard_map/pallas_call | solution.py:675
  3.7 5.6 %collective-permute-start.1 = (f32[192,128]{1,0:T(8,128)S(1)}, f32[192,128]{1,0:T(8,128)S(1)}, u32[]{:S(2)}, u32[]{:S(2)}) collective-permute-start(f32[192,128]{1,0:T(8,128)S(1)} %get-tuple-element.66), channel_id=1, source_target_pairs={{0,15},{1,2},{2,1},{3,4},{4,3},{5,6},{6,5},{7,8},{8,7},{9,10},{10,... | collective-permute-start | bytes 294920 | tf_op jit(solution)/shard_map/ppermute | solution.py:691
  9.3 3.9 %collective-permute-start.2 = (f32[96,128]{1,0:T(8,128)S(1)}, f32[96,128]{1,0:T(8,128)S(1)}, u32[]{:S(2)}, u32[]{:S(2)}) collective-permute-start(f32[96,128]{1,0:T(8,128)S(1)} %get-tuple-element.67), channel_id=1, source_target_pairs={{0,64},{16,80},{32,96},{48,112},{64,0},{80,16},{96,32},{112,48},{1... | collective-permute-start | bytes 147464 | tf_op jit(solution)/shard_map/ppermute | solution.py:701
  13.2 0.7 collective-permute-start.3
  13.8 1.5 %collective-permute-start.4 = (f32[48,128]{1,0:T(8,128)S(1)}, f32[48,128]{1,0:T(8,128)S(1)}, u32[]{:S(2)}, u32[]{:S(2)}) collective-permute-start(f32[48,128]{1,0:T(8,128)S(1)} %get-tuple-element.70), channel_id=1, source_target_pairs={{0,112},{16,32},{32,16},{48,64},{64,48},{80,96},{96,80},{112,0},{1... | collective-permute-start | bytes 73736 | tf_op jit(solution)/shard_map/ppermute | solution.py:691
  15.7 1.3 %collective-permute-done.3.x_a = f32[48,128]{1,0:T(8,128)S(1)} collective-permute-done((f32[48,128]{1,0:T(8,128)S(1)}, f32[48,128]{1,0:T(8,128)S(1)}, u32[]{:S(2)}, u32[]{:S(2)}) %collective-permute-start.3) | collective-permute-done | bytes 24608 | tf_op jit(solution)/shard_map/ppermute | solution.py:691
  17.0 2.8 %collective-permute-done.4.x_b = f32[48,128]{1,0:T(8,128)S(1)} collective-permute-done((f32[48,128]{1,0:T(8,128)S(1)}, f32[48,128]{1,0:T(8,128)S(1)}, u32[]{:S(2)}, u32[]{:S(2)}) %collective-permute-start.4) | collective-permute-done | bytes 24608 | tf_op jit(solution)/shard_map/ppermute | solution.py:691
  20.2 1.9 %collective-permute-start.6 = (f32[192,128]{1,0:T(8,128)S(1)}, f32[192,128]{1,0:T(8,128)S(1)}, u32[]{:S(2)}, u32[]{:S(2)}) collective-permute-start(f32[192,128]{1,0:T(8,128)S(1)} %get-tuple-element.75), channel_id=1, source_target_pairs={{0,15},{1,2},{2,1},{3,4},{4,3},{5,6},{6,5},{7,8},{8,7},{9,10},{10,... | collective-permute-start | bytes 294920 | tf_op jit(solution)/shard_map/ppermute | solution.py:691
  22.3 3.8 %collective-permute-start.9 = (f32[48,128]{1,0:T(8,128)S(1)}, f32[48,128]{1,0:T(8,128)S(1)}, u32[]{:S(2)}, u32[]{:S(2)}) collective-permute-start(f32[48,128]{1,0:T(8,128)S(1)} %get-tuple-element.80), channel_id=1, source_target_pairs={{0,112},{16,32},{32,16},{48,64},{64,48},{80,96},{96,80},{112,0},{1... | collective-permute-start | bytes 73736 | tf_op jit(solution)/shard_map/ppermute | solution.py:691
  26.1 1.7 %collective-permute-done.7.mirror = f32[96,128]{1,0:T(8,128)S(1)} collective-permute-done((f32[96,128]{1,0:T(8,128)S(1)}, f32[96,128]{1,0:T(8,128)S(1)}, u32[]{:S(2)}, u32[]{:S(2)}) %collective-permute-start.7) | collective-permute-done | bytes 49184 | tf_op jit(solution)/shard_map/ppermute | solution.py:701
  28.8 2.2 %collective-permute-start.10 = (f32[384,128]{1,0:T(8,128)S(1)}, f32[384,128]{1,0:T(8,128)S(1)}, u32[]{:S(2)}, u32[]{:S(2)}) collective-permute-start(f32[384,128]{1,0:T(8,128)S(1)} %get-tuple-element.85), channel_id=1, source_target_pairs={{0,64},{16,80},{32,96},{48,112},{64,0},{80,16},{96,32},{112,48},{1... | collective-permute-start | bytes 589832 | tf_op jit(solution)/shard_map/ppermute | solution.py:701
  31.0 2.2 %collective-permute-start.11 = (f32[192,128]{1,0:T(8,128)S(1)}, f32[192,128]{1,0:T(8,128)S(1)}, u32[]{:S(2)}, u32[]{:S(2)}) collective-permute-start(f32[192,128]{1,0:T(8,128)S(1)} %get-tuple-element.88), channel_id=1, source_target_pairs={{0,15},{1,0},{2,1},{3,2},{4,3},{5,4},{6,5},{7,6},{8,7},{9,8},{10,9... | collective-permute-start | bytes 294920 | tf_op jit(solution)/shard_map/ppermute | solution.py:696
  33.2 1.0 %collective-permute-start.12 = (f32[48,128]{1,0:T(8,128)S(1)}, f32[48,128]{1,0:T(8,128)S(1)}, u32[]{:S(2)}, u32[]{:S(2)}) collective-permute-start(f32[48,128]{1,0:T(8,128)S(1)} %get-tuple-element.89), channel_id=1, source_target_pairs={{0,112},{16,0},{32,16},{48,32},{64,48},{80,64},{96,80},{112,96},{1... | collective-permute-start | bytes 73736 | tf_op jit(solution)/shard_map/ppermute | solution.py:696
  34.3 2.4 %collective-permute-start.13 = (f32[48,128]{1,0:T(8,128)S(1)}, f32[48,128]{1,0:T(8,128)S(1)}, u32[]{:S(2)}, u32[]{:S(2)}) collective-permute-start(f32[48,128]{1,0:T(8,128)S(1)} %get-tuple-element.90), channel_id=1, source_target_pairs={{0,64},{16,80},{32,96},{48,112},{64,0},{80,16},{96,32},{112,48},{1... | collective-permute-start | bytes 73736 | tf_op jit(solution)/shard_map/ppermute | solution.py:701
  36.7 0.4 collective-permute-done.12.r_x
  37.1 2.5 %collective-permute-done.13.r_m = f32[48,128]{1,0:T(8,128)S(1)} collective-permute-done((f32[48,128]{1,0:T(8,128)S(1)}, f32[48,128]{1,0:T(8,128)S(1)}, u32[]{:S(2)}, u32[]{:S(2)}) %collective-permute-start.13) | collective-permute-done | bytes 24608 | tf_op jit(solution)/shard_map/ppermute | solution.py:701
  39.9 2.5 %collective-permute-start.14 = (f32[192,128]{1,0:T(8,128)S(1)}, f32[192,128]{1,0:T(8,128)S(1)}, u32[]{:S(2)}, u32[]{:S(2)}) collective-permute-start(f32[192,128]{1,0:T(8,128)S(1)} %get-tuple-element.94), channel_id=1, source_target_pairs={{0,64},{16,80},{32,96},{48,112},{64,0},{80,16},{96,32},{112,48},{1... | collective-permute-start | bytes 294920 | tf_op jit(solution)/shard_map/ppermute | solution.py:701
  42.5 3.6 %collective-permute-done.14.rest_5_ = f32[192,128]{1,0:T(8,128)S(1)} collective-permute-done((f32[192,128]{1,0:T(8,128)S(1)}, f32[192,128]{1,0:T(8,128)S(1)}, u32[]{:S(2)}, u32[]{:S(2)}) %collective-permute-start.14) | collective-permute-done | bytes 98336 | tf_op jit(solution)/shard_map/ppermute | solution.py:701
  46.1 0.6 shard_map.76
  46.7 2.5 %collective-permute-start.16 = (f32[48,128]{1,0:T(8,128)S(1)}, f32[48,128]{1,0:T(8,128)S(1)}, u32[]{:S(2)}, u32[]{:S(2)}) collective-permute-start(f32[48,128]{1,0:T(8,128)S(1)} %get-tuple-element.100), channel_id=1, source_target_pairs={{0,64},{16,80},{32,96},{48,112},{64,0},{80,16},{96,32},{112,48},{1... | collective-permute-start | bytes 73736 | tf_op jit(solution)/shard_map/ppermute | solution.py:701
  49.3 2.8 %collective-permute-done.16.b_m = f32[48,128]{1,0:T(8,128)S(1)} collective-permute-done((f32[48,128]{1,0:T(8,128)S(1)}, f32[48,128]{1,0:T(8,128)S(1)}, u32[]{:S(2)}, u32[]{:S(2)}) %collective-permute-start.16) | collective-permute-done | bytes 24608 | tf_op jit(solution)/shard_map/ppermute | solution.py:701
  52.2 2.2 %collective-permute-done.15.b_t = f32[192,128]{1,0:T(8,128)S(1)} collective-permute-done((f32[192,128]{1,0:T(8,128)S(1)}, f32[192,128]{1,0:T(8,128)S(1)}, u32[]{:S(2)}, u32[]{:S(2)}) %collective-permute-start.15) | collective-permute-done | bytes 98336 | tf_op jit(solution)/shard_map/ppermute | solution.py:696
  54.6 0.5 collective-permute-done.17.b_x
  55.7 1.9 %collective-permute-start.18 = (f32[384,128]{1,0:T(8,128)S(1)}, f32[384,128]{1,0:T(8,128)S(1)}, u32[]{:S(2)}, u32[]{:S(2)}) collective-permute-start(f32[384,128]{1,0:T(8,128)S(1)} %get-tuple-element.108), channel_id=1, source_target_pairs={{0,64},{16,80},{32,96},{48,112},{64,0},{80,16},{96,32},{112,48},{1... | collective-permute-start | bytes 589832 | tf_op jit(solution)/shard_map/ppermute | solution.py:701
  57.6 2.1 %collective-permute-start.19 = (f32[192,128]{1,0:T(8,128)S(1)}, f32[192,128]{1,0:T(8,128)S(1)}, u32[]{:S(2)}, u32[]{:S(2)}) collective-permute-start(f32[192,128]{1,0:T(8,128)S(1)} %get-tuple-element.111), channel_id=1, source_target_pairs={{0,15},{1,0},{2,1},{3,2},{4,3},{5,4},{6,5},{7,6},{8,7},{9,8},{10,9... | collective-permute-start | bytes 294920 | tf_op jit(solution)/shard_map/ppermute | solution.py:696
  59.7 1.3 %collective-permute-start.20 = (f32[48,128]{1,0:T(8,128)S(1)}, f32[48,128]{1,0:T(8,128)S(1)}, u32[]{:S(2)}, u32[]{:S(2)}) collective-permute-start(f32[48,128]{1,0:T(8,128)S(1)} %get-tuple-element.112), channel_id=1, source_target_pairs={{0,112},{16,0},{32,16},{48,32},{64,48},{80,64},{96,80},{112,96},{1... | collective-permute-start | bytes 73736 | tf_op jit(solution)/shard_map/ppermute | solution.py:696
  61.0 1.9 %collective-permute-start.21 = (f32[48,128]{1,0:T(8,128)S(1)}, f32[48,128]{1,0:T(8,128)S(1)}, u32[]{:S(2)}, u32[]{:S(2)}) collective-permute-start(f32[48,128]{1,0:T(8,128)S(1)} %get-tuple-element.113), channel_id=1, source_target_pairs={{0,64},{16,80},{32,96},{48,112},{64,0},{80,16},{96,32},{112,48},{1... | collective-permute-start | bytes 73736 | tf_op jit(solution)/shard_map/ppermute | solution.py:701
  62.9 0.7 collective-permute-done.20.r_x
  63.5 2.8 %collective-permute-done.21.r_m = f32[48,128]{1,0:T(8,128)S(1)} collective-permute-done((f32[48,128]{1,0:T(8,128)S(1)}, f32[48,128]{1,0:T(8,128)S(1)}, u32[]{:S(2)}, u32[]{:S(2)}) %collective-permute-start.21) | collective-permute-done | bytes 24608 | tf_op jit(solution)/shard_map/ppermute | solution.py:701
  66.6 2.0 %collective-permute-start.22 = (f32[192,128]{1,0:T(8,128)S(1)}, f32[192,128]{1,0:T(8,128)S(1)}, u32[]{:S(2)}, u32[]{:S(2)}) collective-permute-start(f32[192,128]{1,0:T(8,128)S(1)} %get-tuple-element.117), channel_id=1, source_target_pairs={{0,64},{16,80},{32,96},{48,112},{64,0},{80,16},{96,32},{112,48},{1... | collective-permute-start | bytes 294920 | tf_op jit(solution)/shard_map/ppermute | solution.py:701
  68.7 4.1 %collective-permute-done.22.rest_5_ = f32[192,128]{1,0:T(8,128)S(1)} collective-permute-done((f32[192,128]{1,0:T(8,128)S(1)}, f32[192,128]{1,0:T(8,128)S(1)}, u32[]{:S(2)}, u32[]{:S(2)}) %collective-permute-start.22) | collective-permute-done | bytes 98336 | tf_op jit(solution)/shard_map/ppermute | solution.py:701
  72.8 1.2 %shard_map.82 = (f32[1152,128]{1,0:T(8,128)}, f32[1152,128]{1,0:T(8,128)}) custom-call(s32[64,128]{1,0:T(8,128)S(1)} %get-tuple-element.61.info_ref, f32[1152,128]{1,0:T(8,128)S(1)} %get-tuple-element.95.u, f32[576,128]{1,0:T(8,128)S(1)} %get-tuple-element.96.p, f32[1152,128]{1,0:T(8,128)S(1)} %bitcast.22, f32[288,128]{1,0:T(8,128)S(1)} %get-tuple-element.109.u3, ...), custom_call_target="tpu_custom_call" | custom-call | tf_op jit(solution)/shard_map/pallas_call | solution.py:675
  (33 shorter events, 3.9 us)
Async XLA Ops:
  0.6 14.9 %copy-start = (f32[4,2,3,3,4,1,4,128]{7,6,5,4,3,2,1,0:T(4,128)S(1)}, f32[4,2,3,3,4,1,4,128]{7,6,5,4,3,2,1,0:T(4,128)}, u32[]{:S(2)}) copy-start(f32[4,2,3,3,4,1,4,128]{7,6,5,4,3,2,1,0:T(4,128)} %param.5) | copy-start | bytes 1769476
  3.6 11.9 %collective-permute-start = (f32[192,128]{1,0:T(8,128)S(1)}, f32[192,128]{1,0:T(8,128)S(1)}, u32[]{:S(2)}, u32[]{:S(2)}) collective-permute-start(f32[192,128]{1,0:T(8,128)S(1)} %get-tuple-element.65), channel_id=1, source_target_pairs={{0,1},{1,0},{2,3},{3,2},{4,5},{5,4},{6,7},{7,6},{8,9},{9,8},{10,11... | collective-permute-start | bytes 294920 | tf_op jit(solution)/shard_map/ppermute | solution.py:691
  3.7 11.8 %collective-permute-start.1 = (f32[192,128]{1,0:T(8,128)S(1)}, f32[192,128]{1,0:T(8,128)S(1)}, u32[]{:S(2)}, u32[]{:S(2)}) collective-permute-start(f32[192,128]{1,0:T(8,128)S(1)} %get-tuple-element.66), channel_id=1, source_target_pairs={{0,15},{1,2},{2,1},{3,4},{4,3},{5,6},{6,5},{7,8},{8,7},{9,10},{10,... | collective-permute-start | bytes 294920 | tf_op jit(solution)/shard_map/ppermute | solution.py:691
  9.3 6.2 %collective-permute-start.2 = (f32[96,128]{1,0:T(8,128)S(1)}, f32[96,128]{1,0:T(8,128)S(1)}, u32[]{:S(2)}, u32[]{:S(2)}) collective-permute-start(f32[96,128]{1,0:T(8,128)S(1)} %get-tuple-element.67), channel_id=1, source_target_pairs={{0,64},{16,80},{32,96},{48,112},{64,0},{80,16},{96,32},{112,48},{1... | collective-permute-start | bytes 147464 | tf_op jit(solution)/shard_map/ppermute | solution.py:701
  13.2 3.8 %collective-permute-start.3 = (f32[48,128]{1,0:T(8,128)S(1)}, f32[48,128]{1,0:T(8,128)S(1)}, u32[]{:S(2)}, u32[]{:S(2)}) collective-permute-start(f32[48,128]{1,0:T(8,128)S(1)} %get-tuple-element.69), channel_id=1, source_target_pairs={{0,16},{16,0},{32,48},{48,32},{64,80},{80,64},{96,112},{112,96},{1... | collective-permute-start | bytes 73736 | tf_op jit(solution)/shard_map/ppermute | solution.py:691
  13.8 5.9 %collective-permute-start.4 = (f32[48,128]{1,0:T(8,128)S(1)}, f32[48,128]{1,0:T(8,128)S(1)}, u32[]{:S(2)}, u32[]{:S(2)}) collective-permute-start(f32[48,128]{1,0:T(8,128)S(1)} %get-tuple-element.70), channel_id=1, source_target_pairs={{0,112},{16,32},{32,16},{48,64},{64,48},{80,96},{96,80},{112,0},{1... | collective-permute-start | bytes 73736 | tf_op jit(solution)/shard_map/ppermute | solution.py:691
  20.1 7.6 %collective-permute-start.5 = (f32[192,128]{1,0:T(8,128)S(1)}, f32[192,128]{1,0:T(8,128)S(1)}, u32[]{:S(2)}, u32[]{:S(2)}) collective-permute-start(f32[192,128]{1,0:T(8,128)S(1)} %get-tuple-element.74), channel_id=1, source_target_pairs={{0,1},{1,0},{2,3},{3,2},{4,5},{5,4},{6,7},{7,6},{8,9},{9,8},{10,11... | collective-permute-start | bytes 294920 | tf_op jit(solution)/shard_map/ppermute | solution.py:691
  20.2 7.8 %collective-permute-start.6 = (f32[192,128]{1,0:T(8,128)S(1)}, f32[192,128]{1,0:T(8,128)S(1)}, u32[]{:S(2)}, u32[]{:S(2)}) collective-permute-start(f32[192,128]{1,0:T(8,128)S(1)} %get-tuple-element.75), channel_id=1, source_target_pairs={{0,15},{1,2},{2,1},{3,4},{4,3},{5,6},{6,5},{7,8},{8,7},{9,10},{10,... | collective-permute-start | bytes 294920 | tf_op jit(solution)/shard_map/ppermute | solution.py:691
  22.1 5.6 %collective-permute-start.7 = (f32[96,128]{1,0:T(8,128)S(1)}, f32[96,128]{1,0:T(8,128)S(1)}, u32[]{:S(2)}, u32[]{:S(2)}) collective-permute-start(f32[96,128]{1,0:T(8,128)S(1)} %get-tuple-element.76), channel_id=1, source_target_pairs={{0,64},{16,80},{32,96},{48,112},{64,0},{80,16},{96,32},{112,48},{1... | collective-permute-start | bytes 147464 | tf_op jit(solution)/shard_map/ppermute | solution.py:701
  22.1 6.1 %collective-permute-start.8 = (f32[48,128]{1,0:T(8,128)S(1)}, f32[48,128]{1,0:T(8,128)S(1)}, u32[]{:S(2)}, u32[]{:S(2)}) collective-permute-start(f32[48,128]{1,0:T(8,128)S(1)} %get-tuple-element.79), channel_id=1, source_target_pairs={{0,16},{16,0},{32,48},{48,32},{64,80},{80,64},{96,112},{112,96},{1... | collective-permute-start | bytes 73736 | tf_op jit(solution)/shard_map/ppermute | solution.py:691
  22.3 5.9 %collective-permute-start.9 = (f32[48,128]{1,0:T(8,128)S(1)}, f32[48,128]{1,0:T(8,128)S(1)}, u32[]{:S(2)}, u32[]{:S(2)}) collective-permute-start(f32[48,128]{1,0:T(8,128)S(1)} %get-tuple-element.80), channel_id=1, source_target_pairs={{0,112},{16,32},{32,16},{48,64},{64,48},{80,96},{96,80},{112,0},{1... | collective-permute-start | bytes 73736 | tf_op jit(solution)/shard_map/ppermute | solution.py:691
  28.8 13.6 %collective-permute-start.10 = (f32[384,128]{1,0:T(8,128)S(1)}, f32[384,128]{1,0:T(8,128)S(1)}, u32[]{:S(2)}, u32[]{:S(2)}) collective-permute-start(f32[384,128]{1,0:T(8,128)S(1)} %get-tuple-element.85), channel_id=1, source_target_pairs={{0,64},{16,80},{32,96},{48,112},{64,0},{80,16},{96,32},{112,48},{1... | collective-permute-start | bytes 589832 | tf_op jit(solution)/shard_map/ppermute | solution.py:701
  31.0 8.6 %collective-permute-start.11 = (f32[192,128]{1,0:T(8,128)S(1)}, f32[192,128]{1,0:T(8,128)S(1)}, u32[]{:S(2)}, u32[]{:S(2)}) collective-permute-start(f32[192,128]{1,0:T(8,128)S(1)} %get-tuple-element.88), channel_id=1, source_target_pairs={{0,15},{1,0},{2,1},{3,2},{4,3},{5,4},{6,5},{7,6},{8,7},{9,8},{10,9... | collective-permute-start | bytes 294920 | tf_op jit(solution)/shard_map/ppermute | solution.py:696
  33.2 3.8 %collective-permute-start.12 = (f32[48,128]{1,0:T(8,128)S(1)}, f32[48,128]{1,0:T(8,128)S(1)}, u32[]{:S(2)}, u32[]{:S(2)}) collective-permute-start(f32[48,128]{1,0:T(8,128)S(1)} %get-tuple-element.89), channel_id=1, source_target_pairs={{0,112},{16,0},{32,16},{48,32},{64,48},{80,64},{96,80},{112,96},{1... | collective-permute-start | bytes 73736 | tf_op jit(solution)/shard_map/ppermute | solution.py:696
  34.3 8.1 %copy-start.1 = (f32[4,2,3,3,4,1,4,128]{7,6,5,4,3,2,1,0:T(4,128)S(1)}, f32[4,2,3,3,4,1,4,128]{7,6,5,4,3,2,1,0:T(4,128)}, u32[]{:S(2)}) copy-start(f32[4,2,3,3,4,1,4,128]{7,6,5,4,3,2,1,0:T(4,128)} %param.6) | copy-start | bytes 1769476
  34.3 5.3 %collective-permute-start.13 = (f32[48,128]{1,0:T(8,128)S(1)}, f32[48,128]{1,0:T(8,128)S(1)}, u32[]{:S(2)}, u32[]{:S(2)}) collective-permute-start(f32[48,128]{1,0:T(8,128)S(1)} %get-tuple-element.90), channel_id=1, source_target_pairs={{0,64},{16,80},{32,96},{48,112},{64,0},{80,16},{96,32},{112,48},{1... | collective-permute-start | bytes 73736 | tf_op jit(solution)/shard_map/ppermute | solution.py:701
  39.9 6.2 %collective-permute-start.14 = (f32[192,128]{1,0:T(8,128)S(1)}, f32[192,128]{1,0:T(8,128)S(1)}, u32[]{:S(2)}, u32[]{:S(2)}) collective-permute-start(f32[192,128]{1,0:T(8,128)S(1)} %get-tuple-element.94), channel_id=1, source_target_pairs={{0,64},{16,80},{32,96},{48,112},{64,0},{80,16},{96,32},{112,48},{1... | collective-permute-start | bytes 294920 | tf_op jit(solution)/shard_map/ppermute | solution.py:701
  46.7 7.7 %collective-permute-start.15 = (f32[192,128]{1,0:T(8,128)S(1)}, f32[192,128]{1,0:T(8,128)S(1)}, u32[]{:S(2)}, u32[]{:S(2)}) collective-permute-start(f32[192,128]{1,0:T(8,128)S(1)} %get-tuple-element.99), channel_id=1, source_target_pairs={{0,1},{1,2},{2,3},{3,4},{4,5},{5,6},{6,7},{7,8},{8,9},{9,10},{10,1... | collective-permute-start | bytes 294920 | tf_op jit(solution)/shard_map/ppermute | solution.py:696
  46.7 5.4 %collective-permute-start.16 = (f32[48,128]{1,0:T(8,128)S(1)}, f32[48,128]{1,0:T(8,128)S(1)}, u32[]{:S(2)}, u32[]{:S(2)}) collective-permute-start(f32[48,128]{1,0:T(8,128)S(1)} %get-tuple-element.100), channel_id=1, source_target_pairs={{0,64},{16,80},{32,96},{48,112},{64,0},{80,16},{96,32},{112,48},{1... | collective-permute-start | bytes 73736 | tf_op jit(solution)/shard_map/ppermute | solution.py:701
  49.2 5.9 %collective-permute-start.17 = (f32[48,128]{1,0:T(8,128)S(1)}, f32[48,128]{1,0:T(8,128)S(1)}, u32[]{:S(2)}, u32[]{:S(2)}) collective-permute-start(f32[48,128]{1,0:T(8,128)S(1)} %get-tuple-element.103), channel_id=1, source_target_pairs={{0,16},{16,32},{32,48},{48,64},{64,80},{80,96},{96,112},{112,0},{1... | collective-permute-start | bytes 73736 | tf_op jit(solution)/shard_map/ppermute | solution.py:696
  55.7 12.9 %collective-permute-start.18 = (f32[384,128]{1,0:T(8,128)S(1)}, f32[384,128]{1,0:T(8,128)S(1)}, u32[]{:S(2)}, u32[]{:S(2)}) collective-permute-start(f32[384,128]{1,0:T(8,128)S(1)} %get-tuple-element.108), channel_id=1, source_target_pairs={{0,64},{16,80},{32,96},{48,112},{64,0},{80,16},{96,32},{112,48},{1... | collective-permute-start | bytes 589832 | tf_op jit(solution)/shard_map/ppermute | solution.py:701
  57.6 8.7 %collective-permute-start.19 = (f32[192,128]{1,0:T(8,128)S(1)}, f32[192,128]{1,0:T(8,128)S(1)}, u32[]{:S(2)}, u32[]{:S(2)}) collective-permute-start(f32[192,128]{1,0:T(8,128)S(1)} %get-tuple-element.111), channel_id=1, source_target_pairs={{0,15},{1,0},{2,1},{3,2},{4,3},{5,4},{6,5},{7,6},{8,7},{9,8},{10,9... | collective-permute-start | bytes 294920 | tf_op jit(solution)/shard_map/ppermute | solution.py:696
  59.7 3.8 %collective-permute-start.20 = (f32[48,128]{1,0:T(8,128)S(1)}, f32[48,128]{1,0:T(8,128)S(1)}, u32[]{:S(2)}, u32[]{:S(2)}) collective-permute-start(f32[48,128]{1,0:T(8,128)S(1)} %get-tuple-element.112), channel_id=1, source_target_pairs={{0,112},{16,0},{32,16},{48,32},{64,48},{80,64},{96,80},{112,96},{1... | collective-permute-start | bytes 73736 | tf_op jit(solution)/shard_map/ppermute | solution.py:696
  61.0 5.3 %collective-permute-start.21 = (f32[48,128]{1,0:T(8,128)S(1)}, f32[48,128]{1,0:T(8,128)S(1)}, u32[]{:S(2)}, u32[]{:S(2)}) collective-permute-start(f32[48,128]{1,0:T(8,128)S(1)} %get-tuple-element.113), channel_id=1, source_target_pairs={{0,64},{16,80},{32,96},{48,112},{64,0},{80,16},{96,32},{112,48},{1... | collective-permute-start | bytes 73736 | tf_op jit(solution)/shard_map/ppermute | solution.py:701
  66.6 6.2 %collective-permute-start.22 = (f32[192,128]{1,0:T(8,128)S(1)}, f32[192,128]{1,0:T(8,128)S(1)}, u32[]{:S(2)}, u32[]{:S(2)}) collective-permute-start(f32[192,128]{1,0:T(8,128)S(1)} %get-tuple-element.117), channel_id=1, source_target_pairs={{0,64},{16,80},{32,96},{48,112},{64,0},{80,16},{96,32},{112,48},{1... | collective-permute-start | bytes 294920 | tf_op jit(solution)/shard_map/ppermute | solution.py:701

commit v6 on v5

--- a/solution.py
+++ b/solution.py
@@ -8,7 +8,6 @@
 
 HOPPING = 0.13
 STEP = 0.25
-DEGREE = 6
 F32 = jnp.float32
 GAMMA = (
     ((3, 2, 1, 0), ((0, 1), (0, 1), (0, -1), (0, -1))),
@@ -540,15 +539,11 @@
     c1 = 0.5 * (square_diag[0] + square_diag[1] + square_diag[2])
     triple = cmul_conj(cmul(b01, b12), b02)[0]
     c0 = b[0] * (b[1] * b[2] - n12) - b[1] * n02 - b[2] * n01 + 2.0 * triple
-    one = jnp.ones_like(c1)
-    zero = jnp.zeros_like(c1)
-    r0, r1, r2 = (one, zero), (zero, zero), (zero, zero)
-    for k in range(DEGREE, 0, -1):
-        inv = 1.0 / k
-        new0 = (1.0 + (r2[1] * c0) * inv, -(r2[0] * c0) * inv)
-        new1 = ((r0[0] - r2[0] * c1) * inv, (r0[1] - r2[1] * c1) * inv)
-        new2 = (r1[0] * inv, r1[1] * inv)
-        r0, r1, r2 = new0, new1, new2
+    i0 = c0 * (-1.0 / 60)
+    r1 = (1.0 / 3 - c1 * (1.0 / 60), c0 * (-1.0 / 360))
+    r2 = 1.0 / 12 - c1 * (1.0 / 360)
+    i0, r1, r2 = (r2 * c0) * -0.5, (0.5 - (r2 * c1) * 0.5, i0 * 0.5), (r1[0] * 0.5, r1[1] * 0.5)
+    r0, r1, r2 = (1.0 + r2[1] * c0, -(r2[0] * c0)), (1.0 - r2[0] * c1, i0 - r2[1] * c1), r1
     ir1 = (-r1[1], r1[0])
     e = [[None] * 3 for _ in range(3)]
     for i in range(3):

time: 74.1 us -> 74 us (level)
  no operation moved by 1% of the time
where the time goes in v6:
time: 74 us; the launch traced here: 73.9 us
  starting transfers between devices  39.8 us (54%)
  waiting for transfers between devices  25.9 us (35%)
  Pallas kernels  7.38 us (10%)
  between operations  0.76 us (1%)
    ppermute x9, starting transfers between devices, mirror_swap(): return lax.ppermute(value, 'xd', [(i, i ^ n // 2) for i in range(n)])  19.2 us
    ppermute x9, waiting for transfers between devices, mirror_swap(): return lax.ppermute(value, 'xd', [(i, i ^ n // 2) for i in range(n)])  17.7 us
    ppermute x8, starting transfers between devices, swap(): return lax.ppermute(value, axis, pairs)  13.8 us
    pallas_call x15, Pallas kernels, call(): pl.pallas_call(kernel, out_shape=[jax.ShapeDtypeStruct((s, 128), F32) if...  7.38 us
    ppermute x6, starting transfers between devices, shift(): return lax.ppermute(value, axis, [(i, (i + by) % n) for i in range(n)])  6.82 us
    ppermute x8, waiting for transfers between devices, swap(): return lax.ppermute(value, axis, pairs)  4.39 us
    ppermute x6, waiting for transfers between devices, shift(): return lax.ppermute(value, axis, [(i, (i + by) % n) for i in range(n)])  3.84 us
  transfers between devices with their start and end apart: 23, of which 14 were waited for; matrix products, arithmetic and copies ran while one was open for 0% of the time, Pallas kernels for 2%

profile of v6, /device:TPU:0, one launch (start us, length us, event | category | flops | bytes accessed | tf_op | source)
XLA Modules:
  0.0 73.9 jit_solution(6123858518550340371)
XLA Ops:
  0.6 2.9 %shard_map.68 = (f32[384,128]{1,0:T(8,128)S(1)}, f32[192,128]{1,0:T(8,128)S(1)}, f32[192,128]{1,0:T(8,128)S(1)}, f32[48,128]{1,0:T(8,128)S(1)}, f32[48,128]{1,0:...) custom-call(s32[4]{0:T(128)} %partner_hbm.1, ...), custom_call_target="tpu_custom_call" | custom-call | tf_op jit(solution)/shard_map/pallas_call | solution.py:670
  3.7 5.6 %collective-permute-start.1 = (f32[192,128]{1,0:T(8,128)S(1)}, f32[192,128]{1,0:T(8,128)S(1)}, u32[]{:S(2)}, u32[]{:S(2)}) collective-permute-start(f32[192,128]{1,0:T(8,128)S(1)} %get-tuple-element.66), channel_id=1, source_target_pairs={{0,15},{1,2},{2,1},{3,4},{4,3},{5,6},{6,5},{7,8},{8,7},{9,10},{10,... | collective-permute-start | bytes 294920 | tf_op jit(solution)/shard_map/ppermute | solution.py:686
  9.3 3.9 %collective-permute-start.2 = (f32[96,128]{1,0:T(8,128)S(1)}, f32[96,128]{1,0:T(8,128)S(1)}, u32[]{:S(2)}, u32[]{:S(2)}) collective-permute-start(f32[96,128]{1,0:T(8,128)S(1)} %get-tuple-element.67), channel_id=1, source_target_pairs={{0,64},{16,80},{32,96},{48,112},{64,0},{80,16},{96,32},{112,48},{1... | collective-permute-start | bytes 147464 | tf_op jit(solution)/shard_map/ppermute | solution.py:696
  13.2 0.7 collective-permute-start.3
  13.8 1.5 %collective-permute-start.4 = (f32[48,128]{1,0:T(8,128)S(1)}, f32[48,128]{1,0:T(8,128)S(1)}, u32[]{:S(2)}, u32[]{:S(2)}) collective-permute-start(f32[48,128]{1,0:T(8,128)S(1)} %get-tuple-element.70), channel_id=1, source_target_pairs={{0,112},{16,32},{32,16},{48,64},{64,48},{80,96},{96,80},{112,0},{1... | collective-permute-start | bytes 73736 | tf_op jit(solution)/shard_map/ppermute | solution.py:686
  15.7 1.3 %collective-permute-done.3.x_a = f32[48,128]{1,0:T(8,128)S(1)} collective-permute-done((f32[48,128]{1,0:T(8,128)S(1)}, f32[48,128]{1,0:T(8,128)S(1)}, u32[]{:S(2)}, u32[]{:S(2)}) %collective-permute-start.3) | collective-permute-done | bytes 24608 | tf_op jit(solution)/shard_map/ppermute | solution.py:686
  17.0 2.8 %collective-permute-done.4.x_b = f32[48,128]{1,0:T(8,128)S(1)} collective-permute-done((f32[48,128]{1,0:T(8,128)S(1)}, f32[48,128]{1,0:T(8,128)S(1)}, u32[]{:S(2)}, u32[]{:S(2)}) %collective-permute-start.4) | collective-permute-done | bytes 24608 | tf_op jit(solution)/shard_map/ppermute | solution.py:686
  20.2 1.9 %collective-permute-start.6 = (f32[192,128]{1,0:T(8,128)S(1)}, f32[192,128]{1,0:T(8,128)S(1)}, u32[]{:S(2)}, u32[]{:S(2)}) collective-permute-start(f32[192,128]{1,0:T(8,128)S(1)} %get-tuple-element.75), channel_id=1, source_target_pairs={{0,15},{1,2},{2,1},{3,4},{4,3},{5,6},{6,5},{7,8},{8,7},{9,10},{10,... | collective-permute-start | bytes 294920 | tf_op jit(solution)/shard_map/ppermute | solution.py:686
  22.3 3.8 %collective-permute-start.9 = (f32[48,128]{1,0:T(8,128)S(1)}, f32[48,128]{1,0:T(8,128)S(1)}, u32[]{:S(2)}, u32[]{:S(2)}) collective-permute-start(f32[48,128]{1,0:T(8,128)S(1)} %get-tuple-element.80), channel_id=1, source_target_pairs={{0,112},{16,32},{32,16},{48,64},{64,48},{80,96},{96,80},{112,0},{1... | collective-permute-start | bytes 73736 | tf_op jit(solution)/shard_map/ppermute | solution.py:686
  26.1 1.7 %collective-permute-done.7.mirror = f32[96,128]{1,0:T(8,128)S(1)} collective-permute-done((f32[96,128]{1,0:T(8,128)S(1)}, f32[96,128]{1,0:T(8,128)S(1)}, u32[]{:S(2)}, u32[]{:S(2)}) %collective-permute-start.7) | collective-permute-done | bytes 49184 | tf_op jit(solution)/shard_map/ppermute | solution.py:696
  28.8 2.2 %collective-permute-start.10 = (f32[384,128]{1,0:T(8,128)S(1)}, f32[384,128]{1,0:T(8,128)S(1)}, u32[]{:S(2)}, u32[]{:S(2)}) collective-permute-start(f32[384,128]{1,0:T(8,128)S(1)} %get-tuple-element.85), channel_id=1, source_target_pairs={{0,64},{16,80},{32,96},{48,112},{64,0},{80,16},{96,32},{112,48},{1... | collective-permute-start | bytes 589832 | tf_op jit(solution)/shard_map/ppermute | solution.py:696
  31.0 2.2 %collective-permute-start.11 = (f32[192,128]{1,0:T(8,128)S(1)}, f32[192,128]{1,0:T(8,128)S(1)}, u32[]{:S(2)}, u32[]{:S(2)}) collective-permute-start(f32[192,128]{1,0:T(8,128)S(1)} %get-tuple-element.88), channel_id=1, source_target_pairs={{0,15},{1,0},{2,1},{3,2},{4,3},{5,4},{6,5},{7,6},{8,7},{9,8},{10,9... | collective-permute-start | bytes 294920 | tf_op jit(solution)/shard_map/ppermute | solution.py:691
  33.2 1.0 %collective-permute-start.12 = (f32[48,128]{1,0:T(8,128)S(1)}, f32[48,128]{1,0:T(8,128)S(1)}, u32[]{:S(2)}, u32[]{:S(2)}) collective-permute-start(f32[48,128]{1,0:T(8,128)S(1)} %get-tuple-element.89), channel_id=1, source_target_pairs={{0,112},{16,0},{32,16},{48,32},{64,48},{80,64},{96,80},{112,96},{1... | collective-permute-start | bytes 73736 | tf_op jit(solution)/shard_map/ppermute | solution.py:691
  34.3 2.4 %collective-permute-start.13 = (f32[48,128]{1,0:T(8,128)S(1)}, f32[48,128]{1,0:T(8,128)S(1)}, u32[]{:S(2)}, u32[]{:S(2)}) collective-permute-start(f32[48,128]{1,0:T(8,128)S(1)} %get-tuple-element.90), channel_id=1, source_target_pairs={{0,64},{16,80},{32,96},{48,112},{64,0},{80,16},{96,32},{112,48},{1... | collective-permute-start | bytes 73736 | tf_op jit(solution)/shard_map/ppermute | solution.py:696
  36.7 0.4 collective-permute-done.12.r_x
  37.1 2.5 %collective-permute-done.13.r_m = f32[48,128]{1,0:T(8,128)S(1)} collective-permute-done((f32[48,128]{1,0:T(8,128)S(1)}, f32[48,128]{1,0:T(8,128)S(1)}, u32[]{:S(2)}, u32[]{:S(2)}) %collective-permute-start.13) | collective-permute-done | bytes 24608 | tf_op jit(solution)/shard_map/ppermute | solution.py:696
  39.9 2.5 %collective-permute-start.14 = (f32[192,128]{1,0:T(8,128)S(1)}, f32[192,128]{1,0:T(8,128)S(1)}, u32[]{:S(2)}, u32[]{:S(2)}) collective-permute-start(f32[192,128]{1,0:T(8,128)S(1)} %get-tuple-element.94), channel_id=1, source_target_pairs={{0,64},{16,80},{32,96},{48,112},{64,0},{80,16},{96,32},{112,48},{1... | collective-permute-start | bytes 294920 | tf_op jit(solution)/shard_map/ppermute | solution.py:696
  42.5 3.6 %collective-permute-done.14.rest_5_ = f32[192,128]{1,0:T(8,128)S(1)} collective-permute-done((f32[192,128]{1,0:T(8,128)S(1)}, f32[192,128]{1,0:T(8,128)S(1)}, u32[]{:S(2)}, u32[]{:S(2)}) %collective-permute-start.14) | collective-permute-done | bytes 98336 | tf_op jit(solution)/shard_map/ppermute | solution.py:696
  46.1 0.5 shard_map.76
  46.7 2.5 %collective-permute-start.16 = (f32[48,128]{1,0:T(8,128)S(1)}, f32[48,128]{1,0:T(8,128)S(1)}, u32[]{:S(2)}, u32[]{:S(2)}) collective-permute-start(f32[48,128]{1,0:T(8,128)S(1)} %get-tuple-element.100), channel_id=1, source_target_pairs={{0,64},{16,80},{32,96},{48,112},{64,0},{80,16},{96,32},{112,48},{1... | collective-permute-start | bytes 73736 | tf_op jit(solution)/shard_map/ppermute | solution.py:696
  49.3 2.8 %collective-permute-done.16.b_m = f32[48,128]{1,0:T(8,128)S(1)} collective-permute-done((f32[48,128]{1,0:T(8,128)S(1)}, f32[48,128]{1,0:T(8,128)S(1)}, u32[]{:S(2)}, u32[]{:S(2)}) %collective-permute-start.16) | collective-permute-done | bytes 24608 | tf_op jit(solution)/shard_map/ppermute | solution.py:696
  52.1 2.2 %collective-permute-done.15.b_t = f32[192,128]{1,0:T(8,128)S(1)} collective-permute-done((f32[192,128]{1,0:T(8,128)S(1)}, f32[192,128]{1,0:T(8,128)S(1)}, u32[]{:S(2)}, u32[]{:S(2)}) %collective-permute-start.15) | collective-permute-done | bytes 98336 | tf_op jit(solution)/shard_map/ppermute | solution.py:691
  54.6 0.5 collective-permute-done.17.b_x
  55.7 1.9 %collective-permute-start.18 = (f32[384,128]{1,0:T(8,128)S(1)}, f32[384,128]{1,0:T(8,128)S(1)}, u32[]{:S(2)}, u32[]{:S(2)}) collective-permute-start(f32[384,128]{1,0:T(8,128)S(1)} %get-tuple-element.108), channel_id=1, source_target_pairs={{0,64},{16,80},{32,96},{48,112},{64,0},{80,16},{96,32},{112,48},{1... | collective-permute-start | bytes 589832 | tf_op jit(solution)/shard_map/ppermute | solution.py:696
  57.6 2.1 %collective-permute-start.19 = (f32[192,128]{1,0:T(8,128)S(1)}, f32[192,128]{1,0:T(8,128)S(1)}, u32[]{:S(2)}, u32[]{:S(2)}) collective-permute-start(f32[192,128]{1,0:T(8,128)S(1)} %get-tuple-element.111), channel_id=1, source_target_pairs={{0,15},{1,0},{2,1},{3,2},{4,3},{5,4},{6,5},{7,6},{8,7},{9,8},{10,9... | collective-permute-start | bytes 294920 | tf_op jit(solution)/shard_map/ppermute | solution.py:691
  59.7 1.3 %collective-permute-start.20 = (f32[48,128]{1,0:T(8,128)S(1)}, f32[48,128]{1,0:T(8,128)S(1)}, u32[]{:S(2)}, u32[]{:S(2)}) collective-permute-start(f32[48,128]{1,0:T(8,128)S(1)} %get-tuple-element.112), channel_id=1, source_target_pairs={{0,112},{16,0},{32,16},{48,32},{64,48},{80,64},{96,80},{112,96},{1... | collective-permute-start | bytes 73736 | tf_op jit(solution)/shard_map/ppermute | solution.py:691
  60.9 1.9 %collective-permute-start.21 = (f32[48,128]{1,0:T(8,128)S(1)}, f32[48,128]{1,0:T(8,128)S(1)}, u32[]{:S(2)}, u32[]{:S(2)}) collective-permute-start(f32[48,128]{1,0:T(8,128)S(1)} %get-tuple-element.113), channel_id=1, source_target_pairs={{0,64},{16,80},{32,96},{48,112},{64,0},{80,16},{96,32},{112,48},{1... | collective-permute-start | bytes 73736 | tf_op jit(solution)/shard_map/ppermute | solution.py:696
  62.8 0.7 collective-permute-done.20.r_x
  63.5 2.8 %collective-permute-done.21.r_m = f32[48,128]{1,0:T(8,128)S(1)} collective-permute-done((f32[48,128]{1,0:T(8,128)S(1)}, f32[48,128]{1,0:T(8,128)S(1)}, u32[]{:S(2)}, u32[]{:S(2)}) %collective-permute-start.21) | collective-permute-done | bytes 24608 | tf_op jit(solution)/shard_map/ppermute | solution.py:696
  66.6 2.0 %collective-permute-start.22 = (f32[192,128]{1,0:T(8,128)S(1)}, f32[192,128]{1,0:T(8,128)S(1)}, u32[]{:S(2)}, u32[]{:S(2)}) collective-permute-start(f32[192,128]{1,0:T(8,128)S(1)} %get-tuple-element.117), channel_id=1, source_target_pairs={{0,64},{16,80},{32,96},{48,112},{64,0},{80,16},{96,32},{112,48},{1... | collective-permute-start | bytes 294920 | tf_op jit(solution)/shard_map/ppermute | solution.py:696
  68.6 4.1 %collective-permute-done.22.rest_5_ = f32[192,128]{1,0:T(8,128)S(1)} collective-permute-done((f32[192,128]{1,0:T(8,128)S(1)}, f32[192,128]{1,0:T(8,128)S(1)}, u32[]{:S(2)}, u32[]{:S(2)}) %collective-permute-start.22) | collective-permute-done | bytes 98336 | tf_op jit(solution)/shard_map/ppermute | solution.py:696
  72.8 1.1 %shard_map.82 = (f32[1152,128]{1,0:T(8,128)}, f32[1152,128]{1,0:T(8,128)}) custom-call(s32[64,128]{1,0:T(8,128)S(1)} %get-tuple-element.61.info_ref, f32[1152,128]{1,0:T(8,128)S(1)} %get-tuple-element.95.u, f32[576,128]{1,0:T(8,128)S(1)} %get-tuple-element.96.p, f32[1152,128]{1,0:T(8,128)S(1)} %bitcast.22, f32[288,128]{1,0:T(8,128)S(1)} %get-tuple-element.109.u3, ...), custom_call_target="tpu_custom_call" | custom-call | tf_op jit(solution)/shard_map/pallas_call | solution.py:670
  (33 shorter events, 3.8 us)
Async XLA Ops:
  0.6 14.9 %copy-start = (f32[4,2,3,3,4,1,4,128]{7,6,5,4,3,2,1,0:T(4,128)S(1)}, f32[4,2,3,3,4,1,4,128]{7,6,5,4,3,2,1,0:T(4,128)}, u32[]{:S(2)}) copy-start(f32[4,2,3,3,4,1,4,128]{7,6,5,4,3,2,1,0:T(4,128)} %param.5) | copy-start | bytes 1769476
  3.6 11.9 %collective-permute-start = (f32[192,128]{1,0:T(8,128)S(1)}, f32[192,128]{1,0:T(8,128)S(1)}, u32[]{:S(2)}, u32[]{:S(2)}) collective-permute-start(f32[192,128]{1,0:T(8,128)S(1)} %get-tuple-element.65), channel_id=1, source_target_pairs={{0,1},{1,0},{2,3},{3,2},{4,5},{5,4},{6,7},{7,6},{8,9},{9,8},{10,11... | collective-permute-start | bytes 294920 | tf_op jit(solution)/shard_map/ppermute | solution.py:686
  3.7 11.8 %collective-permute-start.1 = (f32[192,128]{1,0:T(8,128)S(1)}, f32[192,128]{1,0:T(8,128)S(1)}, u32[]{:S(2)}, u32[]{:S(2)}) collective-permute-start(f32[192,128]{1,0:T(8,128)S(1)} %get-tuple-element.66), channel_id=1, source_target_pairs={{0,15},{1,2},{2,1},{3,4},{4,3},{5,6},{6,5},{7,8},{8,7},{9,10},{10,... | collective-permute-start | bytes 294920 | tf_op jit(solution)/shard_map/ppermute | solution.py:686
  9.3 6.2 %collective-permute-start.2 = (f32[96,128]{1,0:T(8,128)S(1)}, f32[96,128]{1,0:T(8,128)S(1)}, u32[]{:S(2)}, u32[]{:S(2)}) collective-permute-start(f32[96,128]{1,0:T(8,128)S(1)} %get-tuple-element.67), channel_id=1, source_target_pairs={{0,64},{16,80},{32,96},{48,112},{64,0},{80,16},{96,32},{112,48},{1... | collective-permute-start | bytes 147464 | tf_op jit(solution)/shard_map/ppermute | solution.py:696
  13.2 3.8 %collective-permute-start.3 = (f32[48,128]{1,0:T(8,128)S(1)}, f32[48,128]{1,0:T(8,128)S(1)}, u32[]{:S(2)}, u32[]{:S(2)}) collective-permute-start(f32[48,128]{1,0:T(8,128)S(1)} %get-tuple-element.69), channel_id=1, source_target_pairs={{0,16},{16,0},{32,48},{48,32},{64,80},{80,64},{96,112},{112,96},{1... | collective-permute-start | bytes 73736 | tf_op jit(solution)/shard_map/ppermute | solution.py:686
  13.8 5.9 %collective-permute-start.4 = (f32[48,128]{1,0:T(8,128)S(1)}, f32[48,128]{1,0:T(8,128)S(1)}, u32[]{:S(2)}, u32[]{:S(2)}) collective-permute-start(f32[48,128]{1,0:T(8,128)S(1)} %get-tuple-element.70), channel_id=1, source_target_pairs={{0,112},{16,32},{32,16},{48,64},{64,48},{80,96},{96,80},{112,0},{1... | collective-permute-start | bytes 73736 | tf_op jit(solution)/shard_map/ppermute | solution.py:686
  20.1 7.6 %collective-permute-start.5 = (f32[192,128]{1,0:T(8,128)S(1)}, f32[192,128]{1,0:T(8,128)S(1)}, u32[]{:S(2)}, u32[]{:S(2)}) collective-permute-start(f32[192,128]{1,0:T(8,128)S(1)} %get-tuple-element.74), channel_id=1, source_target_pairs={{0,1},{1,0},{2,3},{3,2},{4,5},{5,4},{6,7},{7,6},{8,9},{9,8},{10,11... | collective-permute-start | bytes 294920 | tf_op jit(solution)/shard_map/ppermute | solution.py:686
  20.2 7.8 %collective-permute-start.6 = (f32[192,128]{1,0:T(8,128)S(1)}, f32[192,128]{1,0:T(8,128)S(1)}, u32[]{:S(2)}, u32[]{:S(2)}) collective-permute-start(f32[192,128]{1,0:T(8,128)S(1)} %get-tuple-element.75), channel_id=1, source_target_pairs={{0,15},{1,2},{2,1},{3,4},{4,3},{5,6},{6,5},{7,8},{8,7},{9,10},{10,... | collective-permute-start | bytes 294920 | tf_op jit(solution)/shard_map/ppermute | solution.py:686
  22.1 5.6 %collective-permute-start.7 = (f32[96,128]{1,0:T(8,128)S(1)}, f32[96,128]{1,0:T(8,128)S(1)}, u32[]{:S(2)}, u32[]{:S(2)}) collective-permute-start(f32[96,128]{1,0:T(8,128)S(1)} %get-tuple-element.76), channel_id=1, source_target_pairs={{0,64},{16,80},{32,96},{48,112},{64,0},{80,16},{96,32},{112,48},{1... | collective-permute-start | bytes 147464 | tf_op jit(solution)/shard_map/ppermute | solution.py:696
  22.1 6.1 %collective-permute-start.8 = (f32[48,128]{1,0:T(8,128)S(1)}, f32[48,128]{1,0:T(8,128)S(1)}, u32[]{:S(2)}, u32[]{:S(2)}) collective-permute-start(f32[48,128]{1,0:T(8,128)S(1)} %get-tuple-element.79), channel_id=1, source_target_pairs={{0,16},{16,0},{32,48},{48,32},{64,80},{80,64},{96,112},{112,96},{1... | collective-permute-start | bytes 73736 | tf_op jit(solution)/shard_map/ppermute | solution.py:686
  22.3 5.9 %collective-permute-start.9 = (f32[48,128]{1,0:T(8,128)S(1)}, f32[48,128]{1,0:T(8,128)S(1)}, u32[]{:S(2)}, u32[]{:S(2)}) collective-permute-start(f32[48,128]{1,0:T(8,128)S(1)} %get-tuple-element.80), channel_id=1, source_target_pairs={{0,112},{16,32},{32,16},{48,64},{64,48},{80,96},{96,80},{112,0},{1... | collective-permute-start | bytes 73736 | tf_op jit(solution)/shard_map/ppermute | solution.py:686
  28.8 13.6 %collective-permute-start.10 = (f32[384,128]{1,0:T(8,128)S(1)}, f32[384,128]{1,0:T(8,128)S(1)}, u32[]{:S(2)}, u32[]{:S(2)}) collective-permute-start(f32[384,128]{1,0:T(8,128)S(1)} %get-tuple-element.85), channel_id=1, source_target_pairs={{0,64},{16,80},{32,96},{48,112},{64,0},{80,16},{96,32},{112,48},{1... | collective-permute-start | bytes 589832 | tf_op jit(solution)/shard_map/ppermute | solution.py:696
  31.0 8.6 %collective-permute-start.11 = (f32[192,128]{1,0:T(8,128)S(1)}, f32[192,128]{1,0:T(8,128)S(1)}, u32[]{:S(2)}, u32[]{:S(2)}) collective-permute-start(f32[192,128]{1,0:T(8,128)S(1)} %get-tuple-element.88), channel_id=1, source_target_pairs={{0,15},{1,0},{2,1},{3,2},{4,3},{5,4},{6,5},{7,6},{8,7},{9,8},{10,9... | collective-permute-start | bytes 294920 | tf_op jit(solution)/shard_map/ppermute | solution.py:691
  33.2 3.8 %collective-permute-start.12 = (f32[48,128]{1,0:T(8,128)S(1)}, f32[48,128]{1,0:T(8,128)S(1)}, u32[]{:S(2)}, u32[]{:S(2)}) collective-permute-start(f32[48,128]{1,0:T(8,128)S(1)} %get-tuple-element.89), channel_id=1, source_target_pairs={{0,112},{16,0},{32,16},{48,32},{64,48},{80,64},{96,80},{112,96},{1... | collective-permute-start | bytes 73736 | tf_op jit(solution)/shard_map/ppermute | solution.py:691
  34.3 8.1 %copy-start.1 = (f32[4,2,3,3,4,1,4,128]{7,6,5,4,3,2,1,0:T(4,128)S(1)}, f32[4,2,3,3,4,1,4,128]{7,6,5,4,3,2,1,0:T(4,128)}, u32[]{:S(2)}) copy-start(f32[4,2,3,3,4,1,4,128]{7,6,5,4,3,2,1,0:T(4,128)} %param.6) | copy-start | bytes 1769476
  34.3 5.3 %collective-permute-start.13 = (f32[48,128]{1,0:T(8,128)S(1)}, f32[48,128]{1,0:T(8,128)S(1)}, u32[]{:S(2)}, u32[]{:S(2)}) collective-permute-start(f32[48,128]{1,0:T(8,128)S(1)} %get-tuple-element.90), channel_id=1, source_target_pairs={{0,64},{16,80},{32,96},{48,112},{64,0},{80,16},{96,32},{112,48},{1... | collective-permute-start | bytes 73736 | tf_op jit(solution)/shard_map/ppermute | solution.py:696
  39.9 6.2 %collective-permute-start.14 = (f32[192,128]{1,0:T(8,128)S(1)}, f32[192,128]{1,0:T(8,128)S(1)}, u32[]{:S(2)}, u32[]{:S(2)}) collective-permute-start(f32[192,128]{1,0:T(8,128)S(1)} %get-tuple-element.94), channel_id=1, source_target_pairs={{0,64},{16,80},{32,96},{48,112},{64,0},{80,16},{96,32},{112,48},{1... | collective-permute-start | bytes 294920 | tf_op jit(solution)/shard_map/ppermute | solution.py:696
  46.6 7.7 %collective-permute-start.15 = (f32[192,128]{1,0:T(8,128)S(1)}, f32[192,128]{1,0:T(8,128)S(1)}, u32[]{:S(2)}, u32[]{:S(2)}) collective-permute-start(f32[192,128]{1,0:T(8,128)S(1)} %get-tuple-element.99), channel_id=1, source_target_pairs={{0,1},{1,2},{2,3},{3,4},{4,5},{5,6},{6,7},{7,8},{8,9},{9,10},{10,1... | collective-permute-start | bytes 294920 | tf_op jit(solution)/shard_map/ppermute | solution.py:691
  46.7 5.4 %collective-permute-start.16 = (f32[48,128]{1,0:T(8,128)S(1)}, f32[48,128]{1,0:T(8,128)S(1)}, u32[]{:S(2)}, u32[]{:S(2)}) collective-permute-start(f32[48,128]{1,0:T(8,128)S(1)} %get-tuple-element.100), channel_id=1, source_target_pairs={{0,64},{16,80},{32,96},{48,112},{64,0},{80,16},{96,32},{112,48},{1... | collective-permute-start | bytes 73736 | tf_op jit(solution)/shard_map/ppermute | solution.py:696
  49.2 5.9 %collective-permute-start.17 = (f32[48,128]{1,0:T(8,128)S(1)}, f32[48,128]{1,0:T(8,128)S(1)}, u32[]{:S(2)}, u32[]{:S(2)}) collective-permute-start(f32[48,128]{1,0:T(8,128)S(1)} %get-tuple-element.103), channel_id=1, source_target_pairs={{0,16},{16,32},{32,48},{48,64},{64,80},{80,96},{96,112},{112,0},{1... | collective-permute-start | bytes 73736 | tf_op jit(solution)/shard_map/ppermute | solution.py:691
  55.7 12.9 %collective-permute-start.18 = (f32[384,128]{1,0:T(8,128)S(1)}, f32[384,128]{1,0:T(8,128)S(1)}, u32[]{:S(2)}, u32[]{:S(2)}) collective-permute-start(f32[384,128]{1,0:T(8,128)S(1)} %get-tuple-element.108), channel_id=1, source_target_pairs={{0,64},{16,80},{32,96},{48,112},{64,0},{80,16},{96,32},{112,48},{1... | collective-permute-start | bytes 589832 | tf_op jit(solution)/shard_map/ppermute | solution.py:696
  57.6 8.7 %collective-permute-start.19 = (f32[192,128]{1,0:T(8,128)S(1)}, f32[192,128]{1,0:T(8,128)S(1)}, u32[]{:S(2)}, u32[]{:S(2)}) collective-permute-start(f32[192,128]{1,0:T(8,128)S(1)} %get-tuple-element.111), channel_id=1, source_target_pairs={{0,15},{1,0},{2,1},{3,2},{4,3},{5,4},{6,5},{7,6},{8,7},{9,8},{10,9... | collective-permute-start | bytes 294920 | tf_op jit(solution)/shard_map/ppermute | solution.py:691
  59.7 3.8 %collective-permute-start.20 = (f32[48,128]{1,0:T(8,128)S(1)}, f32[48,128]{1,0:T(8,128)S(1)}, u32[]{:S(2)}, u32[]{:S(2)}) collective-permute-start(f32[48,128]{1,0:T(8,128)S(1)} %get-tuple-element.112), channel_id=1, source_target_pairs={{0,112},{16,0},{32,16},{48,32},{64,48},{80,64},{96,80},{112,96},{1... | collective-permute-start | bytes 73736 | tf_op jit(solution)/shard_map/ppermute | solution.py:691
  60.9 5.3 %collective-permute-start.21 = (f32[48,128]{1,0:T(8,128)S(1)}, f32[48,128]{1,0:T(8,128)S(1)}, u32[]{:S(2)}, u32[]{:S(2)}) collective-permute-start(f32[48,128]{1,0:T(8,128)S(1)} %get-tuple-element.113), channel_id=1, source_target_pairs={{0,64},{16,80},{32,96},{48,112},{64,0},{80,16},{96,32},{112,48},{1... | collective-permute-start | bytes 73736 | tf_op jit(solution)/shard_map/ppermute | solution.py:696
  66.6 6.2 %collective-permute-start.22 = (f32[192,128]{1,0:T(8,128)S(1)}, f32[192,128]{1,0:T(8,128)S(1)}, u32[]{:S(2)}, u32[]{:S(2)}) collective-permute-start(f32[192,128]{1,0:T(8,128)S(1)} %get-tuple-element.117), channel_id=1, source_target_pairs={{0,64},{16,80},{32,96},{48,112},{64,0},{80,16},{96,32},{112,48},{1... | collective-permute-start | bytes 294920 | tf_op jit(solution)/shard_map/ppermute | solution.py:696

commit v7 on v6

--- a/solution.py
+++ b/solution.py
@@ -305,8 +305,8 @@
 
 
 def noise_kernel(partner_hbm, index_hbm, table_hbm, u_hbm, *rest):
-    psi, t_a, t_b, x_a, x_b, mirror, q0, q2, q3, info_ref = rest[:10]
-    flat, parts, h0, h2, table, u, index, partner, sems = rest[10:]
+    psi, t_a, t_b, x_a, x_b, mirror, q0, q2, q3, info_ref, u = rest[:11]
+    flat, parts, h0, h2, table, index, partner, sems = rest[11:]
     copies = [
         pltpu.make_async_copy(src, dst, sems.at[n])
         for n, (src, dst) in enumerate(
@@ -758,17 +758,16 @@
     halo = [12 * HALO, 12 * HALO]
     spin = 24 * ROWS
 
-    psi, *rest, masks = call(
+    psi, *rest, masks, u = call(
         noise_kernel,
         [pltpu.with_memory_space_constraint(v, pltpu.HBM) for v in (partner, index, table, u)],
-        [spin] + messages + local + [jax.ShapeDtypeStruct((INFO_ROWS, 128), jnp.int32)],
+        [spin] + messages + local + [jax.ShapeDtypeStruct((INFO_ROWS, 128), jnp.int32), 72 * ROWS],
         [
             pltpu.VMEM((24, 4096), F32),
             pltpu.VMEM((384, 768), jnp.bfloat16),
             FULL,
             FULL,
             pltpu.VMEM((2, 3, 4, 4096), F32),
-            72 * ROWS,
             pltpu.VMEM((ROWS, 128), jnp.int32),
             pltpu.SMEM((4,), jnp.int32),
             pltpu.SemaphoreType.DMA((4,)),

time: 74 us -> 73.9 us (level)
  no operation moved by 1% of the time
where the time goes in v7:
time: 73.9 us; the launch traced here: 73.8 us
  starting transfers between devices  39.8 us (54%)
  waiting for transfers between devices  25.9 us (35%)
  Pallas kernels  7.31 us (10%)
  between operations  0.76 us (1%)
    ppermute x9, starting transfers between devices, mirror_swap(): return lax.ppermute(value, 'xd', [(i, i ^ n // 2) for i in range(n)])  19.1 us
    ppermute x9, waiting for transfers between devices, mirror_swap(): return lax.ppermute(value, 'xd', [(i, i ^ n // 2) for i in range(n)])  17.7 us
    ppermute x8, starting transfers between devices, swap(): return lax.ppermute(value, axis, pairs)  13.8 us
    pallas_call x15, Pallas kernels, call(): pl.pallas_call(kernel, out_shape=[jax.ShapeDtypeStruct((s, 128), F32) if...  7.31 us
    ppermute x6, starting transfers between devices, shift(): return lax.ppermute(value, axis, [(i, (i + by) % n) for i in range(n)])  6.82 us
    ppermute x8, waiting for transfers between devices, swap(): return lax.ppermute(value, axis, pairs)  4.39 us
    ppermute x6, waiting for transfers between devices, shift(): return lax.ppermute(value, axis, [(i, (i + by) % n) for i in range(n)])  3.83 us
  transfers between devices with their start and end apart: 23, of which 14 were waited for; matrix products, arithmetic and copies ran while one was open for 0% of the time, Pallas kernels for 2%

profile of v7, /device:TPU:0, one launch (start us, length us, event | category | flops | bytes accessed | tf_op | source)
XLA Modules:
  0.0 73.8 jit_solution(9260999603951909167)
XLA Ops:
  0.6 2.9 %shard_map.68 = (f32[384,128]{1,0:T(8,128)S(1)}, f32[192,128]{1,0:T(8,128)S(1)}, f32[192,128]{1,0:T(8,128)S(1)}, f32[48,128]{1,0:T(8,128)S(1)}, f32[48,128]{1,0:...) custom-call(s32[4]{0:T(128)} %partner_hbm.1, ...), custom_call_target="tpu_custom_call" | custom-call | tf_op jit(solution)/shard_map/pallas_call | solution.py:670
  3.6 5.6 %collective-permute-start.1 = (f32[192,128]{1,0:T(8,128)S(1)}, f32[192,128]{1,0:T(8,128)S(1)}, u32[]{:S(2)}, u32[]{:S(2)}) collective-permute-start(f32[192,128]{1,0:T(8,128)S(1)} %get-tuple-element.68), channel_id=1, source_target_pairs={{0,15},{1,2},{2,1},{3,4},{4,3},{5,6},{6,5},{7,8},{8,7},{9,10},{10,... | collective-permute-start | bytes 294920 | tf_op jit(solution)/shard_map/ppermute | solution.py:686
  9.2 3.9 %collective-permute-start.2 = (f32[96,128]{1,0:T(8,128)S(1)}, f32[96,128]{1,0:T(8,128)S(1)}, u32[]{:S(2)}, u32[]{:S(2)}) collective-permute-start(f32[96,128]{1,0:T(8,128)S(1)} %get-tuple-element.69), channel_id=1, source_target_pairs={{0,64},{16,80},{32,96},{48,112},{64,0},{80,16},{96,32},{112,48},{1... | collective-permute-start | bytes 147464 | tf_op jit(solution)/shard_map/ppermute | solution.py:696
  13.1 0.7 collective-permute-start.3
  13.8 1.5 %collective-permute-start.4 = (f32[48,128]{1,0:T(8,128)S(1)}, f32[48,128]{1,0:T(8,128)S(1)}, u32[]{:S(2)}, u32[]{:S(2)}) collective-permute-start(f32[48,128]{1,0:T(8,128)S(1)} %get-tuple-element.72), channel_id=1, source_target_pairs={{0,112},{16,32},{32,16},{48,64},{64,48},{80,96},{96,80},{112,0},{1... | collective-permute-start | bytes 73736 | tf_op jit(solution)/shard_map/ppermute | solution.py:686
  15.6 1.3 %collective-permute-done.3.x_a = f32[48,128]{1,0:T(8,128)S(1)} collective-permute-done((f32[48,128]{1,0:T(8,128)S(1)}, f32[48,128]{1,0:T(8,128)S(1)}, u32[]{:S(2)}, u32[]{:S(2)}) %collective-permute-start.3) | collective-permute-done | bytes 24608 | tf_op jit(solution)/shard_map/ppermute | solution.py:686
  16.9 2.8 %collective-permute-done.4.x_b = f32[48,128]{1,0:T(8,128)S(1)} collective-permute-done((f32[48,128]{1,0:T(8,128)S(1)}, f32[48,128]{1,0:T(8,128)S(1)}, u32[]{:S(2)}, u32[]{:S(2)}) %collective-permute-start.4) | collective-permute-done | bytes 24608 | tf_op jit(solution)/shard_map/ppermute | solution.py:686
  20.1 1.9 %collective-permute-start.6 = (f32[192,128]{1,0:T(8,128)S(1)}, f32[192,128]{1,0:T(8,128)S(1)}, u32[]{:S(2)}, u32[]{:S(2)}) collective-permute-start(f32[192,128]{1,0:T(8,128)S(1)} %get-tuple-element.77), channel_id=1, source_target_pairs={{0,15},{1,2},{2,1},{3,4},{4,3},{5,6},{6,5},{7,8},{8,7},{9,10},{10,... | collective-permute-start | bytes 294920 | tf_op jit(solution)/shard_map/ppermute | solution.py:686
  22.2 3.8 %collective-permute-start.9 = (f32[48,128]{1,0:T(8,128)S(1)}, f32[48,128]{1,0:T(8,128)S(1)}, u32[]{:S(2)}, u32[]{:S(2)}) collective-permute-start(f32[48,128]{1,0:T(8,128)S(1)} %get-tuple-element.82), channel_id=1, source_target_pairs={{0,112},{16,32},{32,16},{48,64},{64,48},{80,96},{96,80},{112,0},{1... | collective-permute-start | bytes 73736 | tf_op jit(solution)/shard_map/ppermute | solution.py:686
  26.0 1.7 %collective-permute-done.7.mirror = f32[96,128]{1,0:T(8,128)S(1)} collective-permute-done((f32[96,128]{1,0:T(8,128)S(1)}, f32[96,128]{1,0:T(8,128)S(1)}, u32[]{:S(2)}, u32[]{:S(2)}) %collective-permute-start.7) | collective-permute-done | bytes 49184 | tf_op jit(solution)/shard_map/ppermute | solution.py:696
  28.7 2.2 %collective-permute-start.10 = (f32[384,128]{1,0:T(8,128)S(1)}, f32[384,128]{1,0:T(8,128)S(1)}, u32[]{:S(2)}, u32[]{:S(2)}) collective-permute-start(f32[384,128]{1,0:T(8,128)S(1)} %get-tuple-element.87), channel_id=1, source_target_pairs={{0,64},{16,80},{32,96},{48,112},{64,0},{80,16},{96,32},{112,48},{1... | collective-permute-start | bytes 589832 | tf_op jit(solution)/shard_map/ppermute | solution.py:696
  30.9 2.2 %collective-permute-start.11 = (f32[192,128]{1,0:T(8,128)S(1)}, f32[192,128]{1,0:T(8,128)S(1)}, u32[]{:S(2)}, u32[]{:S(2)}) collective-permute-start(f32[192,128]{1,0:T(8,128)S(1)} %get-tuple-element.90), channel_id=1, source_target_pairs={{0,15},{1,0},{2,1},{3,2},{4,3},{5,4},{6,5},{7,6},{8,7},{9,8},{10,9... | collective-permute-start | bytes 294920 | tf_op jit(solution)/shard_map/ppermute | solution.py:691
  33.2 1.0 %collective-permute-start.12 = (f32[48,128]{1,0:T(8,128)S(1)}, f32[48,128]{1,0:T(8,128)S(1)}, u32[]{:S(2)}, u32[]{:S(2)}) collective-permute-start(f32[48,128]{1,0:T(8,128)S(1)} %get-tuple-element.91), channel_id=1, source_target_pairs={{0,112},{16,0},{32,16},{48,32},{64,48},{80,64},{96,80},{112,96},{1... | collective-permute-start | bytes 73736 | tf_op jit(solution)/shard_map/ppermute | solution.py:691
  34.2 2.4 %collective-permute-start.13 = (f32[48,128]{1,0:T(8,128)S(1)}, f32[48,128]{1,0:T(8,128)S(1)}, u32[]{:S(2)}, u32[]{:S(2)}) collective-permute-start(f32[48,128]{1,0:T(8,128)S(1)} %get-tuple-element.92), channel_id=1, source_target_pairs={{0,64},{16,80},{32,96},{48,112},{64,0},{80,16},{96,32},{112,48},{1... | collective-permute-start | bytes 73736 | tf_op jit(solution)/shard_map/ppermute | solution.py:696
  36.6 0.4 collective-permute-done.12.r_x
  37.0 2.5 %collective-permute-done.13.r_m = f32[48,128]{1,0:T(8,128)S(1)} collective-permute-done((f32[48,128]{1,0:T(8,128)S(1)}, f32[48,128]{1,0:T(8,128)S(1)}, u32[]{:S(2)}, u32[]{:S(2)}) %collective-permute-start.13) | collective-permute-done | bytes 24608 | tf_op jit(solution)/shard_map/ppermute | solution.py:696
  39.8 2.5 %collective-permute-start.14 = (f32[192,128]{1,0:T(8,128)S(1)}, f32[192,128]{1,0:T(8,128)S(1)}, u32[]{:S(2)}, u32[]{:S(2)}) collective-permute-start(f32[192,128]{1,0:T(8,128)S(1)} %get-tuple-element.96), channel_id=1, source_target_pairs={{0,64},{16,80},{32,96},{48,112},{64,0},{80,16},{96,32},{112,48},{1... | collective-permute-start | bytes 294920 | tf_op jit(solution)/shard_map/ppermute | solution.py:696
  42.4 3.6 %collective-permute-done.14.rest_5_ = f32[192,128]{1,0:T(8,128)S(1)} collective-permute-done((f32[192,128]{1,0:T(8,128)S(1)}, f32[192,128]{1,0:T(8,128)S(1)}, u32[]{:S(2)}, u32[]{:S(2)}) %collective-permute-start.14) | collective-permute-done | bytes 98336 | tf_op jit(solution)/shard_map/ppermute | solution.py:696
  46.0 0.5 shard_map.76
  46.6 2.5 %collective-permute-start.16 = (f32[48,128]{1,0:T(8,128)S(1)}, f32[48,128]{1,0:T(8,128)S(1)}, u32[]{:S(2)}, u32[]{:S(2)}) collective-permute-start(f32[48,128]{1,0:T(8,128)S(1)} %get-tuple-element.102), channel_id=1, source_target_pairs={{0,64},{16,80},{32,96},{48,112},{64,0},{80,16},{96,32},{112,48},{1... | collective-permute-start | bytes 73736 | tf_op jit(solution)/shard_map/ppermute | solution.py:696
  49.2 2.8 %collective-permute-done.16.b_m = f32[48,128]{1,0:T(8,128)S(1)} collective-permute-done((f32[48,128]{1,0:T(8,128)S(1)}, f32[48,128]{1,0:T(8,128)S(1)}, u32[]{:S(2)}, u32[]{:S(2)}) %collective-permute-start.16) | collective-permute-done | bytes 24608 | tf_op jit(solution)/shard_map/ppermute | solution.py:696
  52.0 2.2 %collective-permute-done.15.b_t = f32[192,128]{1,0:T(8,128)S(1)} collective-permute-done((f32[192,128]{1,0:T(8,128)S(1)}, f32[192,128]{1,0:T(8,128)S(1)}, u32[]{:S(2)}, u32[]{:S(2)}) %collective-permute-start.15) | collective-permute-done | bytes 98336 | tf_op jit(solution)/shard_map/ppermute | solution.py:691
  54.5 0.5 collective-permute-done.17.b_x
  55.6 1.9 %collective-permute-start.18 = (f32[384,128]{1,0:T(8,128)S(1)}, f32[384,128]{1,0:T(8,128)S(1)}, u32[]{:S(2)}, u32[]{:S(2)}) collective-permute-start(f32[384,128]{1,0:T(8,128)S(1)} %get-tuple-element.110), channel_id=1, source_target_pairs={{0,64},{16,80},{32,96},{48,112},{64,0},{80,16},{96,32},{112,48},{1... | collective-permute-start | bytes 589832 | tf_op jit(solution)/shard_map/ppermute | solution.py:696
  57.5 2.1 %collective-permute-start.19 = (f32[192,128]{1,0:T(8,128)S(1)}, f32[192,128]{1,0:T(8,128)S(1)}, u32[]{:S(2)}, u32[]{:S(2)}) collective-permute-start(f32[192,128]{1,0:T(8,128)S(1)} %get-tuple-element.113), channel_id=1, source_target_pairs={{0,15},{1,0},{2,1},{3,2},{4,3},{5,4},{6,5},{7,6},{8,7},{9,8},{10,9... | collective-permute-start | bytes 294920 | tf_op jit(solution)/shard_map/ppermute | solution.py:691
  59.6 1.3 %collective-permute-start.20 = (f32[48,128]{1,0:T(8,128)S(1)}, f32[48,128]{1,0:T(8,128)S(1)}, u32[]{:S(2)}, u32[]{:S(2)}) collective-permute-start(f32[48,128]{1,0:T(8,128)S(1)} %get-tuple-element.114), channel_id=1, source_target_pairs={{0,112},{16,0},{32,16},{48,32},{64,48},{80,64},{96,80},{112,96},{1... | collective-permute-start | bytes 73736 | tf_op jit(solution)/shard_map/ppermute | solution.py:691
  60.9 1.9 %collective-permute-start.21 = (f32[48,128]{1,0:T(8,128)S(1)}, f32[48,128]{1,0:T(8,128)S(1)}, u32[]{:S(2)}, u32[]{:S(2)}) collective-permute-start(f32[48,128]{1,0:T(8,128)S(1)} %get-tuple-element.115), channel_id=1, source_target_pairs={{0,64},{16,80},{32,96},{48,112},{64,0},{80,16},{96,32},{112,48},{1... | collective-permute-start | bytes 73736 | tf_op jit(solution)/shard_map/ppermute | solution.py:696
  62.8 0.7 collective-permute-done.20.r_x
  63.4 2.8 %collective-permute-done.21.r_m = f32[48,128]{1,0:T(8,128)S(1)} collective-permute-done((f32[48,128]{1,0:T(8,128)S(1)}, f32[48,128]{1,0:T(8,128)S(1)}, u32[]{:S(2)}, u32[]{:S(2)}) %collective-permute-start.21) | collective-permute-done | bytes 24608 | tf_op jit(solution)/shard_map/ppermute | solution.py:696
  66.5 2.0 %collective-permute-start.22 = (f32[192,128]{1,0:T(8,128)S(1)}, f32[192,128]{1,0:T(8,128)S(1)}, u32[]{:S(2)}, u32[]{:S(2)}) collective-permute-start(f32[192,128]{1,0:T(8,128)S(1)} %get-tuple-element.119), channel_id=1, source_target_pairs={{0,64},{16,80},{32,96},{48,112},{64,0},{80,16},{96,32},{112,48},{1... | collective-permute-start | bytes 294920 | tf_op jit(solution)/shard_map/ppermute | solution.py:696
  68.6 4.1 %collective-permute-done.22.rest_5_ = f32[192,128]{1,0:T(8,128)S(1)} collective-permute-done((f32[192,128]{1,0:T(8,128)S(1)}, f32[192,128]{1,0:T(8,128)S(1)}, u32[]{:S(2)}, u32[]{:S(2)}) %collective-permute-start.22) | collective-permute-done | bytes 98336 | tf_op jit(solution)/shard_map/ppermute | solution.py:696
  72.7 1.1 %shard_map.82 = (f32[1152,128]{1,0:T(8,128)}, f32[1152,128]{1,0:T(8,128)}) custom-call(s32[64,128]{1,0:T(8,128)S(1)} %get-tuple-element.62.info_ref, f32[1152,128]{1,0:T(8,128)S(1)} %get-tuple-element.97.u, f32[576,128]{1,0:T(8,128)S(1)} %get-tuple-element.98.p, f32[1152,128]{1,0:T(8,128)S(1)} %bitcast.13, f32[288,128]{1,0:T(8,128)S(1)} %get-tuple-element.111.u3, ...), custom_call_target="tpu_custom_call" | custom-call | tf_op jit(solution)/shard_map/pallas_call | solution.py:670
  (31 shorter events, 3.8 us)
Async XLA Ops:
  3.5 11.9 %collective-permute-start = (f32[192,128]{1,0:T(8,128)S(1)}, f32[192,128]{1,0:T(8,128)S(1)}, u32[]{:S(2)}, u32[]{:S(2)}) collective-permute-start(f32[192,128]{1,0:T(8,128)S(1)} %get-tuple-element.67), channel_id=1, source_target_pairs={{0,1},{1,0},{2,3},{3,2},{4,5},{5,4},{6,7},{7,6},{8,9},{9,8},{10,11... | collective-permute-start | bytes 294920 | tf_op jit(solution)/shard_map/ppermute | solution.py:686
  3.6 11.8 %collective-permute-start.1 = (f32[192,128]{1,0:T(8,128)S(1)}, f32[192,128]{1,0:T(8,128)S(1)}, u32[]{:S(2)}, u32[]{:S(2)}) collective-permute-start(f32[192,128]{1,0:T(8,128)S(1)} %get-tuple-element.68), channel_id=1, source_target_pairs={{0,15},{1,2},{2,1},{3,4},{4,3},{5,6},{6,5},{7,8},{8,7},{9,10},{10,... | collective-permute-start | bytes 294920 | tf_op jit(solution)/shard_map/ppermute | solution.py:686
  9.2 6.2 %collective-permute-start.2 = (f32[96,128]{1,0:T(8,128)S(1)}, f32[96,128]{1,0:T(8,128)S(1)}, u32[]{:S(2)}, u32[]{:S(2)}) collective-permute-start(f32[96,128]{1,0:T(8,128)S(1)} %get-tuple-element.69), channel_id=1, source_target_pairs={{0,64},{16,80},{32,96},{48,112},{64,0},{80,16},{96,32},{112,48},{1... | collective-permute-start | bytes 147464 | tf_op jit(solution)/shard_map/ppermute | solution.py:696
  13.1 3.8 %collective-permute-start.3 = (f32[48,128]{1,0:T(8,128)S(1)}, f32[48,128]{1,0:T(8,128)S(1)}, u32[]{:S(2)}, u32[]{:S(2)}) collective-permute-start(f32[48,128]{1,0:T(8,128)S(1)} %get-tuple-element.71), channel_id=1, source_target_pairs={{0,16},{16,0},{32,48},{48,32},{64,80},{80,64},{96,112},{112,96},{1... | collective-permute-start | bytes 73736 | tf_op jit(solution)/shard_map/ppermute | solution.py:686
  13.8 5.9 %collective-permute-start.4 = (f32[48,128]{1,0:T(8,128)S(1)}, f32[48,128]{1,0:T(8,128)S(1)}, u32[]{:S(2)}, u32[]{:S(2)}) collective-permute-start(f32[48,128]{1,0:T(8,128)S(1)} %get-tuple-element.72), channel_id=1, source_target_pairs={{0,112},{16,32},{32,16},{48,64},{64,48},{80,96},{96,80},{112,0},{1... | collective-permute-start | bytes 73736 | tf_op jit(solution)/shard_map/ppermute | solution.py:686
  20.0 7.6 %collective-permute-start.5 = (f32[192,128]{1,0:T(8,128)S(1)}, f32[192,128]{1,0:T(8,128)S(1)}, u32[]{:S(2)}, u32[]{:S(2)}) collective-permute-start(f32[192,128]{1,0:T(8,128)S(1)} %get-tuple-element.76), channel_id=1, source_target_pairs={{0,1},{1,0},{2,3},{3,2},{4,5},{5,4},{6,7},{7,6},{8,9},{9,8},{10,11... | collective-permute-start | bytes 294920 | tf_op jit(solution)/shard_map/ppermute | solution.py:686
  20.1 7.8 %collective-permute-start.6 = (f32[192,128]{1,0:T(8,128)S(1)}, f32[192,128]{1,0:T(8,128)S(1)}, u32[]{:S(2)}, u32[]{:S(2)}) collective-permute-start(f32[192,128]{1,0:T(8,128)S(1)} %get-tuple-element.77), channel_id=1, source_target_pairs={{0,15},{1,2},{2,1},{3,4},{4,3},{5,6},{6,5},{7,8},{8,7},{9,10},{10,... | collective-permute-start | bytes 294920 | tf_op jit(solution)/shard_map/ppermute | solution.py:686
  22.0 5.6 %collective-permute-start.7 = (f32[96,128]{1,0:T(8,128)S(1)}, f32[96,128]{1,0:T(8,128)S(1)}, u32[]{:S(2)}, u32[]{:S(2)}) collective-permute-start(f32[96,128]{1,0:T(8,128)S(1)} %get-tuple-element.78), channel_id=1, source_target_pairs={{0,64},{16,80},{32,96},{48,112},{64,0},{80,16},{96,32},{112,48},{1... | collective-permute-start | bytes 147464 | tf_op jit(solution)/shard_map/ppermute | solution.py:696
  22.0 6.1 %collective-permute-start.8 = (f32[48,128]{1,0:T(8,128)S(1)}, f32[48,128]{1,0:T(8,128)S(1)}, u32[]{:S(2)}, u32[]{:S(2)}) collective-permute-start(f32[48,128]{1,0:T(8,128)S(1)} %get-tuple-element.81), channel_id=1, source_target_pairs={{0,16},{16,0},{32,48},{48,32},{64,80},{80,64},{96,112},{112,96},{1... | collective-permute-start | bytes 73736 | tf_op jit(solution)/shard_map/ppermute | solution.py:686
  22.2 5.9 %collective-permute-start.9 = (f32[48,128]{1,0:T(8,128)S(1)}, f32[48,128]{1,0:T(8,128)S(1)}, u32[]{:S(2)}, u32[]{:S(2)}) collective-permute-start(f32[48,128]{1,0:T(8,128)S(1)} %get-tuple-element.82), channel_id=1, source_target_pairs={{0,112},{16,32},{32,16},{48,64},{64,48},{80,96},{96,80},{112,0},{1... | collective-permute-start | bytes 73736 | tf_op jit(solution)/shard_map/ppermute | solution.py:686
  28.7 13.6 %collective-permute-start.10 = (f32[384,128]{1,0:T(8,128)S(1)}, f32[384,128]{1,0:T(8,128)S(1)}, u32[]{:S(2)}, u32[]{:S(2)}) collective-permute-start(f32[384,128]{1,0:T(8,128)S(1)} %get-tuple-element.87), channel_id=1, source_target_pairs={{0,64},{16,80},{32,96},{48,112},{64,0},{80,16},{96,32},{112,48},{1... | collective-permute-start | bytes 589832 | tf_op jit(solution)/shard_map/ppermute | solution.py:696
  30.9 8.6 %collective-permute-start.11 = (f32[192,128]{1,0:T(8,128)S(1)}, f32[192,128]{1,0:T(8,128)S(1)}, u32[]{:S(2)}, u32[]{:S(2)}) collective-permute-start(f32[192,128]{1,0:T(8,128)S(1)} %get-tuple-element.90), channel_id=1, source_target_pairs={{0,15},{1,0},{2,1},{3,2},{4,3},{5,4},{6,5},{7,6},{8,7},{9,8},{10,9... | collective-permute-start | bytes 294920 | tf_op jit(solution)/shard_map/ppermute | solution.py:691
  33.2 3.8 %collective-permute-start.12 = (f32[48,128]{1,0:T(8,128)S(1)}, f32[48,128]{1,0:T(8,128)S(1)}, u32[]{:S(2)}, u32[]{:S(2)}) collective-permute-start(f32[48,128]{1,0:T(8,128)S(1)} %get-tuple-element.91), channel_id=1, source_target_pairs={{0,112},{16,0},{32,16},{48,32},{64,48},{80,64},{96,80},{112,96},{1... | collective-permute-start | bytes 73736 | tf_op jit(solution)/shard_map/ppermute | solution.py:691
  34.2 8.1 %copy-start = (f32[4,2,3,3,4,1,4,128]{7,6,5,4,3,2,1,0:T(4,128)S(1)}, f32[4,2,3,3,4,1,4,128]{7,6,5,4,3,2,1,0:T(4,128)}, u32[]{:S(2)}) copy-start(f32[4,2,3,3,4,1,4,128]{7,6,5,4,3,2,1,0:T(4,128)} %param.6) | copy-start | bytes 1769476
  34.2 5.3 %collective-permute-start.13 = (f32[48,128]{1,0:T(8,128)S(1)}, f32[48,128]{1,0:T(8,128)S(1)}, u32[]{:S(2)}, u32[]{:S(2)}) collective-permute-start(f32[48,128]{1,0:T(8,128)S(1)} %get-tuple-element.92), channel_id=1, source_target_pairs={{0,64},{16,80},{32,96},{48,112},{64,0},{80,16},{96,32},{112,48},{1... | collective-permute-start | bytes 73736 | tf_op jit(solution)/shard_map/ppermute | solution.py:696
  39.8 6.2 %collective-permute-start.14 = (f32[192,128]{1,0:T(8,128)S(1)}, f32[192,128]{1,0:T(8,128)S(1)}, u32[]{:S(2)}, u32[]{:S(2)}) collective-permute-start(f32[192,128]{1,0:T(8,128)S(1)} %get-tuple-element.96), channel_id=1, source_target_pairs={{0,64},{16,80},{32,96},{48,112},{64,0},{80,16},{96,32},{112,48},{1... | collective-permute-start | bytes 294920 | tf_op jit(solution)/shard_map/ppermute | solution.py:696
  46.6 7.7 %collective-permute-start.15 = (f32[192,128]{1,0:T(8,128)S(1)}, f32[192,128]{1,0:T(8,128)S(1)}, u32[]{:S(2)}, u32[]{:S(2)}) collective-permute-start(f32[192,128]{1,0:T(8,128)S(1)} %get-tuple-element.101), channel_id=1, source_target_pairs={{0,1},{1,2},{2,3},{3,4},{4,5},{5,6},{6,7},{7,8},{8,9},{9,10},{10,1... | collective-permute-start | bytes 294920 | tf_op jit(solution)/shard_map/ppermute | solution.py:691
  46.6 5.4 %collective-permute-start.16 = (f32[48,128]{1,0:T(8,128)S(1)}, f32[48,128]{1,0:T(8,128)S(1)}, u32[]{:S(2)}, u32[]{:S(2)}) collective-permute-start(f32[48,128]{1,0:T(8,128)S(1)} %get-tuple-element.102), channel_id=1, source_target_pairs={{0,64},{16,80},{32,96},{48,112},{64,0},{80,16},{96,32},{112,48},{1... | collective-permute-start | bytes 73736 | tf_op jit(solution)/shard_map/ppermute | solution.py:696
  49.1 5.9 %collective-permute-start.17 = (f32[48,128]{1,0:T(8,128)S(1)}, f32[48,128]{1,0:T(8,128)S(1)}, u32[]{:S(2)}, u32[]{:S(2)}) collective-permute-start(f32[48,128]{1,0:T(8,128)S(1)} %get-tuple-element.105), channel_id=1, source_target_pairs={{0,16},{16,32},{32,48},{48,64},{64,80},{80,96},{96,112},{112,0},{1... | collective-permute-start | bytes 73736 | tf_op jit(solution)/shard_map/ppermute | solution.py:691
  55.6 12.9 %collective-permute-start.18 = (f32[384,128]{1,0:T(8,128)S(1)}, f32[384,128]{1,0:T(8,128)S(1)}, u32[]{:S(2)}, u32[]{:S(2)}) collective-permute-start(f32[384,128]{1,0:T(8,128)S(1)} %get-tuple-element.110), channel_id=1, source_target_pairs={{0,64},{16,80},{32,96},{48,112},{64,0},{80,16},{96,32},{112,48},{1... | collective-permute-start | bytes 589832 | tf_op jit(solution)/shard_map/ppermute | solution.py:696
  57.5 8.7 %collective-permute-start.19 = (f32[192,128]{1,0:T(8,128)S(1)}, f32[192,128]{1,0:T(8,128)S(1)}, u32[]{:S(2)}, u32[]{:S(2)}) collective-permute-start(f32[192,128]{1,0:T(8,128)S(1)} %get-tuple-element.113), channel_id=1, source_target_pairs={{0,15},{1,0},{2,1},{3,2},{4,3},{5,4},{6,5},{7,6},{8,7},{9,8},{10,9... | collective-permute-start | bytes 294920 | tf_op jit(solution)/shard_map/ppermute | solution.py:691
  59.6 3.8 %collective-permute-start.20 = (f32[48,128]{1,0:T(8,128)S(1)}, f32[48,128]{1,0:T(8,128)S(1)}, u32[]{:S(2)}, u32[]{:S(2)}) collective-permute-start(f32[48,128]{1,0:T(8,128)S(1)} %get-tuple-element.114), channel_id=1, source_target_pairs={{0,112},{16,0},{32,16},{48,32},{64,48},{80,64},{96,80},{112,96},{1... | collective-permute-start | bytes 73736 | tf_op jit(solution)/shard_map/ppermute | solution.py:691
  60.9 5.3 %collective-permute-start.21 = (f32[48,128]{1,0:T(8,128)S(1)}, f32[48,128]{1,0:T(8,128)S(1)}, u32[]{:S(2)}, u32[]{:S(2)}) collective-permute-start(f32[48,128]{1,0:T(8,128)S(1)} %get-tuple-element.115), channel_id=1, source_target_pairs={{0,64},{16,80},{32,96},{48,112},{64,0},{80,16},{96,32},{112,48},{1... | collective-permute-start | bytes 73736 | tf_op jit(solution)/shard_map/ppermute | solution.py:696
  66.5 6.2 %collective-permute-start.22 = (f32[192,128]{1,0:T(8,128)S(1)}, f32[192,128]{1,0:T(8,128)S(1)}, u32[]{:S(2)}, u32[]{:S(2)}) collective-permute-start(f32[192,128]{1,0:T(8,128)S(1)} %get-tuple-element.119), channel_id=1, source_target_pairs={{0,64},{16,80},{32,96},{48,112},{64,0},{80,16},{96,32},{112,48},{1... | collective-permute-start | bytes 294920 | tf_op jit(solution)/shard_map/ppermute | solution.py:696
